TPU v7x, 32 devices: a whole 2x2x4 slice. The times are simulated.
32 devices in a mesh: gauge: 8 (over y, x, core), focus: 4 (over z).
Axes of the slice: x: 2, y: 2, z: 4, core: 2. Of those that a mesh axis runs over, the one named last changes fastest.
Arguments:
- aerial_clips: bfloat16 [4, 512, 8192], P('focus', 'gauge'), may hold values from 0 to 1
- basis_terms: bfloat16 [8192, 512], replicated, may hold values from -0.0625 to 0.0625
- holder: int32 [4, 512, 2], P('focus', 'gauge'), may hold values from 0 to 7, all different within a row; in each aligned block of 64 rows (0 to 63, 64 to 127, ..., all dimensions but the last counted through in order) at most 32 rows name the same one
- cache_slot: int32 [4, 512, 2], P('focus', 'gauge'), may hold values from 0 to 63
- dose_index: int32 [4, 512, 11], P('focus', 'gauge'), may hold values from 0 to 15
- dose_levels: float32 [16], replicated, may hold values from 0.7 to 1.4
- threshold: float32 [4], P('focus'), may hold values from 0.3 to 0.7
- measured: float32 [4, 512, 11], P('focus', 'gauge'), may hold values from -3 to 3
- parameters: float32 [512], replicated, may hold values from -0.25 to 0.25
Outputs:
- upper_factor: float32 [512, 512], replicated
- new_params: float32 [512], replicated
- linear_residual: float32 [4, 512, 11], P('focus', 'gauge')
Inputs may be any that keep to these rules, and one draw needn't show every extreme that they name: A gauge's two exposures have different holders; among the 64 gauges of one device no holder is named more than 32 times.
All inputs are finite; a program needn't handle non-finite values.
Results may differ from a plain program's by a relative error of at most 0.0013.
Values may be sent and summed in bfloat16 or wider, within the bound.
No kernel may reach another device: no remote copies, remote signals or barrier semaphores. Data moves between devices by JAX's collectives and lax.ppermute only.
A program may use at most 256 MiB of HBM per device.

v0:
```python
import jax
import jax.numpy as jnp
from jax import lax
from jax.sharding import PartitionSpec as P

DAMPING = 0.05
STEEPNESS = 4.0


def high_dot(left, right):
    return jnp.dot(left, right, precision=lax.Precision.HIGHEST)


def factor_block(block):
    width = block.shape[0]
    rows = jnp.arange(width, dtype=jnp.int32)

    def column_step(j, lower):
        pick = (rows == j).astype(jnp.float32)
        row_j = high_dot(pick, lower)
        column = high_dot(block, pick) - high_dot(lower, row_j)
        pivot = jnp.sqrt(jnp.sum(column * pick))
        filled = jnp.where(rows > j, column / pivot, jnp.where(rows == j, pivot, 0.0))
        return lower + filled[:, None] * pick[None, :]

    lower = lax.fori_loop(0, width, column_step, jnp.zeros((width, width), jnp.float32))

    def invert_step(i, inverse):
        pick = (rows == i).astype(jnp.float32)
        row_i = high_dot(pick, lower)
        pivot = jnp.sum(row_i * pick)
        new_row = (pick - high_dot(row_i, inverse)) / pivot
        return inverse + pick[:, None] * new_row[None, :]

    inverse = lax.fori_loop(0, width, invert_step, jnp.zeros((width, width), jnp.float32))
    return (lower, inverse)


def blocked_factor(matrix):
    terms = matrix.shape[0]
    width = min(64, terms)
    count = terms // width
    lower = jnp.zeros((terms, terms), jnp.float32)
    inverses = []
    for k in range(count):
        low = k * width
        high = low + width
        done = lower[low:high, :low]
        diag_block = matrix[low:high, low:high] - high_dot(done, done.T)
        diag_lower, diag_inverse = factor_block(diag_block)
        inverses.append(diag_inverse)
        lower = lower.at[low:high, low:high].set(diag_lower)
        if high < terms:
            below = matrix[high:, low:high] - high_dot(lower[high:, :low], done.T)
            lower = lower.at[high:, low:high].set(high_dot(below, diag_inverse.T))
    return (lower, inverses)


def forward_solve(lower, inverses, right):
    width = inverses[0].shape[0]
    pieces = []
    for k in range(len(inverses)):
        low = k * width
        rest = right[low : low + width]
        if k > 0:
            rest = rest - high_dot(lower[low : low + width, :low], jnp.concatenate(pieces))
        pieces.append(high_dot(inverses[k], rest))
    return jnp.concatenate(pieces)


def backward_solve(lower, inverses, right):
    width = inverses[0].shape[0]
    count = len(inverses)
    terms = right.shape[0]
    pieces = []
    for k in range(count - 1, -1, -1):
        low = k * width
        high = low + width
        rest = right[low:high]
        if high < terms:
            rest = rest - high_dot(lower[high:, low:high].T, jnp.concatenate(pieces))
        pieces.insert(0, high_dot(inverses[k].T, rest))
    return jnp.concatenate(pieces)


def local(
    aerial_clips,
    basis_terms,
    holder,
    cache_slot,
    dose_index,
    dose_levels,
    threshold,
    measured,
    parameters,
):
    gauge_count = lax.axis_size("gauge")
    focus_count = lax.axis_size("focus")
    clip_cache = aerial_clips[0]
    cached_rows = clip_cache.shape[0]
    pixels = clip_cache.shape[1]
    owners = holder[0].reshape(-1)
    places = cache_slot[0].reshape(-1)
    ref_count = owners.shape[0]
    gauge_local = ref_count // 2
    capacity = max(2, 4 * gauge_local // gauge_count)
    matches = (owners[:, None] == jnp.arange(gauge_count, dtype=jnp.int32)[None, :]).astype(
        jnp.int32
    )
    position = jnp.sum((jnp.cumsum(matches, axis=0) - matches) * matches, axis=1)
    flat_place = owners * capacity + position
    placing = flat_place[:, None] == jnp.arange(gauge_count * capacity, dtype=jnp.int32)[None, :]
    requests = jnp.sum(placing.astype(jnp.int32) * places[:, None], axis=0).reshape(
        gauge_count, capacity
    )
    wanted = lax.all_to_all(requests, "gauge", split_axis=0, concat_axis=0, tiled=True)
    flat_wanted = wanted.reshape(-1)
    chooser = (flat_wanted[:, None] == jnp.arange(cached_rows, dtype=jnp.int32)[None, :]).astype(
        jnp.bfloat16
    )
    picked = jnp.dot(chooser, clip_cache, preferred_element_type=jnp.float32).astype(jnp.bfloat16)
    picked = picked.reshape(wanted.shape[0], wanted.shape[1], pixels)
    replies = lax.all_to_all(picked, "gauge", split_axis=0, concat_axis=0, tiled=True)
    exposures = jnp.dot(
        placing.astype(jnp.bfloat16),
        replies.reshape(gauge_count * capacity, pixels),
        preferred_element_type=jnp.float32,
    ).astype(jnp.bfloat16)
    clip_pairs = exposures.astype(jnp.float32).reshape(gauge_local, 2, pixels)
    intensity = 0.5 * (clip_pairs[:, 0] + clip_pairs[:, 1])
    level_count = dose_levels.shape[0]
    one_hot = (
        dose_index[0][:, :, None] == jnp.arange(level_count, dtype=jnp.int32)[None, None, :]
    ).astype(jnp.float32)
    dose_rows = jnp.sum(one_hot * dose_levels[None, None, :], axis=2)
    per_gauge = dose_rows.shape[1]
    response = jnp.tanh(
        STEEPNESS * (dose_rows[:, :, None] * intensity[:, None, :] - threshold[0])
    ).astype(jnp.bfloat16)
    row_count = gauge_local * per_gauge
    features = jnp.dot(
        response.reshape(row_count, pixels), basis_terms, preferred_element_type=jnp.float32
    )
    linear = high_dot(features, parameters)
    signal = jnp.tanh(linear)
    derivative = 1.0 - signal * signal
    misfit = measured[0].reshape(-1) - signal
    scale = float(row_count * gauge_count * focus_count) ** (-0.5)
    jacobian = scale * derivative[:, None] * features
    normal_mat = high_dot(jacobian.T, jacobian)
    projected = high_dot(jacobian.T, scale * misfit)
    terms = normal_mat.shape[0]
    identity = jnp.eye(terms, dtype=jnp.float32)
    summed_mat, summed_proj = lax.psum((normal_mat, projected), ("gauge", "focus"))
    lower_factor, inverses = blocked_factor(summed_mat + DAMPING * identity)
    carried = forward_solve(lower_factor, inverses, summed_proj)
    update = backward_solve(lower_factor, inverses, carried)
    new_params = parameters + update
    moved = high_dot(features, update)
    linear_residual = (misfit - derivative * moved).reshape(1, gauge_local, per_gauge)
    return (lower_factor.T, new_params, linear_residual)


def solution(mesh):
    return jax.shard_map(
        local,
        mesh=mesh,
        in_specs=(
            P("focus", "gauge", None),
            P(),
            P("focus", "gauge", None),
            P("focus", "gauge", None),
            P("focus", "gauge", None),
            P(),
            P("focus"),
            P("focus", "gauge", None),
            P(),
        ),
        out_specs=(P(), P(), P("focus", "gauge", None)),
        check_vma=False,
    )
```

profile of v0, /device:TPU:0, one launch (start us, length us, event | category | flops | bytes accessed | tf_op | source)
XLA Modules:
  0.0 2160.2 jit_solution(9085346160487572990)
XLA Ops:
  9.8 9.6 all_to_all.14
  20.6 3.3 convolution_convert_fusion
  23.9 4.7 all-to-all-start.1
  29.9 47.8 %all-to-all-done.1 = bf16[8,32,8192]{2,1,0:T(8,128)(2,1)} async-done(((bf16[8,32,8192]{2,1,0:T(8,128)(2,1)}), bf16[8,32,8192]{2,1,0:T(8,128)(2,1)}, u32[]{:S(2)}, u32[]{:S(2)}) %all-to-all-start.1) | async-done | bytes 4194336 | tf_op jit(solution)/shard_map/all_to_all | solution.py:123
  77.7 4.9 fusion.268
  82.6 5.8 reshape.601
  88.4 6.7 fusion.269
  96.4 11.1 mul.753
  107.5 19.8 mul.754
  127.4 13.4 fusion.264
  142.1 4.2 fusion.273
  147.4 39.5 %psum.15 = f32[512]{0:T(512)S(1)} all-reduce(f32[512]{0:T(512)S(1)} %bitcast.766), channel_id=1, replica_groups=mesh['gauge'=8,'focus'=4] {'gauge','focus'}, use_global_device_ids=true, to_apply=%region_50.51 | all-reduce | flops 512 | bytes 4096 | tf_op jit(solution)/shard_map/psum | solution.py:154
  186.9 88.9 %all-reduce.3.cloned.1.call-done = f32[512,512]{1,0:T(8,128)} async-done(((f32[512,512]{1,0:T(8,128)}), f32[512,512]{1,0:T(8,128)}) %all-reduce.3.cloned.1.call-update) | async-done | bytes 1048592 | tf_op jit(solution)/shard_map/psum | solution.py:154
  278.2 119.8 %while.255 = (s32[]{:T(128)}, f32[64,64]{1,0:T(8,128)S(1)}, f32[64,64]{1,0:T(8,128)S(1)}, s32[]{:T(128)}, s32[]{:T(128)}) while((s32[]{:T(128)}, f32[64,64]{1,0:T(8,128)S(1)}, f32[64,64]{1,0:T(8,128)S(1)}, s32[]{:T(128)}, s32[]{:T(128)}) %tuple.576), condition=%wide.region_7.8_spmd.clone.clone, body=%wide.region_5.7_spmd.clone.clone.sunk | while | flops 168770 | bytes 84589 | solution.py:26
  398.1 103.4 %while.247 = (s32[]{:T(128)}, f32[64,64]{1,0:T(8,128)S(1)}, f32[64,64]{1,0:T(8,128)S(1)}, s32[]{:T(128)}, s32[]{:T(128)}) while((s32[]{:T(128)}, f32[64,64]{1,0:T(8,128)S(1)}, f32[64,64]{1,0:T(8,128)S(1)}, s32[]{:T(128)}, s32[]{:T(128)}) %tuple.579), condition=%wide.region_10.11_spmd.clone, body=%wide.region_8.10_spmd.clone.sunk | while | flops 115330 | bytes 67164 | solution.py:35
  503.9 119.9 %while.256 = (s32[]{:T(128)}, f32[64,64]{1,0:T(8,128)S(1)}, f32[64,64]{1,0:T(8,128)S(1)}, s32[]{:T(128)}, s32[]{:T(128)}) while((s32[]{:T(128)}, f32[64,64]{1,0:T(8,128)S(1)}, f32[64,64]{1,0:T(8,128)S(1)}, s32[]{:T(128)}, s32[]{:T(128)}) %tuple.582), condition=%wide.region_13.14_spmd.clone.clone, body=%wide.region_11.13_spmd.clone.clone.sunk | while | flops 168770 | bytes 84589 | solution.py:26
  627.8 2.9 scatter.54
  632.2 103.4 %while.248 = (s32[]{:T(128)}, f32[64,64]{1,0:T(8,128)S(1)}, f32[64,64]{1,0:T(8,128)S(1)}, s32[]{:T(128)}, s32[]{:T(128)}) while((s32[]{:T(128)}, f32[64,64]{1,0:T(8,128)S(1)}, f32[64,64]{1,0:T(8,128)S(1)}, s32[]{:T(128)}, s32[]{:T(128)}) %tuple.585), condition=%wide.region_16.17_spmd.clone, body=%wide.region_14.16_spmd.clone.sunk | while | flops 115330 | bytes 67164 | solution.py:35
  740.2 119.8 %while.257 = (s32[]{:T(128)}, f32[64,64]{1,0:T(8,128)S(1)}, f32[64,64]{1,0:T(8,128)S(1)}, s32[]{:T(128)}, s32[]{:T(128)}) while((s32[]{:T(128)}, f32[64,64]{1,0:T(8,128)S(1)}, f32[64,64]{1,0:T(8,128)S(1)}, s32[]{:T(128)}, s32[]{:T(128)}) %tuple.588), condition=%wide.region_19.20_spmd.clone.clone, body=%wide.region_17.19_spmd.clone.clone.sunk | while | flops 168770 | bytes 84589 | solution.py:26
  864.6 103.4 %while.249 = (s32[]{:T(128)}, f32[64,64]{1,0:T(8,128)S(1)}, f32[64,64]{1,0:T(8,128)S(1)}, s32[]{:T(128)}, s32[]{:T(128)}) while((s32[]{:T(128)}, f32[64,64]{1,0:T(8,128)S(1)}, f32[64,64]{1,0:T(8,128)S(1)}, s32[]{:T(128)}, s32[]{:T(128)}) %tuple.591), condition=%wide.region_22.23_spmd.clone, body=%wide.region_20.22_spmd.clone.sunk | while | flops 115330 | bytes 67164 | solution.py:35
  974.8 119.8 %while.258 = (s32[]{:T(128)}, f32[64,64]{1,0:T(8,128)S(1)}, f32[64,64]{1,0:T(8,128)S(1)}, s32[]{:T(128)}, s32[]{:T(128)}) while((s32[]{:T(128)}, f32[64,64]{1,0:T(8,128)S(1)}, f32[64,64]{1,0:T(8,128)S(1)}, s32[]{:T(128)}, s32[]{:T(128)}) %tuple.594), condition=%wide.region_25.26_spmd.clone.clone, body=%wide.region_23.25_spmd.clone.clone.sunk | while | flops 168770 | bytes 84589 | solution.py:26
  1094.7 3.0 scatter.60
  1099.4 103.4 %while.250 = (s32[]{:T(128)}, f32[64,64]{1,0:T(8,128)S(1)}, f32[64,64]{1,0:T(8,128)S(1)}, s32[]{:T(128)}, s32[]{:T(128)}) while((s32[]{:T(128)}, f32[64,64]{1,0:T(8,128)S(1)}, f32[64,64]{1,0:T(8,128)S(1)}, s32[]{:T(128)}, s32[]{:T(128)}) %tuple.597), condition=%wide.region_28.29_spmd.clone, body=%wide.region_26.28_spmd.clone.sunk | while | flops 115330 | bytes 67164 | solution.py:35
  1207.4 119.8 %while.259 = (s32[]{:T(128)}, f32[64,64]{1,0:T(8,128)S(1)}, f32[64,64]{1,0:T(8,128)S(1)}, s32[]{:T(128)}, s32[]{:T(128)}) while((s32[]{:T(128)}, f32[64,64]{1,0:T(8,128)S(1)}, f32[64,64]{1,0:T(8,128)S(1)}, s32[]{:T(128)}, s32[]{:T(128)}) %tuple.600), condition=%wide.region_31.32_spmd.clone.clone, body=%wide.region_29.31_spmd.clone.clone.sunk | while | flops 168770 | bytes 84589 | solution.py:26
  1331.9 103.4 %while.251 = (s32[]{:T(128)}, f32[64,64]{1,0:T(8,128)S(1)}, f32[64,64]{1,0:T(8,128)S(1)}, s32[]{:T(128)}, s32[]{:T(128)}) while((s32[]{:T(128)}, f32[64,64]{1,0:T(8,128)S(1)}, f32[64,64]{1,0:T(8,128)S(1)}, s32[]{:T(128)}, s32[]{:T(128)}) %tuple.603), condition=%wide.region_34.35_spmd.clone, body=%wide.region_32.34_spmd.clone.sunk | while | flops 115330 | bytes 67164 | solution.py:35
  1442.1 119.8 %while.260 = (s32[]{:T(128)}, f32[64,64]{1,0:T(8,128)S(1)}, f32[64,64]{1,0:T(8,128)S(1)}, s32[]{:T(128)}, s32[]{:T(128)}) while((s32[]{:T(128)}, f32[64,64]{1,0:T(8,128)S(1)}, f32[64,64]{1,0:T(8,128)S(1)}, s32[]{:T(128)}, s32[]{:T(128)}) %tuple.606), condition=%wide.region_37.38_spmd.clone.clone, body=%wide.region_35.37_spmd.clone.clone.sunk | while | flops 168770 | bytes 84589 | solution.py:26
  1562.0 3.0 scatter.66
  1566.6 103.4 %while.252 = (s32[]{:T(128)}, f32[64,64]{1,0:T(8,128)S(1)}, f32[64,64]{1,0:T(8,128)S(1)}, s32[]{:T(128)}, s32[]{:T(128)}) while((s32[]{:T(128)}, f32[64,64]{1,0:T(8,128)S(1)}, f32[64,64]{1,0:T(8,128)S(1)}, s32[]{:T(128)}, s32[]{:T(128)}) %tuple.609), condition=%wide.region_40.41_spmd.clone, body=%wide.region_38.40_spmd.clone.sunk | while | flops 115330 | bytes 67164 | solution.py:35
  1674.7 119.8 %while.261 = (s32[]{:T(128)}, f32[64,64]{1,0:T(8,128)S(1)}, f32[64,64]{1,0:T(8,128)S(1)}, s32[]{:T(128)}, s32[]{:T(128)}) while((s32[]{:T(128)}, f32[64,64]{1,0:T(8,128)S(1)}, f32[64,64]{1,0:T(8,128)S(1)}, s32[]{:T(128)}, s32[]{:T(128)}) %tuple.612), condition=%wide.region_43.44_spmd.clone.clone, body=%wide.region_41.43_spmd.clone.clone.sunk | while | flops 168770 | bytes 84589 | solution.py:26
  1798.4 103.4 %while.253 = (s32[]{:T(128)}, f32[64,64]{1,0:T(8,128)S(1)}, f32[64,64]{1,0:T(8,128)S(1)}, s32[]{:T(128)}, s32[]{:T(128)}) while((s32[]{:T(128)}, f32[64,64]{1,0:T(8,128)S(1)}, f32[64,64]{1,0:T(8,128)S(1)}, s32[]{:T(128)}, s32[]{:T(128)}) %tuple.615), condition=%wide.region_46.47_spmd.clone, body=%wide.region_44.46_spmd.clone.sunk | while | flops 115330 | bytes 67164 | solution.py:35
  1906.3 120.0 %while.262 = (s32[]{:T(128)}, f32[64,64]{1,0:T(8,128)S(1)}, f32[64,64]{1,0:T(8,128)S(1)}, s32[]{:T(128)}, s32[]{:T(128)}) while((s32[]{:T(128)}, f32[64,64]{1,0:T(8,128)S(1)}, f32[64,64]{1,0:T(8,128)S(1)}, s32[]{:T(128)}, s32[]{:T(128)}) %tuple.618), condition=%wide.region_49.50_spmd.clone.clone, body=%wide.region_47.49_spmd.clone.clone.sunk | while | flops 168770 | bytes 84589 | solution.py:26
  2037.7 103.5 %while.254 = (s32[]{:T(128)}, f32[64,64]{1,0:T(8,128)S(1)}, f32[64,64]{1,0:T(8,128)S(1)}, s32[]{:T(128)}, s32[]{:T(128)}) while((s32[]{:T(128)}, f32[64,64]{1,0:T(8,128)S(1)}, f32[64,64]{1,0:T(8,128)S(1)}, s32[]{:T(128)}, s32[]{:T(128)}) %tuple.621), condition=%wide.region_53.54_spmd.clone, body=%wide.region_51.53_spmd.clone.sunk | while | flops 115330 | bytes 67164 | solution.py:35
  (5270 shorter events, 1508.8 us)
Async XLA Ops:
  7.2 13.5 copy-start
  23.9 4.7 copy-start.5
  23.9 4.8 copy-start.6
  23.9 5.7 copy-start.4
  23.9 53.8 %all-to-all-start.1 = ((bf16[8,32,8192]{2,1,0:T(8,128)(2,1)}), bf16[8,32,8192]{2,1,0:T(8,128)(2,1)}, u32[]{:S(2)}, u32[]{:S(2)}) async-start(bf16[8,32,8192]{2,1,0:T(8,128)(2,1)} %bitcast.747), calls=%async_computation.1 | async-start | bytes 8388608 | tf_op jit(solution)/shard_map/all_to_all | solution.py:123
  28.6 247.3 %all-reduce.3.cloned.1.call-start = ((), (), s32[]{:S(2)}) async-start(), calls=%async_computation.2 | async-start | bytes 2097152 | tf_op jit(solution)/shard_map/psum | solution.py:154
  127.3 13.4 copy-start.3
  277.2 1.0 copy-start.2
  1674.7 478.6 %copy-start.1 = (bf16[1,64,8192]{2,1,0:T(8,128)(2,1)S(1)}, bf16[1,64,8192]{2,1,0:T(8,128)(2,1)}, u32[]{:S(2)}) copy-start(bf16[1,64,8192]{2,1,0:T(8,128)(2,1)} %param.71) | copy-start | bytes 3145732
Sparse Core Ops, SparseCore 0:
  146.4 129.4 all-reduce.2
where the time goes:
time: 2200 us; the launch traced here: 2160 us
  matrix products  1400 us (64%)
  loops' own time  368 us (17%)
  waiting for transfers between devices  137 us (6%)
  other arithmetic  96.3 us (4%)
  local copies, waits for them, and re-layouts  85.7 us (4%)
  blocking collectives  49.2 us (2%)
    dot_general x2614, matrix products, high_dot(): return jnp.dot(left, right, precision=lax.Precision.HIGHEST)  1380 us
    another operation x8, loops' own time, factor_block(): lax.fori_loop(0, width, column_step, jnp.zeros((width, width), jnp.float32))  364 us
    psum x1, waiting for transfers between devices, local(): lax.psum((normal_mat, projected), ('gauge', 'focus'))  88.9 us
    all_to_all x1, waiting for transfers between devices, local(): lax.all_to_all(picked, 'gauge', split_axis=0, concat_axis=0, tiled=True)  47.8 us

commit v1 on v0

v1 whole, which is shorter than its diff:
```python
import functools

import jax
import jax.numpy as jnp
from jax import lax
from jax.experimental import pallas as pl
from jax.experimental.pallas import tpu as pltpu
from jax.sharding import PartitionSpec as P

DAMPING = 0.05
STEEPNESS = 4.0
TILE = 128
GROUP = 8
HALVINGS = 3
PIECES = 1 << HALVINGS
PIECE_ROWS = TILE + 8
CHUNKS = 4
VMEM_BYTES = 56 << 20
HIGHEST = lax.Precision.HIGHEST


def bits_of(size):
    return [1 << k for k in range(size.bit_length() - 1)]


def flipped(place):
    return sum(((place >> k) & 1) << (HALVINGS - 1 - k) for k in range(HALVINGS))


def swap(value, axis, bit):
    size = lax.axis_size(axis)
    return lax.ppermute(value, axis, [(i, i ^ bit) for i in range(size)])


def dot_rows(left, right):
    return lax.dot_general(
        left, right, (((0,), (0,)), ((), ())), precision=HIGHEST, preferred_element_type=jnp.float32
    )


def dot_plain(left, right):
    return lax.dot_general(
        left, right, (((1,), (0,)), ((), ())), precision=HIGHEST, preferred_element_type=jnp.float32
    )


def dot_columns(left, right):
    return lax.dot_general(
        left, right, (((1,), (1,)), ((), ())), precision=HIGHEST, preferred_element_type=jnp.float32
    )


def full(value):
    return jnp.broadcast_to(value, (8, TILE))


def piece_table(count):
    table = []
    for b in range(0, count, 2):
        table.append((b, b + 1, True))
    for r in range(count):
        for c in range(r + 1, count):
            table.append((r, c, False))
    return table


def resist_kernel(first, gauges, doses, block_ref, threshold_ref, dose_ref, select_ref, *refs):
    pieces = refs[: len(refs) - (3 if first else 4)]
    rest = refs[len(pieces) :]
    basis_ref = rest[0]
    out_ref, rows_ref = rest[-2], rest[-1]
    width = pieces[0].shape[0]
    picked = None
    for o, piece in enumerate(pieces):
        term = jnp.dot(
            select_ref[:, o * width : (o + 1) * width],
            piece[...],
            preferred_element_type=jnp.float32,
        )
        picked = term if picked is None else picked + term
    level = threshold_ref[0]
    for d in range(doses):
        answer = jnp.tanh(dose_ref[:, d : d + 1] * picked - level).astype(jnp.bfloat16)
        for who in range(2):
            low = (who * doses + d) * gauges
            rows_ref[low : low + gauges, :] = answer[who * gauges : (who + 1) * gauges, :]
    summed = jnp.dot(rows_ref[...], basis_ref[...], preferred_element_type=jnp.float32)
    if first:
        out_ref[...] = summed
    else:
        out_ref[...] = rest[1][...] + summed


def resist_rows(block, threshold, doses_by_gauge, select, pieces, basis, total, doses):
    pair = pieces[0].shape[0]
    gauges = doses_by_gauge.shape[0] // 2
    pixels = pieces[0].shape[1]
    terms = basis.shape[1]
    rows = 2 * gauges * doses
    first = total is None
    whole = lambda shape: pl.BlockSpec(shape, lambda i, s: (0, 0))
    in_specs = [
        pl.BlockSpec(memory_space=pltpu.SMEM),
        whole(doses_by_gauge.shape),
        whole(select.shape),
        *[whole((pair, pixels)) for _ in pieces],
        pl.BlockSpec((pixels, terms), lambda i, s: (s[0], 0)),
    ]
    operands = [threshold, doses_by_gauge, select, *pieces, basis]
    if not first:
        in_specs.append(whole((rows, terms)))
        operands.append(total)
    return pl.pallas_call(
        functools.partial(resist_kernel, first, gauges, doses),
        out_shape=jax.ShapeDtypeStruct((rows, terms), jnp.float32),
        grid_spec=pltpu.PrefetchScalarGridSpec(
            num_scalar_prefetch=1,
            grid=(1,),
            in_specs=in_specs,
            out_specs=whole((rows, terms)),
            scratch_shapes=[pltpu.VMEM((rows, pixels), jnp.bfloat16)],
        ),
        input_output_aliases={} if first else {len(operands): 0},
        compiler_params=pltpu.CompilerParams(vmem_limit_bytes=VMEM_BYTES),
        cost_estimate=pl.CostEstimate(
            flops=2 * rows * pixels * terms,
            bytes_accessed=2 * pixels * (terms + pair * len(pieces)) + 8 * rows * terms,
            transcendentals=rows * pixels,
        ),
        name="resist",
    )(block, *operands)


def normal_kernel(scale, table, me_ref, mine_ref, other_ref, measured_ref, params_ref, feat_ref, misfit_ref, deriv_ref, out_ref, jac_ref):
    gauges, doses = measured_ref.shape
    terms = mine_ref.shape[1]
    count = terms // TILE
    me = me_ref[0]
    params = params_ref[...]
    lane = lax.broadcasted_iota(jnp.int32, (gauges, doses), 1)
    linear = jnp.zeros((gauges, doses), jnp.float32)
    for d in range(doses):
        low, high = d * gauges, (d + 1) * gauges
        feat = mine_ref[low:high, :] + other_ref[low:high, :]
        feat_ref[low:high, :] = feat
        along = jnp.sum(feat * params, axis=1, keepdims=True)
        linear = jnp.where(lane == d, along, linear)
    signal = jnp.tanh(linear)
    deriv = 1.0 - signal * signal
    misfit = measured_ref[...] - signal
    deriv_ref[...] = deriv
    misfit_ref[...] = misfit
    projected = jnp.zeros((1, terms), jnp.float32)
    for d in range(doses):
        low, high = d * gauges, (d + 1) * gauges
        jac = (scale * deriv[:, d : d + 1]) * feat_ref[low:high, :]
        jac_ref[low:high, :] = jac
        projected = projected + jnp.sum(jac * (scale * misfit[:, d : d + 1]), axis=0, keepdims=True)
    row = lax.broadcasted_iota(jnp.int32, (TILE, TILE), 0)
    col = lax.broadcasted_iota(jnp.int32, (TILE, TILE), 1)
    blocks = {}
    for b in range(count):
        strip = dot_rows(jac_ref[:, b * TILE : (b + 1) * TILE], jac_ref[:, b * TILE :])
        for c in range(b, count):
            blocks[b, c] = strip[:, (c - b) * TILE : (c - b + 1) * TILE]
    extra = [projected[:, b * TILE : (b + 1) * TILE] for b in range(count)]
    for p, (r, c, paired) in enumerate(table):
        where = flipped(p ^ me)
        if paired:
            second = blocks[c, c]
            block = jnp.where(row <= col, blocks[r, r], second)
            extra.append(jnp.sum(jnp.where(row == col, second, 0.0), axis=0, keepdims=True))
        else:
            block = blocks[r, c]
        out_ref[where, :TILE, :] = block
        out_ref[where, TILE:, :] = jnp.zeros((8, TILE), jnp.float32)
    home = flipped(me)
    for k, line in enumerate(extra):
        out_ref[home, TILE + k : TILE + k + 1, :] = line


def factor_tile(block):
    count = TILE // GROUP
    sub = lax.broadcasted_iota(jnp.int32, (8, TILE), 0)
    lane = lax.broadcasted_iota(jnp.int32, (8, TILE), 1)
    left = [block[8 * q : 8 * q + 8, :] for q in range(count)]
    right = [jnp.where(lane == sub + 8 * q, 1.0, 0.0).astype(jnp.float32) for q in range(count)]
    for p in range(count):
        base = GROUP * p
        cols = [full(left[p][:, base + k : base + k + 1]) for k in range(GROUP)]
        a = [[full(cols[k][m : m + 1, :]) if m >= k else None for k in range(GROUP)] for m in range(GROUP)]
        low = [[None] * GROUP for _ in range(GROUP)]
        root = []
        for k in range(GROUP):
            inverse = 1.0 / a[k][k]
            root.append(lax.rsqrt(a[k][k]))
            for m in range(k + 1, GROUP):
                for j in range(k + 1, m + 1):
                    a[m][j] = a[m][j] - (a[m][k] * a[j][k]) * inverse
        for k in range(GROUP):
            for m in range(k + 1, GROUP):
                low[m][k] = a[m][k] * root[k]
        upper = [full(left[p][k : k + 1, :]) for k in range(GROUP)]
        other = [full(right[p][k : k + 1, :]) for k in range(GROUP)]
        for k in range(GROUP):
            upper[k] = upper[k] * root[k]
            other[k] = other[k] * root[k]
            for m in range(k + 1, GROUP):
                upper[m] = upper[m] - low[m][k] * upper[k]
                other[m] = other[m] - low[m][k] * other[k]
        for q in range(p + 1, count):
            c = [full(left[q][:, base + k : base + k + 1]) for k in range(GROUP)]
            for k in range(GROUP):
                c[k] = c[k] * root[k]
                for m in range(k + 1, GROUP):
                    c[m] = c[m] - low[m][k] * c[k]
            for k in range(GROUP):
                left[q] = left[q] - c[k] * upper[k]
                right[q] = right[q] - c[k] * other[k]
        new_left, new_right = upper[GROUP - 1], other[GROUP - 1]
        for k in range(GROUP - 1):
            new_left = jnp.where(sub == k, upper[k], new_left)
            new_right = jnp.where(sub == k, other[k], new_right)
        left[p] = jnp.where(lane >= sub + base, new_left, 0.0)
        right[p] = new_right
    return left, right


def factor_kernel(table, groups, me_ref, *refs):
    sources = refs[: len(groups)]
    feat_ref, misfit_ref, deriv_ref, params_ref, upper_ref, new_ref, resid_ref, stage, work, inv, rhs = refs[len(groups) :]
    terms = work.shape[0]
    count = terms // TILE
    me = me_ref[0]
    for source, places in zip(sources, groups):
        for k, place in enumerate(places):
            stage[place ^ me] = source[k]
    row = lax.broadcasted_iota(jnp.int32, (TILE, TILE), 0)
    col = lax.broadcasted_iota(jnp.int32, (TILE, TILE), 1)
    damp = jnp.where(row == col, DAMPING, 0.0)
    extra = count
    for p, (r, c, paired) in enumerate(table):
        block = stage[p, :TILE, :]
        if paired:
            turned = block.T
            diag = stage[0, TILE + extra : TILE + extra + 1, :]
            extra += 1
            work[r * TILE : (r + 1) * TILE, r * TILE : (r + 1) * TILE] = jnp.where(row <= col, block, turned) + damp
            second = jnp.where(row == col, diag, jnp.where(row > col, block, turned))
            work[c * TILE : (c + 1) * TILE, c * TILE : (c + 1) * TILE] = second + damp
        else:
            work[r * TILE : (r + 1) * TILE, c * TILE : (c + 1) * TILE] = block
    for b in range(count):
        rhs[:, b * TILE : (b + 1) * TILE] = full(stage[0, TILE + b : TILE + b + 1, :])
    upper_ref[...] = jnp.zeros_like(upper_ref)

    def step(b, carry):
        off = pl.multiple_of(b * TILE, TILE)
        left, right = factor_tile(work[pl.ds(off, TILE), pl.ds(off, TILE)])
        for q in range(TILE // GROUP):
            upper_ref[pl.ds(off + 8 * q, 8), pl.ds(off, TILE)] = left[q]
            inv[pl.ds(off + 8 * q, 8), :] = right[q]
        for bb in range(count):

            @pl.when(b == bb)
            def _():
                lo, hi = bb * TILE, (bb + 1) * TILE
                solved = dot_columns(rhs[:, lo:hi], inv[lo:hi, :])
                rhs[:, lo:hi] = solved
                if hi < terms:
                    panel = dot_plain(inv[lo:hi, :], work[lo:hi, hi:])
                    upper_ref[lo:hi, hi:] = panel
                    rhs[:, hi:] -= dot_plain(solved, panel)
                    for r in range(bb + 1, count):
                        s = (r - bb - 1) * TILE
                        work[r * TILE : (r + 1) * TILE, r * TILE :] -= dot_rows(panel[:, s : s + TILE], panel[:, s:])

        return carry

    lax.fori_loop(0, count, step, 0)
    for b in range(count - 1, -1, -1):
        lo, hi = b * TILE, (b + 1) * TILE
        rest = rhs[:, lo:hi]
        if hi < terms:
            rest = rest - dot_columns(rhs[:, hi:], upper_ref[lo:hi, hi:])
        rhs[:, lo:hi] = dot_plain(rest, inv[lo:hi, :])
    update = rhs[0:1, :]
    new_ref[...] = params_ref[...] + update
    gauges, doses = misfit_ref.shape
    lane = lax.broadcasted_iota(jnp.int32, (gauges, doses), 1)
    moved = jnp.zeros((gauges, doses), jnp.float32)
    for d in range(doses):
        along = jnp.sum(feat_ref[d * gauges : (d + 1) * gauges, :] * update, axis=1, keepdims=True)
        moved = jnp.where(lane == d, along, moved)
    resid_ref[...] = misfit_ref[...] - deriv_ref[...] * moved


def local(
    aerial_clips,
    basis_terms,
    holder,
    cache_slot,
    dose_index,
    dose_levels,
    threshold,
    measured,
    parameters,
):
    gauge_count = lax.axis_size("gauge")
    focus_count = lax.axis_size("focus")
    me = lax.axis_index("gauge")
    core = me & 1
    clips = aerial_clips[0]
    cached, pixels = clips.shape
    gauges = holder.shape[1]
    doses = dose_index.shape[2]
    terms = basis_terms.shape[1]
    half = pixels // 2
    step = half // CHUNKS
    gauge_bits = bits_of(gauge_count)
    offsets = list(range(0, gauge_count, 2))
    wide = gauge_bits[1:]

    notes = jnp.concatenate([holder[0], cache_slot[0], dose_index[0]], axis=1)
    both = jnp.concatenate([notes, swap(notes, "gauge", 1)], axis=0)
    relative = both[:, 0:2] ^ me
    place = relative * cached + both[:, 2:4]
    spots = jnp.arange(gauge_count * cached, dtype=jnp.int32)[None, :]
    select = (
        jnp.where(place[:, 0:1] == spots, 0.5, 0.0) + jnp.where(place[:, 1:2] == spots, 0.5, 0.0)
    ).astype(jnp.bfloat16)
    level = jnp.arange(dose_levels.shape[0], dtype=jnp.int32)
    chosen = (both[:, 4:, None] == level[None, None, :]).astype(jnp.float32)
    doses_by_gauge = STEEPNESS * jnp.sum(chosen * dose_levels[None, None, :], axis=2)

    total = None
    for k in range(CHUNKS):
        mine = lax.dynamic_slice(clips, (0, core * half + k * step), (cached, step))
        theirs = lax.dynamic_slice(clips, (0, (1 - core) * half + k * step), (cached, step))
        pieces = {0: jnp.concatenate([mine, swap(theirs, "gauge", 1)], axis=0)}
        order = wide if k % 2 == 0 else wide[::-1]
        have = [0]
        for bit in order:
            for o in list(have):
                pieces[o ^ bit] = swap(pieces[o], "gauge", bit)
                have.append(o ^ bit)
        block = (core * CHUNKS + k).astype(jnp.int32)[None]
        total = resist_rows(
            block,
            STEEPNESS * threshold,
            doses_by_gauge,
            select,
            [pieces[o] for o in offsets],
            basis_terms,
            total,
            doses,
        )
    rows = gauges * doses
    other = swap(total[rows:], "gauge", 1)

    count = terms // TILE
    table = piece_table(count)
    scale = float(rows * gauge_count * focus_count) ** (-0.5)
    slot = (me % PIECES).astype(jnp.int32)[None]
    vmem = pl.BlockSpec(memory_space=pltpu.VMEM)
    smem = pl.BlockSpec(memory_space=pltpu.SMEM)
    feat, misfit, deriv, packed = pl.pallas_call(
        functools.partial(normal_kernel, scale, table),
        grid=(1,),
        in_specs=[
            smem,
            pl.BlockSpec((rows, terms), lambda i: (0, 0)),
            pl.BlockSpec((rows, terms), lambda i: (0, 0)),
            pl.BlockSpec((gauges, doses), lambda i: (0, 0)),
            pl.BlockSpec((1, terms), lambda i: (0, 0)),
        ],
        out_specs=(
            pl.BlockSpec((rows, terms), lambda i: (0, 0)),
            pl.BlockSpec((gauges, doses), lambda i: (0, 0)),
            pl.BlockSpec((gauges, doses), lambda i: (0, 0)),
            pl.BlockSpec((PIECES, PIECE_ROWS, TILE), lambda i: (0, 0, 0)),
        ),
        out_shape=(
            jax.ShapeDtypeStruct((rows, terms), jnp.float32),
            jax.ShapeDtypeStruct((gauges, doses), jnp.float32),
            jax.ShapeDtypeStruct((gauges, doses), jnp.float32),
            jax.ShapeDtypeStruct((PIECES, PIECE_ROWS, TILE), jnp.float32),
        ),
        scratch_shapes=[pltpu.VMEM((rows, terms), jnp.float32)],
        compiler_params=pltpu.CompilerParams(vmem_limit_bytes=VMEM_BYTES),
        name="normal",
    )(slot, total, other, measured[0], parameters[None, :])

    halving, others = gauge_bits[:HALVINGS], gauge_bits[HALVINGS:]
    current = packed
    for bit in halving:
        keep = current.shape[0] // 2
        current = current[:keep] + swap(current[keep:], "gauge", bit)
    for bit in others:
        current = current + swap(current, "gauge", bit)
    for bit in bits_of(focus_count):
        current = current + swap(current, "focus", bit)
    parts = [current]
    for bit in halving[::-1]:
        parts = parts + [swap(part, "gauge", bit) for part in parts]
    groups = [[flipped(k)] for k in range(PIECES)]

    upper, new_params, residual = pl.pallas_call(
        functools.partial(factor_kernel, table, groups),
        in_specs=[smem] + [vmem] * (len(parts) + 4),
        out_specs=(vmem, vmem, vmem),
        out_shape=(
            jax.ShapeDtypeStruct((terms, terms), jnp.float32),
            jax.ShapeDtypeStruct((1, terms), jnp.float32),
            jax.ShapeDtypeStruct((gauges, doses), jnp.float32),
        ),
        scratch_shapes=[
            pltpu.VMEM((PIECES, PIECE_ROWS, TILE), jnp.float32),
            pltpu.VMEM((terms, terms), jnp.float32),
            pltpu.VMEM((terms, TILE), jnp.float32),
            pltpu.VMEM((8, terms), jnp.float32),
        ],
        compiler_params=pltpu.CompilerParams(vmem_limit_bytes=VMEM_BYTES),
        name="factor",
    )(slot, *parts, feat, misfit, deriv, parameters[None, :])
    return upper, new_params[0], residual[None]


def solution(mesh):
    return jax.shard_map(
        local,
        mesh=mesh,
        in_specs=(
            P("focus", "gauge", None),
            P(),
            P("focus", "gauge", None),
            P("focus", "gauge", None),
            P("focus", "gauge", None),
            P(),
            P("focus"),
            P("focus", "gauge", None),
            P(),
        ),
        out_specs=(P(), P(), P("focus", "gauge", None)),
        check_vma=False,
    )
```

time: 2200 us -> 132 us (0.06); the launches traced: 2160 us -> 132 us
  matrix products: 1400 us -> 0 us
  loops' own time: 368 us -> 0 us
  waiting for transfers between devices: 137 us -> 33.6 us
  other arithmetic: 96.3 us -> 5 us
  local copies, waits for them, and re-layouts: 85.7 us -> 10.8 us
  Pallas kernels: 0 us -> 52.9 us
  blocking collectives: 49.2 us -> 0 us
  starting transfers between devices: 4.72 us -> 27.8 us
    dot_general x2617 -> x0, matrix products: 1400 us -> none  [the longest x2614 1380 us: high_dot(): return jnp.dot(left, right, precision=lax.Precision.HIGHEST)]
    another operation x16 -> x0, loops' own time: 368 us -> none  [the longest x8 364 us: factor_block(): lax.fori_loop(0, width, column_step, jnp.zeros((width, width), jnp.float32))]
    psum x1 -> x0, waiting for transfers between devices: 88.9 us -> none  [local(): lax.psum((normal_mat, projected), ('gauge', 'focus'))]
    add x1027 -> x6, other arithmetic: 81.1 us -> 1.88 us  [the longest x3 1.02 us: local(): current = current[:keep] + swap(current[keep:], 'gauge', bit)]
    pallas_call x0 -> x6, Pallas kernels: none -> 52.9 us  [the longest x4 23.8 us: resist_rows(): pl.pallas_call(functools.partial(resist_kernel, first, gauges, doses), ou...]
    all_to_all x1 -> x0, waiting for transfers between devices: 47.8 us -> none  [local(): lax.all_to_all(picked, 'gauge', split_axis=0, concat_axis=0, tiled=True)]
    psum x1 -> x0, blocking collectives: 39.5 us -> none  [local(): lax.psum((normal_mat, projected), ('gauge', 'focus'))]
    ppermute x0 -> x30, waiting for transfers between devices: none -> 33.6 us  [swap(): return lax.ppermute(value, axis, [(i, i ^ bit) for i in range(size)])]
where the time goes in v1:
time: 132 us
  Pallas kernels  52.9 us (40%)
  waiting for transfers between devices  33.6 us (25%)
  starting transfers between devices  27.8 us (21%)
  local copies, waits for them, and re-layouts  10.8 us (8%)
  other arithmetic  5 us (4%)
  between operations  1.64 us (1%)
    ppermute x30, waiting for transfers between devices, swap(): return lax.ppermute(value, axis, [(i, i ^ bit) for i in range(size)])  33.6 us
    ppermute x30, starting transfers between devices, swap(): return lax.ppermute(value, axis, [(i, i ^ bit) for i in range(size)])  27.8 us
    pallas_call x4, Pallas kernels, resist_rows(): pl.pallas_call(functools.partial(resist_kernel, first, gauges, doses), ou...  23.8 us
    pallas_call x1, Pallas kernels, local(): pl.pallas_call(functools.partial(factor_kernel, table, groups), in_specs=...  23.7 us
    unnamed x57, local copies, waits for them, and re-layouts  6.85 us
    pallas_call x1, Pallas kernels, local(): pl.pallas_call(functools.partial(normal_kernel, scale, table), grid=(1,),...  5.43 us
  transfers between devices with their start and end apart: 30, of which 14 were waited for; matrix products, arithmetic and copies ran while one was open for 4% of the time, Pallas kernels for 13%

profile of v1, /device:TPU:0, one launch (start us, length us, event | category | flops | bytes accessed | tf_op | source)
XLA Modules:
  0.0 131.7 jit_solution(18031513370591711527)
XLA Ops:
  2.5 1.4 %dynamic-slice_bitcast_fusion.1 = (bf16[64,1024]{1,0:T(8,128)(2,1)S(1)}, bf16[64,1024]{1,0:T(8,128)(2,1)S(1)}, bf16[64,1024]{1,0:T(8,128)(2,1)S(1)}, bf16[64,102...) fusion(bf16[1,64,8192]{2,1,0:T(8,128)(2,1)} %param.9, ...), kind=kLoop, calls=%fused_computation.10 | loop fusion | bytes 2097184 | tf_op jit(solution)/shard_map/dynamic_slice | solution.py:338
  8.1 2.6 %collective-permute-start.14 = (bf16[128,1024]{1,0:T(8,128)(2,1)S(1)}, bf16[128,1024]{1,0:T(8,128)(2,1)S(1)}, u32[]{:S(2)}, u32[]{:S(2)}) collective-permute-start(bf16[128,1024]{1,0:T(8,128)(2,1)S(1)} %pad_maximum_fusion.3.refs_0_), channel_id=1, source_target_pairs={{0,8},{4,12},{8,0},{12,4},{16,24},{20,28},{24,16},{28,20},{1,9},{5... | collective-permute-start | bytes 786440 | tf_op jit(solution)/shard_map/ppermute | solution.py:32
  10.8 1.5 %collective-permute-start.15 = (bf16[128,1024]{1,0:T(8,128)(2,1)S(1)}, bf16[128,1024]{1,0:T(8,128)(2,1)S(1)}, u32[]{:S(2)}, u32[]{:S(2)}) collective-permute-start(bf16[128,1024]{1,0:T(8,128)(2,1)S(1)} %pad_maximum_fusion.3.refs_0_), channel_id=1, source_target_pairs={{0,16},{4,20},{8,24},{12,28},{16,0},{20,4},{24,8},{28,12},{1,17},{... | collective-permute-start | bytes 786440 | tf_op jit(solution)/shard_map/ppermute | solution.py:32
  13.3 2.0 %collective-permute-start.6 = (bf16[128,1024]{1,0:T(8,128)(2,1)S(1)}, bf16[128,1024]{1,0:T(8,128)(2,1)S(1)}, u32[]{:S(2)}, u32[]{:S(2)}) collective-permute-start(bf16[128,1024]{1,0:T(8,128)(2,1)S(1)} %pad_maximum_fusion.1.refs_0_), channel_id=1, source_target_pairs={{0,8},{4,12},{8,0},{12,4},{16,24},{20,28},{24,16},{28,20},{1,9},{5... | collective-permute-start | bytes 786440 | tf_op jit(solution)/shard_map/ppermute | solution.py:32
  15.3 2.6 %collective-permute-done.14.refs_1_ = bf16[128,1024]{1,0:T(8,128)(2,1)S(1)} collective-permute-done((bf16[128,1024]{1,0:T(8,128)(2,1)S(1)}, bf16[128,1024]{1,0:T(8,128)(2,1)S(1)}, u32[]{:S(2)}, u32[]{:S(2)}) %collective-permute-start.14) | collective-permute-done | bytes 262176 | tf_op jit(solution)/shard_map/ppermute | solution.py:32
  17.9 2.0 %collective-permute-start.16 = (bf16[128,1024]{1,0:T(8,128)(2,1)S(1)}, bf16[128,1024]{1,0:T(8,128)(2,1)S(1)}, u32[]{:S(2)}, u32[]{:S(2)}) collective-permute-start(bf16[128,1024]{1,0:T(8,128)(2,1)S(1)} %collective-permute-done.14.refs_1_), channel_id=1, source_target_pairs={{0,16},{4,20},{8,24},{12,28},{16,0},{20,4},{24,8},{28,12},{1,17},{... | collective-permute-start | bytes 786440 | tf_op jit(solution)/shard_map/ppermute | solution.py:32
  20.0 1.5 %collective-permute-start.3 = (bf16[128,1024]{1,0:T(8,128)(2,1)S(1)}, bf16[128,1024]{1,0:T(8,128)(2,1)S(1)}, u32[]{:S(2)}, u32[]{:S(2)}) collective-permute-start(bf16[128,1024]{1,0:T(8,128)(2,1)S(1)} %pad_maximum_fusion.refs_0_), channel_id=1, source_target_pairs={{0,16},{4,20},{8,24},{12,28},{16,0},{20,4},{24,8},{28,12},{1,17},{... | collective-permute-start | bytes 786440 | tf_op jit(solution)/shard_map/ppermute | solution.py:32
  21.4 4.1 %collective-permute-done.11.refs_2_ = bf16[128,1024]{1,0:T(8,128)(2,1)S(1)} collective-permute-done((bf16[128,1024]{1,0:T(8,128)(2,1)S(1)}, bf16[128,1024]{1,0:T(8,128)(2,1)S(1)}, u32[]{:S(2)}, u32[]{:S(2)}) %collective-permute-start.11) | collective-permute-done | bytes 262176 | tf_op jit(solution)/shard_map/ppermute | solution.py:32
  26.3 2.9 %collective-permute-done.6.refs_1_ = bf16[128,1024]{1,0:T(8,128)(2,1)S(1)} collective-permute-done((bf16[128,1024]{1,0:T(8,128)(2,1)S(1)}, bf16[128,1024]{1,0:T(8,128)(2,1)S(1)}, u32[]{:S(2)}, u32[]{:S(2)}) %collective-permute-start.6) | collective-permute-done | bytes 262176 | tf_op jit(solution)/shard_map/ppermute | solution.py:32
  29.2 2.0 %collective-permute-start.7 = (bf16[128,1024]{1,0:T(8,128)(2,1)S(1)}, bf16[128,1024]{1,0:T(8,128)(2,1)S(1)}, u32[]{:S(2)}, u32[]{:S(2)}) collective-permute-start(bf16[128,1024]{1,0:T(8,128)(2,1)S(1)} %pad_maximum_fusion.1.refs_0_), channel_id=1, source_target_pairs={{0,16},{4,20},{8,24},{12,28},{16,0},{20,4},{24,8},{28,12},{1,17},{... | collective-permute-start | bytes 786440 | tf_op jit(solution)/shard_map/ppermute | solution.py:32
  31.2 1.5 %collective-permute-start.8 = (bf16[128,1024]{1,0:T(8,128)(2,1)S(1)}, bf16[128,1024]{1,0:T(8,128)(2,1)S(1)}, u32[]{:S(2)}, u32[]{:S(2)}) collective-permute-start(bf16[128,1024]{1,0:T(8,128)(2,1)S(1)} %collective-permute-done.6.refs_1_), channel_id=1, source_target_pairs={{0,16},{4,20},{8,24},{12,28},{16,0},{20,4},{24,8},{28,12},{1,17},{... | collective-permute-start | bytes 786440 | tf_op jit(solution)/shard_map/ppermute | solution.py:32
  32.7 5.2 %resist.4.refs_5_ = f32[1408,512]{1,0:T(8,128)} custom-call(s32[1]{0:T(128)} %bitcast.14.block_ref, f32[1]{0:T(128)S(6)} %mul.21.threshold_ref, f32[128,11]{1,0:T(8,128)} %broadcast_multiply_fusion.dose_ref, bf16[128,512]{1,0:T(8,128)(2,1)} %add_convert_fusion.select_ref, bf16[128,1024]{1,0:T(8,128)(2,1)} %copy-done.4, bf16[128,1024]{1,0:T(8,128)(2,1)} %copy-done.15, ...), custom_call_target="tpu_custom_call" | custom-call | flops 1476395008 | bytes 7864320 | tf_op jit(solution)/shard_map/resist/pallas_call | solution.py:113
  38.7 1.4 %collective-permute-start.4 = (bf16[128,1024]{1,0:T(8,128)(2,1)S(1)}, bf16[128,1024]{1,0:T(8,128)(2,1)S(1)}, u32[]{:S(2)}, u32[]{:S(2)}) collective-permute-start(bf16[128,1024]{1,0:T(8,128)(2,1)S(1)} %collective-permute-done.3.refs_2_), channel_id=1, source_target_pairs={{0,8},{4,12},{8,0},{12,4},{16,24},{20,28},{24,16},{28,20},{1,9},{5... | collective-permute-start | bytes 786440 | tf_op jit(solution)/shard_map/ppermute | solution.py:32
  40.8 6.2 %resist.5.refs_5_ = f32[1408,512]{1,0:T(8,128)} custom-call(s32[1]{0:T(128)} %bitcast.11.block_ref, f32[1]{0:T(128)S(6)} %mul.21.threshold_ref, f32[128,11]{1,0:T(8,128)} %broadcast_multiply_fusion.dose_ref, bf16[128,512]{1,0:T(8,128)(2,1)} %add_convert_fusion.select_ref, bf16[128,1024]{1,0:T(8,128)(2,1)} %copy-done.1, ...), custom_call_target="tpu_custom_call", output_to_operand_aliasing={{}: (9, {})} | custom-call | flops 1476395008 | bytes 7864320 | tf_op jit(solution)/shard_map/resist/pallas_call | solution.py:113
  47.9 6.2 %resist.6.refs_5_ = f32[1408,512]{1,0:T(8,128)} custom-call(s32[1]{0:T(128)} %bitcast.8.block_ref, f32[1]{0:T(128)S(6)} %mul.21.threshold_ref, f32[128,11]{1,0:T(8,128)} %broadcast_multiply_fusion.dose_ref, bf16[128,512]{1,0:T(8,128)(2,1)} %add_convert_fusion.select_ref, bf16[128,1024]{1,0:T(8,128)(2,1)} %copy-done.2, ...), custom_call_target="tpu_custom_call", output_to_operand_aliasing={{}: (9, {})} | custom-call | flops 1476395008 | bytes 7864320 | tf_op jit(solution)/shard_map/resist/pallas_call | solution.py:113
  54.9 6.2 %resist.7.mine_ref = f32[1408,512]{1,0:T(8,128)} custom-call(s32[1]{0:T(128)} %bitcast.1.block_ref, f32[1]{0:T(128)S(6)} %mul.21.threshold_ref, f32[128,11]{1,0:T(8,128)} %broadcast_multiply_fusion.dose_ref, bf16[128,512]{1,0:T(8,128)(2,1)} %add_convert_fusion.select_ref, bf16[128,1024]{1,0:T(8,128)(2,1)} %copy-done.3, ...), custom_call_target="tpu_custom_call", output_to_operand_aliasing={{}: (9, {})} | custom-call | flops 1476395008 | bytes 7864320 | tf_op jit(solution)/shard_map/resist/pallas_call | solution.py:113
  61.1 1.5 %slice.49 = f32[704,512]{1,0:T(8,128)S(1)} slice(f32[1408,512]{1,0:T(8,128)} %resist.7.mine_ref), slice={[704:1408], [0:512]} | slice | bytes 2883584 | tf_op jit(solution)/shard_map/slice | solution.py:359
  63.4 2.5 %collective-permute-done.17.other_ref = f32[704,512]{1,0:T(8,128)S(1)} collective-permute-done((f32[704,512]{1,0:T(8,128)S(1)}, f32[704,512]{1,0:T(8,128)S(1)}, u32[]{:S(2)}, u32[]{:S(2)}) %collective-permute-start.17) | collective-permute-done | bytes 1441824 | tf_op jit(solution)/shard_map/ppermute | solution.py:32
  67.0 5.4 %normal.1 = (f32[704,512]{1,0:T(8,128)}, f32[64,11]{1,0:T(8,128)}, f32[64,11]{1,0:T(8,128)}, f32[8,136,128]{2,1,0:T(8,128)}) custom-call(s32[1]{0:T(128)} %bitcast.me_ref, f32[1408,512]{1,0:T(8,128)} %resist.7.mine_ref, f32[704,512]{1,0:T(8,128)} %copy-done, f32[64,11]{1,0:T(8,128)} %bitcast.34, f32[1,512]{1,0:T(1,128)} %bitcast.45), custom_call_target="tpu_custom_call" | custom-call | tf_op jit(solution)/shard_map/normal/pallas_call | solution.py:367
  73.6 1.4 %collective-permute-done.18 = f32[4,136,128]{2,1,0:T(8,128)S(1)} collective-permute-done((f32[4,136,128]{2,1,0:T(8,128)S(1)}, f32[4,136,128]{2,1,0:T(8,128)S(1)}, u32[]{:S(2)}, u32[]{:S(2)}) %collective-permute-start.18) | collective-permute-done | bytes 278560 | tf_op jit(solution)/shard_map/ppermute | solution.py:32
  76.7 5.2 %collective-permute-done.19 = f32[2,136,128]{2,1,0:T(8,128)S(1)} collective-permute-done((f32[2,136,128]{2,1,0:T(8,128)S(1)}, f32[2,136,128]{2,1,0:T(8,128)S(1)}, u32[]{:S(2)}, u32[]{:S(2)}) %collective-permute-start.19) | collective-permute-done | bytes 139296 | tf_op jit(solution)/shard_map/ppermute | solution.py:32
  81.9 1.6 %collective-permute-start.20 = (f32[1,136,128]{2,1,0:T(8,128)S(1)}, f32[1,136,128]{2,1,0:T(8,128)S(1)}, u32[]{:S(2)}, u32[]{:S(2)}) collective-permute-start(f32[1,136,128]{2,1,0:T(8,128)S(1)} %slice.53), channel_id=1, source_target_pairs={{0,16},{4,20},{8,24},{12,28},{16,0},{20,4},{24,8},{28,12},{1,17},{... | collective-permute-start | bytes 208904 | tf_op jit(solution)/shard_map/ppermute | solution.py:32
  83.5 2.8 %collective-permute-done.20 = f32[1,136,128]{2,1,0:T(8,128)S(1)} collective-permute-done((f32[1,136,128]{2,1,0:T(8,128)S(1)}, f32[1,136,128]{2,1,0:T(8,128)S(1)}, u32[]{:S(2)}, u32[]{:S(2)}) %collective-permute-start.20) | collective-permute-done | bytes 69664 | tf_op jit(solution)/shard_map/ppermute | solution.py:32
  86.3 1.6 %collective-permute-start.21 = (f32[1,136,128]{2,1,0:T(8,128)S(1)}, f32[1,136,128]{2,1,0:T(8,128)S(1)}, u32[]{:S(2)}, u32[]{:S(2)}) collective-permute-start(f32[1,136,128]{2,1,0:T(8,128)S(1)} %slice_add_fusion.2), channel_id=1, source_target_pairs={{0,1},{1,0},{2,3},{3,2},{4,5},{5,4},{6,7},{7,6},{8,9},{9,8},{10,11... | collective-permute-start | bytes 208904 | tf_op jit(solution)/shard_map/ppermute | solution.py:32
  87.9 2.7 %collective-permute-done.21 = f32[1,136,128]{2,1,0:T(8,128)S(1)} collective-permute-done((f32[1,136,128]{2,1,0:T(8,128)S(1)}, f32[1,136,128]{2,1,0:T(8,128)S(1)}, u32[]{:S(2)}, u32[]{:S(2)}) %collective-permute-start.21) | collective-permute-done | bytes 69664 | tf_op jit(solution)/shard_map/ppermute | solution.py:32
  90.7 3.1 %collective-permute-start.22 = (f32[1,136,128]{2,1,0:T(8,128)S(1)}, f32[1,136,128]{2,1,0:T(8,128)S(1)}, u32[]{:S(2)}, u32[]{:S(2)}) collective-permute-start(f32[1,136,128]{2,1,0:T(8,128)S(1)} %add.111), channel_id=1, source_target_pairs={{0,2},{1,3},{2,0},{3,1},{4,6},{5,7},{6,4},{7,5},{8,10},{9,11},{10,... | collective-permute-start | bytes 208904 | tf_op jit(solution)/shard_map/ppermute | solution.py:32
  93.7 2.3 %collective-permute-done.22 = f32[1,136,128]{2,1,0:T(8,128)S(1)} collective-permute-done((f32[1,136,128]{2,1,0:T(8,128)S(1)}, f32[1,136,128]{2,1,0:T(8,128)S(1)}, u32[]{:S(2)}, u32[]{:S(2)}) %collective-permute-start.22) | collective-permute-done | bytes 69664 | tf_op jit(solution)/shard_map/ppermute | solution.py:32
  96.1 1.6 %collective-permute-start.23 = (f32[1,136,128]{2,1,0:T(8,128)S(1)}, f32[1,136,128]{2,1,0:T(8,128)S(1)}, u32[]{:S(2)}, u32[]{:S(2)}) collective-permute-start(f32[1,136,128]{2,1,0:T(8,128)S(1)} %add.112.refs_0_), channel_id=1, source_target_pairs={{0,16},{4,20},{8,24},{12,28},{16,0},{20,4},{24,8},{28,12},{1,17},{... | collective-permute-start | bytes 208904 | tf_op jit(solution)/shard_map/ppermute | solution.py:32
  98.2 2.3 %collective-permute-done.23.refs_1_ = f32[1,136,128]{2,1,0:T(8,128)S(1)} collective-permute-done((f32[1,136,128]{2,1,0:T(8,128)S(1)}, f32[1,136,128]{2,1,0:T(8,128)S(1)}, u32[]{:S(2)}, u32[]{:S(2)}) %collective-permute-start.23) | collective-permute-done | bytes 69664 | tf_op jit(solution)/shard_map/ppermute | solution.py:32
  102.0 2.8 %collective-permute-done.25.refs_3_ = f32[1,136,128]{2,1,0:T(8,128)S(1)} collective-permute-done((f32[1,136,128]{2,1,0:T(8,128)S(1)}, f32[1,136,128]{2,1,0:T(8,128)S(1)}, u32[]{:S(2)}, u32[]{:S(2)}) %collective-permute-start.25) | collective-permute-done | bytes 69664 | tf_op jit(solution)/shard_map/ppermute | solution.py:32
  106.6 23.7 %factor.1 = (f32[512,512]{1,0:T(8,128)}, f32[1,512]{1,0:T(1,128)}, f32[64,11]{1,0:T(8,128)}) custom-call(s32[1]{0:T(128)} %bitcast.me_ref, f32[1,136,128]{2,1,0:T(8,128)} %copy-done.5, f32[1,136,128]{2,1,0:T(8,128)} %copy-done.18, f32[1,136,128]{2,1,0:T(8,128)} %copy-done.19, f32[1,136,128]{2,1,0:T(8,128)} %copy-done.20, f32[1,136,128]{2,1,0:T(8,128)} %copy-done.21, ...), custom_call_target="tpu_custom_call" | custom-call | tf_op jit(solution)/shard_map/factor/pallas_call | solution.py:408
  130.3 1.4 %copy.20 = f32[1,64,11]{1,0,2:T(1,128)} copy(f32[1,64,11]{2,1,0:T(8,128)} %bitcast.38) | data formatting | bytes 5632
  (114 shorter events, 19.0 us)
Async XLA Ops:
  2.0 3.6 %collective-permute-start = (s32[64,15]{0,1:T(8,128)S(1)}, s32[64,15]{0,1:T(8,128)S(1)}, u32[]{:S(2)}, u32[]{:S(2)}) collective-permute-start(s32[64,15]{0,1:T(8,128)S(1)} %pad_add_fusion), channel_id=1, source_target_pairs={{0,4},{4,0},{8,12},{12,8},{16,20},{20,16},{24,28},{28,24},{1,5},{5... | collective-permute-start | bytes 11528 | tf_op jit(solution)/shard_map/ppermute | solution.py:32
  3.9 4.2 %collective-permute-start.13 = (bf16[64,1024]{1,0:T(8,128)(2,1)S(1)}, bf16[64,1024]{1,0:T(8,128)(2,1)S(1)}, u32[]{:S(2)}, u32[]{:S(2)}) collective-permute-start(bf16[64,1024]{1,0:T(8,128)(2,1)S(1)} %get-tuple-element.30), channel_id=1, source_target_pairs={{0,4},{4,0},{8,12},{12,8},{16,20},{20,16},{24,28},{28,24},{1,5},{5... | collective-permute-start | bytes 393224 | tf_op jit(solution)/shard_map/ppermute | solution.py:32
  4.1 8.2 %collective-permute-start.9 = (bf16[64,1024]{1,0:T(8,128)(2,1)S(1)}, bf16[64,1024]{1,0:T(8,128)(2,1)S(1)}, u32[]{:S(2)}, u32[]{:S(2)}) collective-permute-start(bf16[64,1024]{1,0:T(8,128)(2,1)S(1)} %get-tuple-element.24), channel_id=1, source_target_pairs={{0,4},{4,0},{8,12},{12,8},{16,20},{20,16},{24,28},{28,24},{1,5},{5... | collective-permute-start | bytes 393224 | tf_op jit(solution)/shard_map/ppermute | solution.py:32
  4.5 8.6 %collective-permute-start.5 = (bf16[64,1024]{1,0:T(8,128)(2,1)S(1)}, bf16[64,1024]{1,0:T(8,128)(2,1)S(1)}, u32[]{:S(2)}, u32[]{:S(2)}) collective-permute-start(bf16[64,1024]{1,0:T(8,128)(2,1)S(1)} %get-tuple-element.26), channel_id=1, source_target_pairs={{0,4},{4,0},{8,12},{12,8},{16,20},{20,16},{24,28},{28,24},{1,5},{5... | collective-permute-start | bytes 393224 | tf_op jit(solution)/shard_map/ppermute | solution.py:32
  4.6 8.7 %collective-permute-start.1 = (bf16[64,1024]{1,0:T(8,128)(2,1)S(1)}, bf16[64,1024]{1,0:T(8,128)(2,1)S(1)}, u32[]{:S(2)}, u32[]{:S(2)}) collective-permute-start(bf16[64,1024]{1,0:T(8,128)(2,1)S(1)} %get-tuple-element.28), channel_id=1, source_target_pairs={{0,4},{4,0},{8,12},{12,8},{16,20},{20,16},{24,28},{28,24},{1,5},{5... | collective-permute-start | bytes 393224 | tf_op jit(solution)/shard_map/ppermute | solution.py:32
  8.1 9.8 %collective-permute-start.14 = (bf16[128,1024]{1,0:T(8,128)(2,1)S(1)}, bf16[128,1024]{1,0:T(8,128)(2,1)S(1)}, u32[]{:S(2)}, u32[]{:S(2)}) collective-permute-start(bf16[128,1024]{1,0:T(8,128)(2,1)S(1)} %pad_maximum_fusion.3.refs_0_), channel_id=1, source_target_pairs={{0,8},{4,12},{8,0},{12,4},{16,24},{20,28},{24,16},{28,20},{1,9},{5... | collective-permute-start | bytes 786440 | tf_op jit(solution)/shard_map/ppermute | solution.py:32
  10.8 9.2 %collective-permute-start.15 = (bf16[128,1024]{1,0:T(8,128)(2,1)S(1)}, bf16[128,1024]{1,0:T(8,128)(2,1)S(1)}, u32[]{:S(2)}, u32[]{:S(2)}) collective-permute-start(bf16[128,1024]{1,0:T(8,128)(2,1)S(1)} %pad_maximum_fusion.3.refs_0_), channel_id=1, source_target_pairs={{0,16},{4,20},{8,24},{12,28},{16,0},{20,4},{24,8},{28,12},{1,17},{... | collective-permute-start | bytes 786440 | tf_op jit(solution)/shard_map/ppermute | solution.py:32
  12.3 25.6 %copy-start.1 = (bf16[128,1024]{1,0:T(8,128)(2,1)}, bf16[128,1024]{1,0:T(8,128)(2,1)S(1)}, u32[]{:S(2)}) copy-start(bf16[128,1024]{1,0:T(8,128)(2,1)S(1)} %pad_maximum_fusion.2.refs_0_) | copy-start | bytes 786436
  12.3 13.2 %collective-permute-start.11 = (bf16[128,1024]{1,0:T(8,128)(2,1)S(1)}, bf16[128,1024]{1,0:T(8,128)(2,1)S(1)}, u32[]{:S(2)}, u32[]{:S(2)}) collective-permute-start(bf16[128,1024]{1,0:T(8,128)(2,1)S(1)} %pad_maximum_fusion.2.refs_0_), channel_id=1, source_target_pairs={{0,16},{4,20},{8,24},{12,28},{16,0},{20,4},{24,8},{28,12},{1,17},{... | collective-permute-start | bytes 786440 | tf_op jit(solution)/shard_map/ppermute | solution.py:32
  13.1 24.8 %collective-permute-start.10 = (bf16[128,1024]{1,0:T(8,128)(2,1)S(1)}, bf16[128,1024]{1,0:T(8,128)(2,1)S(1)}, u32[]{:S(2)}, u32[]{:S(2)}) collective-permute-start(bf16[128,1024]{1,0:T(8,128)(2,1)S(1)} %pad_maximum_fusion.2.refs_0_), channel_id=1, source_target_pairs={{0,8},{4,12},{8,0},{12,4},{16,24},{20,28},{24,16},{28,20},{1,9},{5... | collective-permute-start | bytes 786440 | tf_op jit(solution)/shard_map/ppermute | solution.py:32
  13.3 24.7 %copy-start.2 = (bf16[128,1024]{1,0:T(8,128)(2,1)}, bf16[128,1024]{1,0:T(8,128)(2,1)S(1)}, u32[]{:S(2)}) copy-start(bf16[128,1024]{1,0:T(8,128)(2,1)S(1)} %pad_maximum_fusion.1.refs_0_) | copy-start | bytes 786436
  13.3 15.9 %collective-permute-start.6 = (bf16[128,1024]{1,0:T(8,128)(2,1)S(1)}, bf16[128,1024]{1,0:T(8,128)(2,1)S(1)}, u32[]{:S(2)}, u32[]{:S(2)}) collective-permute-start(bf16[128,1024]{1,0:T(8,128)(2,1)S(1)} %pad_maximum_fusion.1.refs_0_), channel_id=1, source_target_pairs={{0,8},{4,12},{8,0},{12,4},{16,24},{20,28},{24,16},{28,20},{1,9},{5... | collective-permute-start | bytes 786440 | tf_op jit(solution)/shard_map/ppermute | solution.py:32
  17.9 13.2 %collective-permute-start.16 = (bf16[128,1024]{1,0:T(8,128)(2,1)S(1)}, bf16[128,1024]{1,0:T(8,128)(2,1)S(1)}, u32[]{:S(2)}, u32[]{:S(2)}) collective-permute-start(bf16[128,1024]{1,0:T(8,128)(2,1)S(1)} %collective-permute-done.14.refs_1_), channel_id=1, source_target_pairs={{0,16},{4,20},{8,24},{12,28},{16,0},{20,4},{24,8},{28,12},{1,17},{... | collective-permute-start | bytes 786440 | tf_op jit(solution)/shard_map/ppermute | solution.py:32
  20.0 18.8 %collective-permute-start.3 = (bf16[128,1024]{1,0:T(8,128)(2,1)S(1)}, bf16[128,1024]{1,0:T(8,128)(2,1)S(1)}, u32[]{:S(2)}, u32[]{:S(2)}) collective-permute-start(bf16[128,1024]{1,0:T(8,128)(2,1)S(1)} %pad_maximum_fusion.refs_0_), channel_id=1, source_target_pairs={{0,16},{4,20},{8,24},{12,28},{16,0},{20,4},{24,8},{28,12},{1,17},{... | collective-permute-start | bytes 786440 | tf_op jit(solution)/shard_map/ppermute | solution.py:32
  25.5 14.5 %collective-permute-start.12 = (bf16[128,1024]{1,0:T(8,128)(2,1)S(1)}, bf16[128,1024]{1,0:T(8,128)(2,1)S(1)}, u32[]{:S(2)}, u32[]{:S(2)}) collective-permute-start(bf16[128,1024]{1,0:T(8,128)(2,1)S(1)} %collective-permute-done.11.refs_2_), channel_id=1, source_target_pairs={{0,8},{4,12},{8,0},{12,4},{16,24},{20,28},{24,16},{28,20},{1,9},{5... | collective-permute-start | bytes 786440 | tf_op jit(solution)/shard_map/ppermute | solution.py:32
  29.2 17.8 %collective-permute-start.7 = (bf16[128,1024]{1,0:T(8,128)(2,1)S(1)}, bf16[128,1024]{1,0:T(8,128)(2,1)S(1)}, u32[]{:S(2)}, u32[]{:S(2)}) collective-permute-start(bf16[128,1024]{1,0:T(8,128)(2,1)S(1)} %pad_maximum_fusion.1.refs_0_), channel_id=1, source_target_pairs={{0,16},{4,20},{8,24},{12,28},{16,0},{20,4},{24,8},{28,12},{1,17},{... | collective-permute-start | bytes 786440 | tf_op jit(solution)/shard_map/ppermute | solution.py:32
  31.2 16.1 %collective-permute-start.8 = (bf16[128,1024]{1,0:T(8,128)(2,1)S(1)}, bf16[128,1024]{1,0:T(8,128)(2,1)S(1)}, u32[]{:S(2)}, u32[]{:S(2)}) collective-permute-start(bf16[128,1024]{1,0:T(8,128)(2,1)S(1)} %collective-permute-done.6.refs_1_), channel_id=1, source_target_pairs={{0,16},{4,20},{8,24},{12,28},{16,0},{20,4},{24,8},{28,12},{1,17},{... | collective-permute-start | bytes 786440 | tf_op jit(solution)/shard_map/ppermute | solution.py:32
  38.0 16.1 %collective-permute-start.2 = (bf16[128,1024]{1,0:T(8,128)(2,1)S(1)}, bf16[128,1024]{1,0:T(8,128)(2,1)S(1)}, u32[]{:S(2)}, u32[]{:S(2)}) collective-permute-start(bf16[128,1024]{1,0:T(8,128)(2,1)S(1)} %pad_maximum_fusion.refs_0_), channel_id=1, source_target_pairs={{0,8},{4,12},{8,0},{12,4},{16,24},{20,28},{24,16},{28,20},{1,9},{5... | collective-permute-start | bytes 786440 | tf_op jit(solution)/shard_map/ppermute | solution.py:32
  38.7 15.4 %collective-permute-start.4 = (bf16[128,1024]{1,0:T(8,128)(2,1)S(1)}, bf16[128,1024]{1,0:T(8,128)(2,1)S(1)}, u32[]{:S(2)}, u32[]{:S(2)}) collective-permute-start(bf16[128,1024]{1,0:T(8,128)(2,1)S(1)} %collective-permute-done.3.refs_2_), channel_id=1, source_target_pairs={{0,8},{4,12},{8,0},{12,4},{16,24},{20,28},{24,16},{28,20},{1,9},{5... | collective-permute-start | bytes 786440 | tf_op jit(solution)/shard_map/ppermute | solution.py:32
  62.6 3.3 %collective-permute-start.17 = (f32[704,512]{1,0:T(8,128)S(1)}, f32[704,512]{1,0:T(8,128)S(1)}, u32[]{:S(2)}, u32[]{:S(2)}) collective-permute-start(f32[704,512]{1,0:T(8,128)S(1)} %slice.49), channel_id=1, source_target_pairs={{0,4},{4,0},{8,12},{12,8},{16,20},{20,16},{24,28},{28,24},{1,5},{5... | collective-permute-start | bytes 4325384 | tf_op jit(solution)/shard_map/ppermute | solution.py:32
  73.4 1.6 %collective-permute-start.18 = (f32[4,136,128]{2,1,0:T(8,128)S(1)}, f32[4,136,128]{2,1,0:T(8,128)S(1)}, u32[]{:S(2)}, u32[]{:S(2)}) collective-permute-start(f32[4,136,128]{2,1,0:T(8,128)S(1)} %slice.43), channel_id=1, source_target_pairs={{0,4},{4,0},{8,12},{12,8},{16,20},{20,16},{24,28},{28,24},{1,5},{5... | collective-permute-start | bytes 835592 | tf_op jit(solution)/shard_map/ppermute | solution.py:32
  76.1 5.8 %collective-permute-start.19 = (f32[2,136,128]{2,1,0:T(8,128)S(1)}, f32[2,136,128]{2,1,0:T(8,128)S(1)}, u32[]{:S(2)}, u32[]{:S(2)}) collective-permute-start(f32[2,136,128]{2,1,0:T(8,128)S(1)} %slice.51), channel_id=1, source_target_pairs={{0,8},{4,12},{8,0},{12,4},{16,24},{20,28},{24,16},{28,20},{1,9},{5... | collective-permute-start | bytes 417800 | tf_op jit(solution)/shard_map/ppermute | solution.py:32
  81.9 4.4 %collective-permute-start.20 = (f32[1,136,128]{2,1,0:T(8,128)S(1)}, f32[1,136,128]{2,1,0:T(8,128)S(1)}, u32[]{:S(2)}, u32[]{:S(2)}) collective-permute-start(f32[1,136,128]{2,1,0:T(8,128)S(1)} %slice.53), channel_id=1, source_target_pairs={{0,16},{4,20},{8,24},{12,28},{16,0},{20,4},{24,8},{28,12},{1,17},{... | collective-permute-start | bytes 208904 | tf_op jit(solution)/shard_map/ppermute | solution.py:32
  86.3 4.4 %collective-permute-start.21 = (f32[1,136,128]{2,1,0:T(8,128)S(1)}, f32[1,136,128]{2,1,0:T(8,128)S(1)}, u32[]{:S(2)}, u32[]{:S(2)}) collective-permute-start(f32[1,136,128]{2,1,0:T(8,128)S(1)} %slice_add_fusion.2), channel_id=1, source_target_pairs={{0,1},{1,0},{2,3},{3,2},{4,5},{5,4},{6,7},{7,6},{8,9},{9,8},{10,11... | collective-permute-start | bytes 208904 | tf_op jit(solution)/shard_map/ppermute | solution.py:32
  90.7 5.4 %collective-permute-start.22 = (f32[1,136,128]{2,1,0:T(8,128)S(1)}, f32[1,136,128]{2,1,0:T(8,128)S(1)}, u32[]{:S(2)}, u32[]{:S(2)}) collective-permute-start(f32[1,136,128]{2,1,0:T(8,128)S(1)} %add.111), channel_id=1, source_target_pairs={{0,2},{1,3},{2,0},{3,1},{4,6},{5,7},{6,4},{7,5},{8,10},{9,11},{10,... | collective-permute-start | bytes 208904 | tf_op jit(solution)/shard_map/ppermute | solution.py:32
  96.1 4.4 %collective-permute-start.23 = (f32[1,136,128]{2,1,0:T(8,128)S(1)}, f32[1,136,128]{2,1,0:T(8,128)S(1)}, u32[]{:S(2)}, u32[]{:S(2)}) collective-permute-start(f32[1,136,128]{2,1,0:T(8,128)S(1)} %add.112.refs_0_), channel_id=1, source_target_pairs={{0,16},{4,20},{8,24},{12,28},{16,0},{20,4},{24,8},{28,12},{1,17},{... | collective-permute-start | bytes 208904 | tf_op jit(solution)/shard_map/ppermute | solution.py:32
  97.6 4.3 %collective-permute-start.24 = (f32[1,136,128]{2,1,0:T(8,128)S(1)}, f32[1,136,128]{2,1,0:T(8,128)S(1)}, u32[]{:S(2)}, u32[]{:S(2)}) collective-permute-start(f32[1,136,128]{2,1,0:T(8,128)S(1)} %add.112.refs_0_), channel_id=1, source_target_pairs={{0,8},{4,12},{8,0},{12,4},{16,24},{20,28},{24,16},{28,20},{1,9},{5... | collective-permute-start | bytes 208904 | tf_op jit(solution)/shard_map/ppermute | solution.py:32
  100.4 4.3 %collective-permute-start.25 = (f32[1,136,128]{2,1,0:T(8,128)S(1)}, f32[1,136,128]{2,1,0:T(8,128)S(1)}, u32[]{:S(2)}, u32[]{:S(2)}) collective-permute-start(f32[1,136,128]{2,1,0:T(8,128)S(1)} %collective-permute-done.23.refs_1_), channel_id=1, source_target_pairs={{0,8},{4,12},{8,0},{12,4},{16,24},{20,28},{24,16},{28,20},{1,9},{5... | collective-permute-start | bytes 208904 | tf_op jit(solution)/shard_map/ppermute | solution.py:32
  101.0 3.8 %collective-permute-start.26 = (f32[1,136,128]{2,1,0:T(8,128)S(1)}, f32[1,136,128]{2,1,0:T(8,128)S(1)}, u32[]{:S(2)}, u32[]{:S(2)}) collective-permute-start(f32[1,136,128]{2,1,0:T(8,128)S(1)} %add.112.refs_0_), channel_id=1, source_target_pairs={{0,4},{4,0},{8,12},{12,8},{16,20},{20,16},{24,28},{28,24},{1,5},{5... | collective-permute-start | bytes 208904 | tf_op jit(solution)/shard_map/ppermute | solution.py:32
  101.0 3.8 %collective-permute-start.27 = (f32[1,136,128]{2,1,0:T(8,128)S(1)}, f32[1,136,128]{2,1,0:T(8,128)S(1)}, u32[]{:S(2)}, u32[]{:S(2)}) collective-permute-start(f32[1,136,128]{2,1,0:T(8,128)S(1)} %collective-permute-done.23.refs_1_), channel_id=1, source_target_pairs={{0,4},{4,0},{8,12},{12,8},{16,20},{20,16},{24,28},{28,24},{1,5},{5... | collective-permute-start | bytes 208904 | tf_op jit(solution)/shard_map/ppermute | solution.py:32
  102.0 2.8 %collective-permute-start.28 = (f32[1,136,128]{2,1,0:T(8,128)S(1)}, f32[1,136,128]{2,1,0:T(8,128)S(1)}, u32[]{:S(2)}, u32[]{:S(2)}) collective-permute-start(f32[1,136,128]{2,1,0:T(8,128)S(1)} %collective-permute-done.24.refs_2_), channel_id=1, source_target_pairs={{0,4},{4,0},{8,12},{12,8},{16,20},{20,16},{24,28},{28,24},{1,5},{5... | collective-permute-start | bytes 208904 | tf_op jit(solution)/shard_map/ppermute | solution.py:32
  104.8 1.3 collective-permute-start.29
  (25 other events, 147.1 us)

commit v2 on v1

--- a/solution.py
+++ b/solution.py
@@ -15,7 +15,11 @@
 PIECES = 1 << HALVINGS
 PIECE_ROWS = TILE + 8
 CHUNKS = 4
-VMEM_BYTES = 56 << 20
+VMEM_BYTES = 16 << 20
+RESIST_BYTES = 44 << 20
+VMEM = pl.BlockSpec(memory_space=pltpu.VMEM)
+ANY = pl.BlockSpec(memory_space=pl.ANY)
+SMEM = pl.BlockSpec(memory_space=pltpu.SMEM)
 HIGHEST = lax.Precision.HIGHEST
 
 
@@ -30,6 +34,21 @@
 def swap(value, axis, bit):
     size = lax.axis_size(axis)
     return lax.ppermute(value, axis, [(i, i ^ bit) for i in range(size)])
+
+
+def add_pairs(values):
+    while len(values) > 1:
+        values = [sum(values[i + 1 : i + 2], values[i]) for i in range(0, len(values), 2)]
+    return values[0]
+
+
+def exchange(value, axis, bits):
+    for i in range(0, len(bits), 2):
+        ways = [0]
+        for bit in bits[i : i + 2]:
+            ways = ways + [way | bit for way in ways]
+        value = add_pairs([swap(value, axis, way) if way else value for way in ways])
+    return value
 
 
 def dot_rows(left, right):
@@ -64,17 +83,27 @@
     return table
 
 
-def resist_kernel(first, gauges, doses, block_ref, threshold_ref, dose_ref, select_ref, *refs):
-    pieces = refs[: len(refs) - (3 if first else 4)]
-    rest = refs[len(pieces) :]
-    basis_ref = rest[0]
-    out_ref, rows_ref = rest[-2], rest[-1]
-    width = pieces[0].shape[0]
+def resist_kernel(first, start_ref, threshold_ref, dose_ref, select_ref, *refs):
+    count = len(refs) - (7 if first else 9)
+    pieces, basis_ref, rest = refs[:count], refs[count], refs[count + 1 :]
+    sums, outs = rest[: len(rest) - 6], rest[-6:-4]
+    rows_ref, piece_buf, basis_buf, sems = rest[-4:]
+    width, pixels = pieces[0].shape
+    gauges, doses = dose_ref.shape[0] // 2, dose_ref.shape[1]
+    start = pl.multiple_of(start_ref[0], pixels)
+    copies = [
+        pltpu.make_async_copy(piece, piece_buf.at[o], sems.at[o]) for o, piece in enumerate(pieces)
+    ]
+    fetch = pltpu.make_async_copy(basis_ref.at[pl.ds(start, pixels), :], basis_buf, sems.at[count])
+    for copy in copies:
+        copy.start()
+    fetch.start()
     picked = None
-    for o, piece in enumerate(pieces):
+    for o, copy in enumerate(copies):
+        copy.wait()
         term = jnp.dot(
             select_ref[:, o * width : (o + 1) * width],
-            piece[...],
+            piece_buf[o],
             preferred_element_type=jnp.float32,
         )
         picked = term if picked is None else picked + term
@@ -84,54 +113,47 @@
         for who in range(2):
             low = (who * doses + d) * gauges
             rows_ref[low : low + gauges, :] = answer[who * gauges : (who + 1) * gauges, :]
-    summed = jnp.dot(rows_ref[...], basis_ref[...], preferred_element_type=jnp.float32)
-    if first:
-        out_ref[...] = summed
-    else:
-        out_ref[...] = rest[1][...] + summed
-
-
-def resist_rows(block, threshold, doses_by_gauge, select, pieces, basis, total, doses):
-    pair = pieces[0].shape[0]
-    gauges = doses_by_gauge.shape[0] // 2
-    pixels = pieces[0].shape[1]
+    fetch.wait()
+    rows = gauges * doses
+    for who in (1, 0):
+        summed = jnp.dot(
+            rows_ref[who * rows : (who + 1) * rows, :], basis_buf[...], preferred_element_type=jnp.float32
+        )
+        outs[who][...] = summed if first else sums[who][...] + summed
+
+
+def resist_rows(start, threshold, dose, select, pieces, basis, totals):
+    doses = dose.shape[1]
+    gauges = dose.shape[0] // 2
+    pair, pixels = pieces[0].shape
     terms = basis.shape[1]
-    rows = 2 * gauges * doses
-    first = total is None
-    whole = lambda shape: pl.BlockSpec(shape, lambda i, s: (0, 0))
-    in_specs = [
-        pl.BlockSpec(memory_space=pltpu.SMEM),
-        whole(doses_by_gauge.shape),
-        whole(select.shape),
-        *[whole((pair, pixels)) for _ in pieces],
-        pl.BlockSpec((pixels, terms), lambda i, s: (s[0], 0)),
-    ]
-    operands = [threshold, doses_by_gauge, select, *pieces, basis]
-    if not first:
-        in_specs.append(whole((rows, terms)))
-        operands.append(total)
+    rows = gauges * doses
+    first = totals is None
+    operands = [dose, select, *pieces, basis] + ([] if first else list(totals))
+    shape = jax.ShapeDtypeStruct((rows, terms), jnp.float32)
     return pl.pallas_call(
-        functools.partial(resist_kernel, first, gauges, doses),
-        out_shape=jax.ShapeDtypeStruct((rows, terms), jnp.float32),
-        grid_spec=pltpu.PrefetchScalarGridSpec(
-            num_scalar_prefetch=1,
-            grid=(1,),
-            in_specs=in_specs,
-            out_specs=whole((rows, terms)),
-            scratch_shapes=[pltpu.VMEM((rows, pixels), jnp.bfloat16)],
-        ),
-        input_output_aliases={} if first else {len(operands): 0},
-        compiler_params=pltpu.CompilerParams(vmem_limit_bytes=VMEM_BYTES),
+        functools.partial(resist_kernel, first),
+        out_shape=(shape, shape),
+        in_specs=[SMEM, SMEM, VMEM, VMEM] + [ANY] * (len(pieces) + 1) + [VMEM] * (0 if first else 2),
+        out_specs=(VMEM, VMEM),
+        scratch_shapes=[
+            pltpu.VMEM((2 * rows, pixels), jnp.bfloat16),
+            pltpu.VMEM((len(pieces), pair, pixels), jnp.bfloat16),
+            pltpu.VMEM((pixels, terms), jnp.bfloat16),
+            pltpu.SemaphoreType.DMA((len(pieces) + 1,)),
+        ],
+        input_output_aliases={} if first else {len(operands): 0, len(operands) + 1: 1},
+        compiler_params=pltpu.CompilerParams(vmem_limit_bytes=RESIST_BYTES),
         cost_estimate=pl.CostEstimate(
-            flops=2 * rows * pixels * terms,
-            bytes_accessed=2 * pixels * (terms + pair * len(pieces)) + 8 * rows * terms,
-            transcendentals=rows * pixels,
+            flops=4 * rows * pixels * terms,
+            bytes_accessed=2 * pixels * (terms + pair * len(pieces)),
+            transcendentals=2 * rows * pixels,
         ),
         name="resist",
-    )(block, *operands)
-
-
-def normal_kernel(scale, table, me_ref, mine_ref, other_ref, measured_ref, params_ref, feat_ref, misfit_ref, deriv_ref, out_ref, jac_ref):
+    )(start, threshold, *operands)
+
+
+def normal_kernel(scale, table, me_ref, mine_ref, other_ref, measured_ref, params_ref, feat_ref, misfit_ref, deriv_ref, keep_ref, send_ref, jac_ref):
     gauges, doses = measured_ref.shape
     terms = mine_ref.shape[1]
     count = terms // TILE
@@ -164,19 +186,22 @@
         for c in range(b, count):
             blocks[b, c] = strip[:, (c - b) * TILE : (c - b + 1) * TILE]
     extra = [projected[:, b * TILE : (b + 1) * TILE] for b in range(count)]
+    for r, c, paired in table:
+        if paired:
+            extra.append(jnp.sum(jnp.where(row == col, blocks[c, c], 0.0), axis=0, keepdims=True))
     for p, (r, c, paired) in enumerate(table):
         where = flipped(p ^ me)
         if paired:
-            second = blocks[c, c]
-            block = jnp.where(row <= col, blocks[r, r], second)
-            extra.append(jnp.sum(jnp.where(row == col, second, 0.0), axis=0, keepdims=True))
+            block = jnp.where(row <= col, blocks[r, r], blocks[c, c])
         else:
             block = blocks[r, c]
-        out_ref[where, :TILE, :] = block
-        out_ref[where, TILE:, :] = jnp.zeros((8, TILE), jnp.float32)
-    home = flipped(me)
-    for k, line in enumerate(extra):
-        out_ref[home, TILE + k : TILE + k + 1, :] = line
+        foot = jnp.concatenate(extra + [extra[0]] * (8 - len(extra)), axis=0) if p == 0 else jnp.zeros((8, TILE), jnp.float32)
+        for ref, low in ((keep_ref, 0), (send_ref, PIECES // 2)):
+
+            @pl.when((where >= low) & (where < low + PIECES // 2))
+            def _():
+                ref[where - low, :TILE, :] = block
+                ref[where - low, TILE:, :] = foot
 
 
 def factor_tile(block):
@@ -192,8 +217,8 @@
         low = [[None] * GROUP for _ in range(GROUP)]
         root = []
         for k in range(GROUP):
-            inverse = 1.0 / a[k][k]
             root.append(lax.rsqrt(a[k][k]))
+            inverse = root[k] * root[k]
             for m in range(k + 1, GROUP):
                 for j in range(k + 1, m + 1):
                     a[m][j] = a[m][j] - (a[m][k] * a[j][k]) * inverse
@@ -322,93 +347,86 @@
     wide = gauge_bits[1:]
 
     notes = jnp.concatenate([holder[0], cache_slot[0], dose_index[0]], axis=1)
-    both = jnp.concatenate([notes, swap(notes, "gauge", 1)], axis=0)
-    relative = both[:, 0:2] ^ me
-    place = relative * cached + both[:, 2:4]
-    spots = jnp.arange(gauge_count * cached, dtype=jnp.int32)[None, :]
-    select = (
-        jnp.where(place[:, 0:1] == spots, 0.5, 0.0) + jnp.where(place[:, 1:2] == spots, 0.5, 0.0)
-    ).astype(jnp.bfloat16)
-    level = jnp.arange(dose_levels.shape[0], dtype=jnp.int32)
-    chosen = (both[:, 4:, None] == level[None, None, :]).astype(jnp.float32)
-    doses_by_gauge = STEEPNESS * jnp.sum(chosen * dose_levels[None, None, :], axis=2)
-
-    total = None
+    theirs_notes = swap(notes, "gauge", 1)
+    chunks = []
     for k in range(CHUNKS):
+        if k == 1:
+            clips, chunks[0][0] = lax.optimization_barrier((clips, chunks[0][0]))
         mine = lax.dynamic_slice(clips, (0, core * half + k * step), (cached, step))
         theirs = lax.dynamic_slice(clips, (0, (1 - core) * half + k * step), (cached, step))
-        pieces = {0: jnp.concatenate([mine, swap(theirs, "gauge", 1)], axis=0)}
+        block = jnp.concatenate([mine, swap(theirs, "gauge", 1)], axis=0)
         order = wide if k % 2 == 0 else wide[::-1]
-        have = [0]
+        if k > 1:
+            before = chunks[k - 2]
+            block, before[order[0]] = lax.optimization_barrier((block, before[order[0]]))
+        pieces, have = {0: block}, [0]
         for bit in order:
             for o in list(have):
                 pieces[o ^ bit] = swap(pieces[o], "gauge", bit)
                 have.append(o ^ bit)
-        block = (core * CHUNKS + k).astype(jnp.int32)[None]
-        total = resist_rows(
-            block,
-            STEEPNESS * threshold,
-            doses_by_gauge,
-            select,
-            [pieces[o] for o in offsets],
-            basis_terms,
-            total,
-            doses,
-        )
+        chunks.append(pieces)
+
+    def orders(own, values):
+        relative = values[:, 0:2] ^ own
+        place = relative * cached + values[:, 2:4]
+        spots = jnp.arange(gauge_count * cached, dtype=jnp.int32)[None, :]
+        select = jnp.where(place[:, 0:1] == spots, 0.5, 0.0) + jnp.where(place[:, 1:2] == spots, 0.5, 0.0)
+        level = jnp.arange(dose_levels.shape[0], dtype=jnp.int32)
+        chosen = (values[:, 4:, None] == level[None, None, :]).astype(jnp.float32)
+        return STEEPNESS * jnp.sum(chosen * dose_levels[None, None, :], axis=2), select.astype(jnp.bfloat16)
+
+    anchor = chunks[0][wide[0]]
+    notes, theirs_notes, anchor = lax.optimization_barrier((notes, theirs_notes, anchor))
+    chunks[0][wide[0]] = anchor
+    mine_orders, their_orders = orders(me, notes), orders(me, theirs_notes)
+    dose, select = [jnp.concatenate(both, axis=0) for both in zip(mine_orders, their_orders)]
+    level = STEEPNESS * threshold
+    totals = None
+    for k in range(CHUNKS):
+        start = (core * half + k * step).astype(jnp.int32)[None]
+        held = [chunks[k][o] for o in offsets]
+        totals = resist_rows(start, level, dose, select, held, basis_terms, totals)
+    mine_total, their_total = totals
     rows = gauges * doses
-    other = swap(total[rows:], "gauge", 1)
+    other = swap(their_total, "gauge", 1)
 
     count = terms // TILE
     table = piece_table(count)
     scale = float(rows * gauge_count * focus_count) ** (-0.5)
     slot = (me % PIECES).astype(jnp.int32)[None]
-    vmem = pl.BlockSpec(memory_space=pltpu.VMEM)
-    smem = pl.BlockSpec(memory_space=pltpu.SMEM)
-    feat, misfit, deriv, packed = pl.pallas_call(
+    feat, misfit, deriv, kept, sent = pl.pallas_call(
         functools.partial(normal_kernel, scale, table),
-        grid=(1,),
-        in_specs=[
-            smem,
-            pl.BlockSpec((rows, terms), lambda i: (0, 0)),
-            pl.BlockSpec((rows, terms), lambda i: (0, 0)),
-            pl.BlockSpec((gauges, doses), lambda i: (0, 0)),
-            pl.BlockSpec((1, terms), lambda i: (0, 0)),
-        ],
-        out_specs=(
-            pl.BlockSpec((rows, terms), lambda i: (0, 0)),
-            pl.BlockSpec((gauges, doses), lambda i: (0, 0)),
-            pl.BlockSpec((gauges, doses), lambda i: (0, 0)),
-            pl.BlockSpec((PIECES, PIECE_ROWS, TILE), lambda i: (0, 0, 0)),
-        ),
+        in_specs=[SMEM] + [VMEM] * 4,
+        out_specs=(VMEM,) * 5,
         out_shape=(
             jax.ShapeDtypeStruct((rows, terms), jnp.float32),
             jax.ShapeDtypeStruct((gauges, doses), jnp.float32),
             jax.ShapeDtypeStruct((gauges, doses), jnp.float32),
-            jax.ShapeDtypeStruct((PIECES, PIECE_ROWS, TILE), jnp.float32),
+            jax.ShapeDtypeStruct((PIECES // 2, PIECE_ROWS, TILE), jnp.float32),
+            jax.ShapeDtypeStruct((PIECES // 2, PIECE_ROWS, TILE), jnp.float32),
         ),
         scratch_shapes=[pltpu.VMEM((rows, terms), jnp.float32)],
         compiler_params=pltpu.CompilerParams(vmem_limit_bytes=VMEM_BYTES),
         name="normal",
-    )(slot, total, other, measured[0], parameters[None, :])
-
-    halving, others = gauge_bits[:HALVINGS], gauge_bits[HALVINGS:]
-    current = packed
-    for bit in halving:
-        keep = current.shape[0] // 2
-        current = current[:keep] + swap(current[keep:], "gauge", bit)
-    for bit in others:
-        current = current + swap(current, "gauge", bit)
-    for bit in bits_of(focus_count):
-        current = current + swap(current, "focus", bit)
-    parts = [current]
-    for bit in halving[::-1]:
-        parts = parts + [swap(part, "gauge", bit) for part in parts]
-    groups = [[flipped(k)] for k in range(PIECES)]
+    )(slot, mine_total, other, measured[0], parameters[None, :])
+
+    first, near, others = gauge_bits[0], gauge_bits[1:HALVINGS], gauge_bits[HALVINGS:]
+    ways = [sum(bit for n, bit in enumerate(near) if (p >> (len(near) - 1 - n)) & 1) for p in range(PIECES // 2)]
+    got = swap(sent, "gauge", first)
+    parts = [kept[p : p + 1] + got[p : p + 1] for p in range(PIECES // 2)]
+    terms_in = [parts[0]] + [swap(parts[p], "gauge", ways[p]) for p in range(1, PIECES // 2)]
+    current = add_pairs(terms_in)
+    current = exchange(current, "gauge", others)
+    current = exchange(current, "focus", bits_of(focus_count))
+    parts = [current] + [swap(current, "gauge", way) for way in ways[1:]]
+    parts = parts + [swap(part, "gauge", first) for part in parts]
+    order = list(range(PIECES))
+    groups = [[flipped(k)] for k in order]
 
     upper, new_params, residual = pl.pallas_call(
         functools.partial(factor_kernel, table, groups),
-        in_specs=[smem] + [vmem] * (len(parts) + 4),
-        out_specs=(vmem, vmem, vmem),
+        in_specs=[SMEM] + [VMEM] * (len(parts) + 4),
+        out_specs=(VMEM, VMEM, VMEM),
         out_shape=(
             jax.ShapeDtypeStruct((terms, terms), jnp.float32),
             jax.ShapeDtypeStruct((1, terms), jnp.float32),

time: 132 us -> 111 us (0.84)
  Pallas kernels: 52.9 us -> 40.8 us
  local copies, waits for them, and re-layouts: 10.8 us -> 5.64 us
  other arithmetic: 5 us -> 1.94 us
    pallas_call x5, Pallas kernels: 29.2 us -> 18.9 us  [the longest x4 14.8 us: resist_rows(): pl.pallas_call(functools.partial(resist_kernel, first), out_shape=(shape,...]
    unnamed x57 -> x29, local copies, waits for them, and re-layouts: 6.85 us -> 4.36 us
    slice x5 -> x2, local copies, waits for them, and re-layouts: 2.48 us -> 0.01 us  [orders(): chosen = (values[:, 4:, None] == level[None, None, :]).astype(jnp.float32)]
    pallas_call x1, Pallas kernels: 23.7 us -> 21.9 us  [local(): pl.pallas_call(functools.partial(factor_kernel, table, groups), in_specs=...]
    add x6 -> x4, other arithmetic: 1.88 us -> 0.08 us  [the longest x2 0.04 us: add_pairs(): sum(values[i + 1:i + 2], values[i])]
    ppermute x30 -> x32, waiting for transfers between devices: 33.6 us -> 32.4 us  [swap(): return lax.ppermute(value, axis, [(i, i ^ bit) for i in range(size)])]
    ppermute x30 -> x32, starting transfers between devices: 27.8 us -> 28.1 us  [swap(): return lax.ppermute(value, axis, [(i, i ^ bit) for i in range(size)])]
  transfers between devices with their start and end apart: 30 -> 32, of which waited for: 14 -> 18; matrix products, arithmetic and copies ran while one was open for 4% -> 2% of each run, Pallas kernels for 13% -> 10%
where the time goes in v2:
time: 111 us; the launch traced here: 110 us
  Pallas kernels  40.8 us (37%)
  waiting for transfers between devices  32.4 us (29%)
  starting transfers between devices  28.1 us (25%)
  local copies, waits for them, and re-layouts  5.64 us (5%)
  other arithmetic  1.94 us (2%)
  between operations  1.57 us (1%)
    ppermute x32, waiting for transfers between devices, swap(): return lax.ppermute(value, axis, [(i, i ^ bit) for i in range(size)])  32.4 us
    ppermute x32, starting transfers between devices, swap(): return lax.ppermute(value, axis, [(i, i ^ bit) for i in range(size)])  28.1 us
    pallas_call x1, Pallas kernels, local(): pl.pallas_call(functools.partial(factor_kernel, table, groups), in_specs=...  21.9 us
    pallas_call x4, Pallas kernels, resist_rows(): pl.pallas_call(functools.partial(resist_kernel, first), out_shape=(shape,...  14.8 us
    unnamed x29, local copies, waits for them, and re-layouts  4.36 us
    pallas_call x1, Pallas kernels, local(): pl.pallas_call(functools.partial(normal_kernel, scale, table), in_specs=[...  4.14 us
  transfers between devices with their start and end apart: 32, of which 18 were waited for; matrix products, arithmetic and copies ran while one was open for 2% of the time, Pallas kernels for 10%

profile of v2, /device:TPU:0, one launch (start us, length us, event | category | flops | bytes accessed | tf_op | source)
XLA Modules:
  0.0 110.4 jit_solution(1597193323858370200)
XLA Ops:
  0.7 1.1 dynamic-slice_bitcast_fusion.1
  5.1 2.7 %collective-permute-start.3 = (bf16[128,1024]{1,0:T(8,128)(2,1)S(1)}, bf16[128,1024]{1,0:T(8,128)(2,1)S(1)}, u32[]{:S(2)}, u32[]{:S(2)}) collective-permute-start(bf16[128,1024]{1,0:T(8,128)(2,1)S(1)} %pad_maximum_fusion.refs_0_), channel_id=1, source_target_pairs={{0,8},{4,12},{8,0},{12,4},{16,24},{20,28},{24,16},{28,20},{1,9},{5... | collective-permute-start | bytes 786440 | tf_op jit(solution)/shard_map/ppermute | solution.py:36
  7.8 1.5 %collective-permute-start.15 = (bf16[128,1024]{1,0:T(8,128)(2,1)S(1)}, bf16[128,1024]{1,0:T(8,128)(2,1)S(1)}, u32[]{:S(2)}, u32[]{:S(2)}) collective-permute-start(bf16[128,1024]{1,0:T(8,128)(2,1)S(1)} %pad_maximum_fusion.refs_0_), channel_id=1, source_target_pairs={{0,16},{4,20},{8,24},{12,28},{16,0},{20,4},{24,8},{28,12},{1,17},{... | collective-permute-start | bytes 786440 | tf_op jit(solution)/shard_map/ppermute | solution.py:36
  11.4 3.4 %collective-permute-done.3.refs_1_ = bf16[128,1024]{1,0:T(8,128)(2,1)S(1)} collective-permute-done((bf16[128,1024]{1,0:T(8,128)(2,1)S(1)}, bf16[128,1024]{1,0:T(8,128)(2,1)S(1)}, u32[]{:S(2)}, u32[]{:S(2)}) %collective-permute-start.3) | collective-permute-done | bytes 262176 | tf_op jit(solution)/shard_map/ppermute | solution.py:36
  14.9 2.1 %collective-permute-start.10 = (bf16[128,1024]{1,0:T(8,128)(2,1)}, bf16[128,1024]{1,0:T(8,128)(2,1)}, u32[]{:S(2)}, u32[]{:S(2)}) collective-permute-start(bf16[128,1024]{1,0:T(8,128)(2,1)} %pad_maximum_fusion.1.refs_0_), channel_id=1, source_target_pairs={{0,8},{4,12},{8,0},{12,4},{16,24},{20,28},{24,16},{28,20},{1,9},{5... | collective-permute-start | bytes 786440 | tf_op jit(solution)/shard_map/ppermute | solution.py:36
  17.4 1.6 %collective-permute-start.16 = (bf16[128,1024]{1,0:T(8,128)(2,1)S(1)}, bf16[128,1024]{1,0:T(8,128)(2,1)S(1)}, u32[]{:S(2)}, u32[]{:S(2)}) collective-permute-start(bf16[128,1024]{1,0:T(8,128)(2,1)S(1)} %collective-permute-done.3.refs_1_), channel_id=1, source_target_pairs={{0,16},{4,20},{8,24},{12,28},{16,0},{20,4},{24,8},{28,12},{1,17},{... | collective-permute-start | bytes 786440 | tf_op jit(solution)/shard_map/ppermute | solution.py:36
  18.9 3.7 %collective-permute-done.6.refs_2_ = bf16[128,1024]{1,0:T(8,128)(2,1)} collective-permute-done((bf16[128,1024]{1,0:T(8,128)(2,1)}, bf16[128,1024]{1,0:T(8,128)(2,1)}, u32[]{:S(2)}, u32[]{:S(2)}) %collective-permute-start.6) | collective-permute-done | bytes 262176 | tf_op jit(solution)/shard_map/ppermute | solution.py:36
  22.7 1.5 %collective-permute-start.8 = (bf16[128,1024]{1,0:T(8,128)(2,1)S(1)}, bf16[128,1024]{1,0:T(8,128)(2,1)}, u32[]{:S(2)}, u32[]{:S(2)}) collective-permute-start(bf16[128,1024]{1,0:T(8,128)(2,1)S(1)} %pad_maximum_fusion.2.refs_0_), channel_id=1, source_target_pairs={{0,16},{4,20},{8,24},{12,28},{16,0},{20,4},{24,8},{28,12},{1,17},{... | collective-permute-start | bytes 786440 | tf_op jit(solution)/shard_map/ppermute | solution.py:36
  24.9 3.2 %collective-permute-done.16.refs_3_ = bf16[128,1024]{1,0:T(8,128)(2,1)S(1)} collective-permute-done((bf16[128,1024]{1,0:T(8,128)(2,1)S(1)}, bf16[128,1024]{1,0:T(8,128)(2,1)S(1)}, u32[]{:S(2)}, u32[]{:S(2)}) %collective-permute-start.16) | collective-permute-done | bytes 262176 | tf_op jit(solution)/shard_map/ppermute | solution.py:36
  28.9 1.5 %collective-permute-start.11 = (bf16[128,1024]{1,0:T(8,128)(2,1)}, bf16[128,1024]{1,0:T(8,128)(2,1)S(1)}, u32[]{:S(2)}, u32[]{:S(2)}) collective-permute-start(bf16[128,1024]{1,0:T(8,128)(2,1)} %pad_maximum_fusion.1.refs_0_), channel_id=1, source_target_pairs={{0,16},{4,20},{8,24},{12,28},{16,0},{20,4},{24,8},{28,12},{1,17},{... | collective-permute-start | bytes 786440 | tf_op jit(solution)/shard_map/ppermute | solution.py:36
  33.8 3.0 %resist.4 = (f32[704,512]{1,0:T(8,128)S(1)}, f32[704,512]{1,0:T(8,128)S(1)}) custom-call(s32[1]{0:T(128)} %bitcast.13.start_ref, f32[1]{0:T(128)S(6)} %mul.21.threshold_ref, f32[128,11]{1,0:T(8,128)S(1)} %copy.33.dose_ref, bf16[128,512]{1,0:T(8,128)(2,1)S(1)} %pad_maximum_fusion.4.select_ref, bf16[128,1024]{1,0:T(8,128)(2,1)S(1)} %pad_maximum_fusion.refs_0_, ...), custom_call_target="tpu_custom_call" | custom-call | flops 1476395008 | bytes 2097152 | tf_op jit(solution)/shard_map/resist/pallas_call | solution.py:134
  36.9 2.0 %collective-permute-start.9 = (bf16[128,1024]{1,0:T(8,128)(2,1)}, bf16[128,1024]{1,0:T(8,128)(2,1)S(1)}, u32[]{:S(2)}, u32[]{:S(2)}) collective-permute-start(bf16[128,1024]{1,0:T(8,128)(2,1)} %collective-permute-done.8.refs_2_), channel_id=1, source_target_pairs={{0,8},{4,12},{8,0},{12,4},{16,24},{20,28},{24,16},{28,20},{1,9},{5... | collective-permute-start | bytes 786440 | tf_op jit(solution)/shard_map/ppermute | solution.py:36
  38.9 4.0 %resist.5 = (f32[704,512]{1,0:T(8,128)S(1)}, f32[704,512]{1,0:T(8,128)S(1)}) custom-call(s32[1]{0:T(128)} %bitcast.12.start_ref, f32[1]{0:T(128)S(6)} %mul.21.threshold_ref, f32[128,11]{1,0:T(8,128)S(1)} %copy.33.dose_ref, bf16[128,512]{1,0:T(8,128)(2,1)S(1)} %pad_maximum_fusion.4.select_ref, ...), custom_call_target="tpu_custom_call", output_to_operand_aliasing={{0}: (9, {}), {1}: (10, {})} | custom-call | flops 1476395008 | bytes 2097152 | tf_op jit(solution)/shard_map/resist/pallas_call | solution.py:134
  42.9 1.2 %collective-permute-done.12.refs_3_ = bf16[128,1024]{1,0:T(8,128)(2,1)S(1)} collective-permute-done((bf16[128,1024]{1,0:T(8,128)(2,1)}, bf16[128,1024]{1,0:T(8,128)(2,1)S(1)}, u32[]{:S(2)}, u32[]{:S(2)}) %collective-permute-start.12) | collective-permute-done | bytes 262176 | tf_op jit(solution)/shard_map/ppermute | solution.py:36
  44.1 4.0 %resist.6 = (f32[704,512]{1,0:T(8,128)S(1)}, f32[704,512]{1,0:T(8,128)S(1)}) custom-call(s32[1]{0:T(128)} %bitcast.11.start_ref, f32[1]{0:T(128)S(6)} %mul.21.threshold_ref, f32[128,11]{1,0:T(8,128)S(1)} %copy.33.dose_ref, bf16[128,512]{1,0:T(8,128)(2,1)S(1)} %pad_maximum_fusion.4.select_ref, ...), custom_call_target="tpu_custom_call", output_to_operand_aliasing={{0}: (9, {}), {1}: (10, {})} | custom-call | flops 1476395008 | bytes 2097152 | tf_op jit(solution)/shard_map/resist/pallas_call | solution.py:134
  48.5 3.8 %resist.7 = (f32[704,512]{1,0:T(8,128)S(1)}, f32[704,512]{1,0:T(8,128)S(1)}) custom-call(s32[1]{0:T(128)} %bitcast.1.start_ref, f32[1]{0:T(128)S(6)} %mul.21.threshold_ref, f32[128,11]{1,0:T(8,128)S(1)} %copy.33.dose_ref, bf16[128,512]{1,0:T(8,128)(2,1)S(1)} %pad_maximum_fusion.4.select_ref, ...), custom_call_target="tpu_custom_call", output_to_operand_aliasing={{0}: (9, {}), {1}: (10, {})} | custom-call | flops 1476395008 | bytes 2097152 | tf_op jit(solution)/shard_map/resist/pallas_call | solution.py:134
  52.5 3.2 %collective-permute-done.17.other_ref = f32[704,512]{1,0:T(8,128)} collective-permute-done((f32[704,512]{1,0:T(8,128)S(1)}, f32[704,512]{1,0:T(8,128)}, u32[]{:S(2)}, u32[]{:S(2)}) %collective-permute-start.17) | collective-permute-done | bytes 1441824 | tf_op jit(solution)/shard_map/ppermute | solution.py:36
  55.7 4.1 %normal.1 = (f32[704,512]{1,0:T(8,128)S(1)}, f32[64,11]{1,0:T(8,128)S(1)}, f32[64,11]{1,0:T(8,128)S(1)}, f32[4,136,128]{2,1,0:T(8,128)S(1)}, f32[4,136,128]{2,1,0:T(8,128)S(1)}) custom-call(s32[1]{0:T(128)} %bitcast.me_ref, f32[704,512]{1,0:T(8,128)S(1)} %get-tuple-element.43.mine_ref, f32[704,512]{1,0:T(8,128)} %collective-permute-done.17.other_ref, ...), custom_call_target="tpu_custom_call" | custom-call | tf_op jit(solution)/shard_map/normal/pallas_call | solution.py:397
  60.0 1.4 %collective-permute-done.18 = f32[4,136,128]{2,1,0:T(8,128)S(1)} collective-permute-done((f32[4,136,128]{2,1,0:T(8,128)S(1)}, f32[4,136,128]{2,1,0:T(8,128)S(1)}, u32[]{:S(2)}, u32[]{:S(2)}) %collective-permute-start.18) | collective-permute-done | bytes 278560 | tf_op jit(solution)/shard_map/ppermute | solution.py:36
  61.5 1.7 %collective-permute-start.19 = (f32[1,136,128]{2,1,0:T(8,128)S(1)}, f32[1,136,128]{2,1,0:T(8,128)S(1)}, u32[]{:S(2)}, u32[]{:S(2)}) collective-permute-start(f32[1,136,128]{2,1,0:T(8,128)S(1)} %get-tuple-element.74), channel_id=1, source_target_pairs={{0,16},{4,20},{8,24},{12,28},{16,0},{20,4},{24,8},{28,12},{1,17},{... | collective-permute-start | bytes 208904 | tf_op jit(solution)/shard_map/ppermute | solution.py:36
  63.7 1.3 %collective-permute-start.21 = (f32[1,136,128]{2,1,0:T(8,128)S(1)}, f32[1,136,128]{2,1,0:T(8,128)S(1)}, u32[]{:S(2)}, u32[]{:S(2)}) collective-permute-start(f32[1,136,128]{2,1,0:T(8,128)S(1)} %get-tuple-element.72), channel_id=1, source_target_pairs={{0,24},{4,28},{8,16},{12,20},{16,8},{20,12},{24,0},{28,4},{1,25},{... | collective-permute-start | bytes 208904 | tf_op jit(solution)/shard_map/ppermute | solution.py:36
  65.9 2.0 %collective-permute-done.20 = f32[1,136,128]{2,1,0:T(8,128)S(1)} collective-permute-done((f32[1,136,128]{2,1,0:T(8,128)S(1)}, f32[1,136,128]{2,1,0:T(8,128)S(1)}, u32[]{:S(2)}, u32[]{:S(2)}) %collective-permute-start.20) | collective-permute-done | bytes 69664 | tf_op jit(solution)/shard_map/ppermute | solution.py:36
  69.0 1.6 %collective-permute-start.22 = (f32[1,136,128]{2,1,0:T(8,128)S(1)}, f32[1,136,128]{2,1,0:T(8,128)S(1)}, u32[]{:S(2)}, u32[]{:S(2)}) collective-permute-start(f32[1,136,128]{2,1,0:T(8,128)S(1)} %fusion.1), channel_id=1, source_target_pairs={{0,1},{1,0},{2,3},{3,2},{4,5},{5,4},{6,7},{7,6},{8,9},{9,8},{10,11... | collective-permute-start | bytes 208904 | tf_op jit(solution)/shard_map/ppermute | solution.py:36
  70.6 2.6 %collective-permute-start.23 = (f32[1,136,128]{2,1,0:T(8,128)S(1)}, f32[1,136,128]{2,1,0:T(8,128)S(1)}, u32[]{:S(2)}, u32[]{:S(2)}) collective-permute-start(f32[1,136,128]{2,1,0:T(8,128)S(1)} %fusion.1), channel_id=1, source_target_pairs={{0,2},{1,3},{2,0},{3,1},{4,6},{5,7},{6,4},{7,5},{8,10},{9,11},{10,... | collective-permute-start | bytes 208904 | tf_op jit(solution)/shard_map/ppermute | solution.py:36
  74.0 3.4 %collective-permute-done.23 = f32[1,136,128]{2,1,0:T(8,128)S(1)} collective-permute-done((f32[1,136,128]{2,1,0:T(8,128)S(1)}, f32[1,136,128]{2,1,0:T(8,128)S(1)}, u32[]{:S(2)}, u32[]{:S(2)}) %collective-permute-start.23) | collective-permute-done | bytes 69664 | tf_op jit(solution)/shard_map/ppermute | solution.py:36
  77.4 1.9 %collective-permute-done.24 = f32[1,136,128]{2,1,0:T(8,128)S(1)} collective-permute-done((f32[1,136,128]{2,1,0:T(8,128)S(1)}, f32[1,136,128]{2,1,0:T(8,128)S(1)}, u32[]{:S(2)}, u32[]{:S(2)}) %collective-permute-start.24) | collective-permute-done | bytes 69664 | tf_op jit(solution)/shard_map/ppermute | solution.py:36
  79.3 1.2 %collective-permute-start.25 = (f32[1,136,128]{2,1,0:T(8,128)S(1)}, f32[1,136,128]{2,1,0:T(8,128)S(1)}, u32[]{:S(2)}, u32[]{:S(2)}) collective-permute-start(f32[1,136,128]{2,1,0:T(8,128)S(1)} %add_add_fusion.refs_0_), channel_id=1, source_target_pairs={{0,16},{4,20},{8,24},{12,28},{16,0},{20,4},{24,8},{28,12},{1,17},{... | collective-permute-start | bytes 208904 | tf_op jit(solution)/shard_map/ppermute | solution.py:36
  81.4 1.4 %collective-permute-start.27 = (f32[1,136,128]{2,1,0:T(8,128)S(1)}, f32[1,136,128]{2,1,0:T(8,128)S(1)}, u32[]{:S(2)}, u32[]{:S(2)}) collective-permute-start(f32[1,136,128]{2,1,0:T(8,128)S(1)} %add_add_fusion.refs_0_), channel_id=1, source_target_pairs={{0,24},{4,28},{8,16},{12,20},{16,8},{20,12},{24,0},{28,4},{1,25},{... | collective-permute-start | bytes 208904 | tf_op jit(solution)/shard_map/ppermute | solution.py:36
  83.7 1.1 %collective-permute-done.26.refs_2_ = f32[1,136,128]{2,1,0:T(8,128)S(1)} collective-permute-done((f32[1,136,128]{2,1,0:T(8,128)S(1)}, f32[1,136,128]{2,1,0:T(8,128)S(1)}, u32[]{:S(2)}, u32[]{:S(2)}) %collective-permute-start.26) | collective-permute-done | bytes 69664 | tf_op jit(solution)/shard_map/ppermute | solution.py:36
  84.9 1.8 %collective-permute-done.27.refs_3_ = f32[1,136,128]{2,1,0:T(8,128)S(1)} collective-permute-done((f32[1,136,128]{2,1,0:T(8,128)S(1)}, f32[1,136,128]{2,1,0:T(8,128)S(1)}, u32[]{:S(2)}, u32[]{:S(2)}) %collective-permute-start.27) | collective-permute-done | bytes 69664 | tf_op jit(solution)/shard_map/ppermute | solution.py:36
  86.7 1.2 %collective-permute-done.31.refs_7_ = f32[1,136,128]{2,1,0:T(8,128)S(1)} collective-permute-done((f32[1,136,128]{2,1,0:T(8,128)S(1)}, f32[1,136,128]{2,1,0:T(8,128)S(1)}, u32[]{:S(2)}, u32[]{:S(2)}) %collective-permute-start.31) | collective-permute-done | bytes 69664 | tf_op jit(solution)/shard_map/ppermute | solution.py:36
  87.9 21.9 %factor.1 = (f32[512,512]{1,0:T(8,128)}, f32[1,512]{1,0:T(1,128)}, f32[64,11]{1,0:T(8,128)S(1)}) custom-call(s32[1]{0:T(128)} %bitcast.me_ref, f32[1,136,128]{2,1,0:T(8,128)S(1)} %add_add_fusion.refs_0_, f32[1,136,128]{2,1,0:T(8,128)S(1)} %collective-permute-done.25.refs_1_, f32[1,136,128]{2,1,0:T(8,128)S(1)} %collective-permute-done.26.refs_2_, ...), custom_call_target="tpu_custom_call" | custom-call | tf_op jit(solution)/shard_map/factor/pallas_call | solution.py:426
  (89 shorter events, 16.4 us)
Async XLA Ops:
  1.8 1.5 %collective-permute-start.1 = (bf16[64,1024]{1,0:T(8,128)(2,1)S(1)}, bf16[64,1024]{1,0:T(8,128)(2,1)S(1)}, u32[]{:S(2)}, u32[]{:S(2)}) collective-permute-start(bf16[64,1024]{1,0:T(8,128)(2,1)S(1)} %get-tuple-element.71), channel_id=1, source_target_pairs={{0,4},{4,0},{8,12},{12,8},{16,20},{20,16},{24,28},{28,24},{1,5},{5... | collective-permute-start | bytes 393224 | tf_op jit(solution)/shard_map/ppermute | solution.py:36
  3.4 5.9 %collective-permute-start.5 = (bf16[64,1024]{1,0:T(8,128)(2,1)S(1)}, bf16[64,1024]{1,0:T(8,128)(2,1)S(1)}, u32[]{:S(2)}, u32[]{:S(2)}) collective-permute-start(bf16[64,1024]{1,0:T(8,128)(2,1)S(1)} %get-tuple-element.65), channel_id=1, source_target_pairs={{0,4},{4,0},{8,12},{12,8},{16,20},{20,16},{24,28},{28,24},{1,5},{5... | collective-permute-start | bytes 393224 | tf_op jit(solution)/shard_map/ppermute | solution.py:36
  3.8 6.2 %collective-permute-start.2 = (bf16[64,1024]{1,0:T(8,128)(2,1)S(1)}, bf16[64,1024]{1,0:T(8,128)(2,1)S(1)}, u32[]{:S(2)}, u32[]{:S(2)}) collective-permute-start(bf16[64,1024]{1,0:T(8,128)(2,1)S(1)} %get-tuple-element.68), channel_id=1, source_target_pairs={{0,4},{4,0},{8,12},{12,8},{16,20},{20,16},{24,28},{28,24},{1,5},{5... | collective-permute-start | bytes 393224 | tf_op jit(solution)/shard_map/ppermute | solution.py:36
  4.0 10.9 %collective-permute-start = (s32[64,15]{0,1:T(8,128)S(1)}, s32[64,15]{0,1:T(8,128)S(1)}, u32[]{:S(2)}, u32[]{:S(2)}) collective-permute-start(s32[64,15]{0,1:T(8,128)S(1)} %pad_add_fusion), channel_id=1, source_target_pairs={{0,4},{4,0},{8,12},{12,8},{16,20},{20,16},{24,28},{28,24},{1,5},{5... | collective-permute-start | bytes 11528 | tf_op jit(solution)/shard_map/ppermute | solution.py:36
  5.1 9.8 %collective-permute-start.3 = (bf16[128,1024]{1,0:T(8,128)(2,1)S(1)}, bf16[128,1024]{1,0:T(8,128)(2,1)S(1)}, u32[]{:S(2)}, u32[]{:S(2)}) collective-permute-start(bf16[128,1024]{1,0:T(8,128)(2,1)S(1)} %pad_maximum_fusion.refs_0_), channel_id=1, source_target_pairs={{0,8},{4,12},{8,0},{12,4},{16,24},{20,28},{24,16},{28,20},{1,9},{5... | collective-permute-start | bytes 786440 | tf_op jit(solution)/shard_map/ppermute | solution.py:36
  7.8 16.4 %collective-permute-start.15 = (bf16[128,1024]{1,0:T(8,128)(2,1)S(1)}, bf16[128,1024]{1,0:T(8,128)(2,1)S(1)}, u32[]{:S(2)}, u32[]{:S(2)}) collective-permute-start(bf16[128,1024]{1,0:T(8,128)(2,1)S(1)} %pad_maximum_fusion.refs_0_), channel_id=1, source_target_pairs={{0,16},{4,20},{8,24},{12,28},{16,0},{20,4},{24,8},{28,12},{1,17},{... | collective-permute-start | bytes 786440 | tf_op jit(solution)/shard_map/ppermute | solution.py:36
  9.3 2.0 %collective-permute-start.4 = (bf16[64,1024]{1,0:T(8,128)(2,1)S(1)}, bf16[64,1024]{1,0:T(8,128)(2,1)S(1)}, u32[]{:S(2)}, u32[]{:S(2)}) collective-permute-start(bf16[64,1024]{1,0:T(8,128)(2,1)S(1)} %get-tuple-element.66), channel_id=1, source_target_pairs={{0,4},{4,0},{8,12},{12,8},{16,20},{20,16},{24,28},{28,24},{1,5},{5... | collective-permute-start | bytes 393224 | tf_op jit(solution)/shard_map/ppermute | solution.py:36
  10.0 12.6 %collective-permute-start.6 = (bf16[128,1024]{1,0:T(8,128)(2,1)}, bf16[128,1024]{1,0:T(8,128)(2,1)}, u32[]{:S(2)}, u32[]{:S(2)}) collective-permute-start(bf16[128,1024]{1,0:T(8,128)(2,1)} %pad_maximum_fusion.3.refs_0_), channel_id=1, source_target_pairs={{0,16},{4,20},{8,24},{12,28},{16,0},{20,4},{24,8},{28,12},{1,17},{... | collective-permute-start | bytes 786440 | tf_op jit(solution)/shard_map/ppermute | solution.py:36
  11.3 25.5 %collective-permute-start.13 = (bf16[128,1024]{1,0:T(8,128)(2,1)}, bf16[128,1024]{1,0:T(8,128)(2,1)}, u32[]{:S(2)}, u32[]{:S(2)}) collective-permute-start(bf16[128,1024]{1,0:T(8,128)(2,1)} %pad_maximum_fusion.3.refs_0_), channel_id=1, source_target_pairs={{0,8},{4,12},{8,0},{12,4},{16,24},{20,28},{24,16},{28,20},{1,9},{5... | collective-permute-start | bytes 786440 | tf_op jit(solution)/shard_map/ppermute | solution.py:36
  14.9 15.5 %collective-permute-start.10 = (bf16[128,1024]{1,0:T(8,128)(2,1)}, bf16[128,1024]{1,0:T(8,128)(2,1)}, u32[]{:S(2)}, u32[]{:S(2)}) collective-permute-start(bf16[128,1024]{1,0:T(8,128)(2,1)} %pad_maximum_fusion.1.refs_0_), channel_id=1, source_target_pairs={{0,8},{4,12},{8,0},{12,4},{16,24},{20,28},{24,16},{28,20},{1,9},{5... | collective-permute-start | bytes 786440 | tf_op jit(solution)/shard_map/ppermute | solution.py:36
  17.4 10.8 %collective-permute-start.16 = (bf16[128,1024]{1,0:T(8,128)(2,1)S(1)}, bf16[128,1024]{1,0:T(8,128)(2,1)S(1)}, u32[]{:S(2)}, u32[]{:S(2)}) collective-permute-start(bf16[128,1024]{1,0:T(8,128)(2,1)S(1)} %collective-permute-done.3.refs_1_), channel_id=1, source_target_pairs={{0,16},{4,20},{8,24},{12,28},{16,0},{20,4},{24,8},{28,12},{1,17},{... | collective-permute-start | bytes 786440 | tf_op jit(solution)/shard_map/ppermute | solution.py:36
  22.7 14.3 %collective-permute-start.8 = (bf16[128,1024]{1,0:T(8,128)(2,1)S(1)}, bf16[128,1024]{1,0:T(8,128)(2,1)}, u32[]{:S(2)}, u32[]{:S(2)}) collective-permute-start(bf16[128,1024]{1,0:T(8,128)(2,1)S(1)} %pad_maximum_fusion.2.refs_0_), channel_id=1, source_target_pairs={{0,16},{4,20},{8,24},{12,28},{16,0},{20,4},{24,8},{28,12},{1,17},{... | collective-permute-start | bytes 786440 | tf_op jit(solution)/shard_map/ppermute | solution.py:36
  24.2 14.7 %collective-permute-start.14 = (bf16[128,1024]{1,0:T(8,128)(2,1)}, bf16[128,1024]{1,0:T(8,128)(2,1)}, u32[]{:S(2)}, u32[]{:S(2)}) collective-permute-start(bf16[128,1024]{1,0:T(8,128)(2,1)} %collective-permute-done.6.refs_2_), channel_id=1, source_target_pairs={{0,8},{4,12},{8,0},{12,4},{16,24},{20,28},{24,16},{28,20},{1,9},{5... | collective-permute-start | bytes 786440 | tf_op jit(solution)/shard_map/ppermute | solution.py:36
  28.9 14.0 %collective-permute-start.11 = (bf16[128,1024]{1,0:T(8,128)(2,1)}, bf16[128,1024]{1,0:T(8,128)(2,1)S(1)}, u32[]{:S(2)}, u32[]{:S(2)}) collective-permute-start(bf16[128,1024]{1,0:T(8,128)(2,1)} %pad_maximum_fusion.1.refs_0_), channel_id=1, source_target_pairs={{0,16},{4,20},{8,24},{12,28},{16,0},{20,4},{24,8},{28,12},{1,17},{... | collective-permute-start | bytes 786440 | tf_op jit(solution)/shard_map/ppermute | solution.py:36
  30.4 13.7 %collective-permute-start.12 = (bf16[128,1024]{1,0:T(8,128)(2,1)}, bf16[128,1024]{1,0:T(8,128)(2,1)S(1)}, u32[]{:S(2)}, u32[]{:S(2)}) collective-permute-start(bf16[128,1024]{1,0:T(8,128)(2,1)} %collective-permute-done.10.refs_1_), channel_id=1, source_target_pairs={{0,16},{4,20},{8,24},{12,28},{16,0},{20,4},{24,8},{28,12},{1,17},{... | collective-permute-start | bytes 786440 | tf_op jit(solution)/shard_map/ppermute | solution.py:36
  36.8 11.4 %collective-permute-start.7 = (bf16[128,1024]{1,0:T(8,128)(2,1)S(1)}, bf16[128,1024]{1,0:T(8,128)(2,1)S(1)}, u32[]{:S(2)}, u32[]{:S(2)}) collective-permute-start(bf16[128,1024]{1,0:T(8,128)(2,1)S(1)} %pad_maximum_fusion.2.refs_0_), channel_id=1, source_target_pairs={{0,8},{4,12},{8,0},{12,4},{16,24},{20,28},{24,16},{28,20},{1,9},{5... | collective-permute-start | bytes 786440 | tf_op jit(solution)/shard_map/ppermute | solution.py:36
  36.9 11.5 %collective-permute-start.9 = (bf16[128,1024]{1,0:T(8,128)(2,1)}, bf16[128,1024]{1,0:T(8,128)(2,1)S(1)}, u32[]{:S(2)}, u32[]{:S(2)}) collective-permute-start(bf16[128,1024]{1,0:T(8,128)(2,1)} %collective-permute-done.8.refs_2_), channel_id=1, source_target_pairs={{0,8},{4,12},{8,0},{12,4},{16,24},{20,28},{24,16},{28,20},{1,9},{5... | collective-permute-start | bytes 786440 | tf_op jit(solution)/shard_map/ppermute | solution.py:36
  52.3 3.4 %collective-permute-start.17 = (f32[704,512]{1,0:T(8,128)S(1)}, f32[704,512]{1,0:T(8,128)}, u32[]{:S(2)}, u32[]{:S(2)}) collective-permute-start(f32[704,512]{1,0:T(8,128)S(1)} %get-tuple-element.44), channel_id=1, source_target_pairs={{0,4},{4,0},{8,12},{12,8},{16,20},{20,16},{24,28},{28,24},{1,5},{5... | collective-permute-start | bytes 4325384 | tf_op jit(solution)/shard_map/ppermute | solution.py:36
  59.8 1.6 %collective-permute-start.18 = (f32[4,136,128]{2,1,0:T(8,128)S(1)}, f32[4,136,128]{2,1,0:T(8,128)S(1)}, u32[]{:S(2)}, u32[]{:S(2)}) collective-permute-start(f32[4,136,128]{2,1,0:T(8,128)S(1)} %get-tuple-element.46), channel_id=1, source_target_pairs={{0,4},{4,0},{8,12},{12,8},{16,20},{20,16},{24,28},{28,24},{1,5},{5... | collective-permute-start | bytes 835592 | tf_op jit(solution)/shard_map/ppermute | solution.py:36
  61.5 4.4 %collective-permute-start.19 = (f32[1,136,128]{2,1,0:T(8,128)S(1)}, f32[1,136,128]{2,1,0:T(8,128)S(1)}, u32[]{:S(2)}, u32[]{:S(2)}) collective-permute-start(f32[1,136,128]{2,1,0:T(8,128)S(1)} %get-tuple-element.74), channel_id=1, source_target_pairs={{0,16},{4,20},{8,24},{12,28},{16,0},{20,4},{24,8},{28,12},{1,17},{... | collective-permute-start | bytes 208904 | tf_op jit(solution)/shard_map/ppermute | solution.py:36
  63.2 4.7 %collective-permute-start.20 = (f32[1,136,128]{2,1,0:T(8,128)S(1)}, f32[1,136,128]{2,1,0:T(8,128)S(1)}, u32[]{:S(2)}, u32[]{:S(2)}) collective-permute-start(f32[1,136,128]{2,1,0:T(8,128)S(1)} %get-tuple-element.73), channel_id=1, source_target_pairs={{0,8},{4,12},{8,0},{12,4},{16,24},{20,28},{24,16},{28,20},{1,9},{5... | collective-permute-start | bytes 208904 | tf_op jit(solution)/shard_map/ppermute | solution.py:36
  63.7 5.2 %collective-permute-start.21 = (f32[1,136,128]{2,1,0:T(8,128)S(1)}, f32[1,136,128]{2,1,0:T(8,128)S(1)}, u32[]{:S(2)}, u32[]{:S(2)}) collective-permute-start(f32[1,136,128]{2,1,0:T(8,128)S(1)} %get-tuple-element.72), channel_id=1, source_target_pairs={{0,24},{4,28},{8,16},{12,20},{16,8},{20,12},{24,0},{28,4},{1,25},{... | collective-permute-start | bytes 208904 | tf_op jit(solution)/shard_map/ppermute | solution.py:36
  69.0 5.1 %collective-permute-start.22 = (f32[1,136,128]{2,1,0:T(8,128)S(1)}, f32[1,136,128]{2,1,0:T(8,128)S(1)}, u32[]{:S(2)}, u32[]{:S(2)}) collective-permute-start(f32[1,136,128]{2,1,0:T(8,128)S(1)} %fusion.1), channel_id=1, source_target_pairs={{0,1},{1,0},{2,3},{3,2},{4,5},{5,4},{6,7},{7,6},{8,9},{9,8},{10,11... | collective-permute-start | bytes 208904 | tf_op jit(solution)/shard_map/ppermute | solution.py:36
  70.6 6.8 %collective-permute-start.23 = (f32[1,136,128]{2,1,0:T(8,128)S(1)}, f32[1,136,128]{2,1,0:T(8,128)S(1)}, u32[]{:S(2)}, u32[]{:S(2)}) collective-permute-start(f32[1,136,128]{2,1,0:T(8,128)S(1)} %fusion.1), channel_id=1, source_target_pairs={{0,2},{1,3},{2,0},{3,1},{4,6},{5,7},{6,4},{7,5},{8,10},{9,11},{10,... | collective-permute-start | bytes 208904 | tf_op jit(solution)/shard_map/ppermute | solution.py:36
  73.2 6.1 %collective-permute-start.24 = (f32[1,136,128]{2,1,0:T(8,128)S(1)}, f32[1,136,128]{2,1,0:T(8,128)S(1)}, u32[]{:S(2)}, u32[]{:S(2)}) collective-permute-start(f32[1,136,128]{2,1,0:T(8,128)S(1)} %fusion.1), channel_id=1, source_target_pairs={{0,3},{1,2},{2,1},{3,0},{4,7},{5,6},{6,5},{7,4},{8,11},{9,10},{10,... | collective-permute-start | bytes 208904 | tf_op jit(solution)/shard_map/ppermute | solution.py:36
  79.3 4.4 %collective-permute-start.25 = (f32[1,136,128]{2,1,0:T(8,128)S(1)}, f32[1,136,128]{2,1,0:T(8,128)S(1)}, u32[]{:S(2)}, u32[]{:S(2)}) collective-permute-start(f32[1,136,128]{2,1,0:T(8,128)S(1)} %add_add_fusion.refs_0_), channel_id=1, source_target_pairs={{0,16},{4,20},{8,24},{12,28},{16,0},{20,4},{24,8},{28,12},{1,17},{... | collective-permute-start | bytes 208904 | tf_op jit(solution)/shard_map/ppermute | solution.py:36
  80.5 4.3 %collective-permute-start.26 = (f32[1,136,128]{2,1,0:T(8,128)S(1)}, f32[1,136,128]{2,1,0:T(8,128)S(1)}, u32[]{:S(2)}, u32[]{:S(2)}) collective-permute-start(f32[1,136,128]{2,1,0:T(8,128)S(1)} %add_add_fusion.refs_0_), channel_id=1, source_target_pairs={{0,8},{4,12},{8,0},{12,4},{16,24},{20,28},{24,16},{28,20},{1,9},{5... | collective-permute-start | bytes 208904 | tf_op jit(solution)/shard_map/ppermute | solution.py:36
  81.4 5.2 %collective-permute-start.27 = (f32[1,136,128]{2,1,0:T(8,128)S(1)}, f32[1,136,128]{2,1,0:T(8,128)S(1)}, u32[]{:S(2)}, u32[]{:S(2)}) collective-permute-start(f32[1,136,128]{2,1,0:T(8,128)S(1)} %add_add_fusion.refs_0_), channel_id=1, source_target_pairs={{0,24},{4,28},{8,16},{12,20},{16,8},{20,12},{24,0},{28,4},{1,25},{... | collective-permute-start | bytes 208904 | tf_op jit(solution)/shard_map/ppermute | solution.py:36
  82.9 3.8 %collective-permute-start.28 = (f32[1,136,128]{2,1,0:T(8,128)S(1)}, f32[1,136,128]{2,1,0:T(8,128)S(1)}, u32[]{:S(2)}, u32[]{:S(2)}) collective-permute-start(f32[1,136,128]{2,1,0:T(8,128)S(1)} %add_add_fusion.refs_0_), channel_id=1, source_target_pairs={{0,4},{4,0},{8,12},{12,8},{16,20},{20,16},{24,28},{28,24},{1,5},{5... | collective-permute-start | bytes 208904 | tf_op jit(solution)/shard_map/ppermute | solution.py:36
  83.7 3.0 %collective-permute-start.29 = (f32[1,136,128]{2,1,0:T(8,128)S(1)}, f32[1,136,128]{2,1,0:T(8,128)S(1)}, u32[]{:S(2)}, u32[]{:S(2)}) collective-permute-start(f32[1,136,128]{2,1,0:T(8,128)S(1)} %collective-permute-done.25.refs_1_), channel_id=1, source_target_pairs={{0,4},{4,0},{8,12},{12,8},{16,20},{20,16},{24,28},{28,24},{1,5},{5... | collective-permute-start | bytes 208904 | tf_op jit(solution)/shard_map/ppermute | solution.py:36
  84.8 1.8 %collective-permute-start.30 = (f32[1,136,128]{2,1,0:T(8,128)S(1)}, f32[1,136,128]{2,1,0:T(8,128)S(1)}, u32[]{:S(2)}, u32[]{:S(2)}) collective-permute-start(f32[1,136,128]{2,1,0:T(8,128)S(1)} %collective-permute-done.26.refs_2_), channel_id=1, source_target_pairs={{0,4},{4,0},{8,12},{12,8},{16,20},{20,16},{24,28},{28,24},{1,5},{5... | collective-permute-start | bytes 208904 | tf_op jit(solution)/shard_map/ppermute | solution.py:36
  86.6 1.3 %collective-permute-start.31 = (f32[1,136,128]{2,1,0:T(8,128)S(1)}, f32[1,136,128]{2,1,0:T(8,128)S(1)}, u32[]{:S(2)}, u32[]{:S(2)}) collective-permute-start(f32[1,136,128]{2,1,0:T(8,128)S(1)} %collective-permute-done.27.refs_3_), channel_id=1, source_target_pairs={{0,4},{4,0},{8,12},{12,8},{16,20},{20,16},{24,28},{28,24},{1,5},{5... | collective-permute-start | bytes 208904 | tf_op jit(solution)/shard_map/ppermute | solution.py:36
  (13 other events, 63.9 us)

commit v3 on v2

--- a/solution.py
+++ b/solution.py
@@ -15,6 +15,7 @@
 PIECES = 1 << HALVINGS
 PIECE_ROWS = TILE + 8
 CHUNKS = 4
+TOGETHER = 2
 VMEM_BYTES = 16 << 20
 RESIST_BYTES = 44 << 20
 VMEM = pl.BlockSpec(memory_space=pltpu.VMEM)
@@ -89,31 +90,38 @@
     sums, outs = rest[: len(rest) - 6], rest[-6:-4]
     rows_ref, piece_buf, basis_buf, sems = rest[-4:]
     width, pixels = pieces[0].shape
+    each = select_ref.shape[1] // width
     gauges, doses = dose_ref.shape[0] // 2, dose_ref.shape[1]
+    taken = basis_buf.shape[0]
     start = pl.multiple_of(start_ref[0], pixels)
     copies = [
-        pltpu.make_async_copy(piece, piece_buf.at[o], sems.at[o]) for o, piece in enumerate(pieces)
+        pltpu.make_async_copy(piece, piece_buf.at[at], sems.at[at]) for at, piece in enumerate(pieces)
     ]
-    fetch = pltpu.make_async_copy(basis_ref.at[pl.ds(start, pixels), :], basis_buf, sems.at[count])
+    fetch = pltpu.make_async_copy(basis_ref.at[pl.ds(start, taken), :], basis_buf, sems.at[count])
     for copy in copies:
         copy.start()
     fetch.start()
-    picked = None
-    for o, copy in enumerate(copies):
-        copy.wait()
-        term = jnp.dot(
-            select_ref[:, o * width : (o + 1) * width],
-            piece_buf[o],
-            preferred_element_type=jnp.float32,
-        )
-        picked = term if picked is None else picked + term
     level = threshold_ref[0]
-    for d in range(doses):
-        answer = jnp.tanh(dose_ref[:, d : d + 1] * picked - level).astype(jnp.bfloat16)
-        for who in range(2):
-            low = (who * doses + d) * gauges
-            rows_ref[low : low + gauges, :] = answer[who * gauges : (who + 1) * gauges, :]
-    fetch.wait()
+    for g in range(count // each):
+        for copy in copies[g * each : (g + 1) * each]:
+            copy.wait()
+        if (g + 1) * each == count:
+            fetch.wait()
+        picked = None
+        for o in range(each):
+            term = jnp.dot(
+                select_ref[:, o * width : (o + 1) * width],
+                piece_buf[g * each + o],
+                preferred_element_type=jnp.float32,
+            )
+            picked = term if picked is None else picked + term
+        for d in range(doses):
+            answer = jnp.tanh(dose_ref[:, d : d + 1] * picked - level).astype(jnp.bfloat16)
+            for who in range(2):
+                low = (who * doses + d) * gauges
+                rows_ref[low : low + gauges, g * pixels : (g + 1) * pixels] = answer[
+                    who * gauges : (who + 1) * gauges, :
+                ]
     rows = gauges * doses
     for who in (1, 0):
         summed = jnp.dot(
@@ -128,6 +136,7 @@
     pair, pixels = pieces[0].shape
     terms = basis.shape[1]
     rows = gauges * doses
+    taken = pixels * len(pieces) * pair // select.shape[1]
     first = totals is None
     operands = [dose, select, *pieces, basis] + ([] if first else list(totals))
     shape = jax.ShapeDtypeStruct((rows, terms), jnp.float32)
@@ -137,17 +146,17 @@
         in_specs=[SMEM, SMEM, VMEM, VMEM] + [ANY] * (len(pieces) + 1) + [VMEM] * (0 if first else 2),
         out_specs=(VMEM, VMEM),
         scratch_shapes=[
-            pltpu.VMEM((2 * rows, pixels), jnp.bfloat16),
+            pltpu.VMEM((2 * rows, taken), jnp.bfloat16),
             pltpu.VMEM((len(pieces), pair, pixels), jnp.bfloat16),
-            pltpu.VMEM((pixels, terms), jnp.bfloat16),
+            pltpu.VMEM((taken, terms), jnp.bfloat16),
             pltpu.SemaphoreType.DMA((len(pieces) + 1,)),
         ],
         input_output_aliases={} if first else {len(operands): 0, len(operands) + 1: 1},
         compiler_params=pltpu.CompilerParams(vmem_limit_bytes=RESIST_BYTES),
         cost_estimate=pl.CostEstimate(
-            flops=4 * rows * pixels * terms,
-            bytes_accessed=2 * pixels * (terms + pair * len(pieces)),
-            transcendentals=2 * rows * pixels,
+            flops=4 * rows * taken * terms,
+            bytes_accessed=2 * taken * (terms + select.shape[1]),
+            transcendentals=2 * rows * taken,
         ),
         name="resist",
     )(start, threshold, *operands)
@@ -204,16 +213,24 @@
                 ref[where - low, TILE:, :] = foot
 
 
-def factor_tile(block):
+def factor_tile(block, cols_ref, ahead_ref):
     count = TILE // GROUP
     sub = lax.broadcasted_iota(jnp.int32, (8, TILE), 0)
     lane = lax.broadcasted_iota(jnp.int32, (8, TILE), 1)
     left = [block[8 * q : 8 * q + 8, :] for q in range(count)]
     right = [jnp.where(lane == sub + 8 * q, 1.0, 0.0).astype(jnp.float32) for q in range(count)]
+    cols = [full(left[0][:, k : k + 1]) for k in range(GROUP)]
     for p in range(count):
         base = GROUP * p
-        cols = [full(left[p][:, base + k : base + k + 1]) for k in range(GROUP)]
-        a = [[full(cols[k][m : m + 1, :]) if m >= k else None for k in range(GROUP)] for m in range(GROUP)]
+        corner = 64 * p
+        for k in range(GROUP):
+            cols_ref[corner + 8 * k : corner + 8 * k + 8, :] = cols[k]
+        a = [
+            [cols_ref[pl.ds(corner + 8 * k + m, 8, stride=0), :] if m >= k else None for k in range(GROUP)]
+            for m in range(GROUP)
+        ]
+        if p + 1 < count:
+            cols = [full(left[p + 1][:, base + 8 + k : base + 9 + k]) for k in range(GROUP)]
         low = [[None] * GROUP for _ in range(GROUP)]
         root = []
         for k in range(GROUP):
@@ -239,6 +256,12 @@
                 c[k] = c[k] * root[k]
                 for m in range(k + 1, GROUP):
                     c[m] = c[m] - low[m][k] * c[k]
+            if q == p + 1:
+                for k in range(GROUP):
+                    ahead_ref[corner + 8 * k : corner + 8 * k + 8, :] = c[k]
+                for m in range(GROUP):
+                    for k in range(GROUP):
+                        cols[m] = cols[m] - c[k] * ahead_ref[pl.ds(corner + 8 * k + m, 8, stride=0), :]
             for k in range(GROUP):
                 left[q] = left[q] - c[k] * upper[k]
                 right[q] = right[q] - c[k] * other[k]
@@ -253,7 +276,7 @@
 
 def factor_kernel(table, groups, me_ref, *refs):
     sources = refs[: len(groups)]
-    feat_ref, misfit_ref, deriv_ref, params_ref, upper_ref, new_ref, resid_ref, stage, work, inv, rhs = refs[len(groups) :]
+    feat_ref, misfit_ref, deriv_ref, params_ref, upper_ref, new_ref, resid_ref, stage, work, inv, rhs, cols_ref, ahead_ref = refs[len(groups) :]
     terms = work.shape[0]
     count = terms // TILE
     me = me_ref[0]
@@ -281,7 +304,7 @@
 
     def step(b, carry):
         off = pl.multiple_of(b * TILE, TILE)
-        left, right = factor_tile(work[pl.ds(off, TILE), pl.ds(off, TILE)])
+        left, right = factor_tile(work[pl.ds(off, TILE), pl.ds(off, TILE)], cols_ref, ahead_ref)
         for q in range(TILE // GROUP):
             upper_ref[pl.ds(off + 8 * q, 8), pl.ds(off, TILE)] = left[q]
             inv[pl.ds(off + 8 * q, 8), :] = right[q]
@@ -382,9 +405,9 @@
     dose, select = [jnp.concatenate(both, axis=0) for both in zip(mine_orders, their_orders)]
     level = STEEPNESS * threshold
     totals = None
-    for k in range(CHUNKS):
+    for k in range(0, CHUNKS, TOGETHER):
         start = (core * half + k * step).astype(jnp.int32)[None]
-        held = [chunks[k][o] for o in offsets]
+        held = [chunk[o] for chunk in chunks[k : k + TOGETHER] for o in offsets]
         totals = resist_rows(start, level, dose, select, held, basis_terms, totals)
     mine_total, their_total = totals
     rows = gauges * doses
@@ -437,6 +460,8 @@
             pltpu.VMEM((terms, terms), jnp.float32),
             pltpu.VMEM((terms, TILE), jnp.float32),
             pltpu.VMEM((8, terms), jnp.float32),
+            pltpu.VMEM((TILE * GROUP, TILE), jnp.float32),
+            pltpu.VMEM((TILE * GROUP, TILE), jnp.float32),
         ],
         compiler_params=pltpu.CompilerParams(vmem_limit_bytes=VMEM_BYTES),
         name="factor",

time: 111 us -> 105 us (0.946)
  Pallas kernels: 40.8 us -> 33.7 us
  waiting for transfers between devices: 32.4 us -> 38.8 us
  local copies, waits for them, and re-layouts: 5.64 us -> 3.72 us
  starting transfers between devices: 28.1 us -> 26.4 us
  other arithmetic: 1.94 us -> 0.54 us
    ppermute x32, waiting for transfers between devices: 32.4 us -> 38.8 us  [swap(): return lax.ppermute(value, axis, [(i, i ^ bit) for i in range(size)])]
    pallas_call x4 -> x2, Pallas kernels: 14.8 us -> 11.9 us  [resist_rows(): pl.pallas_call(functools.partial(resist_kernel, first), out_shape=(shape,...]
    pallas_call x1, Pallas kernels: 21.9 us -> 19 us  [local(): pl.pallas_call(functools.partial(factor_kernel, table, groups), in_specs=...]
    unnamed x29 -> x21, local copies, waits for them, and re-layouts: 4.36 us -> 2.44 us
    ppermute x32, starting transfers between devices: 28.1 us -> 26.4 us  [swap(): return lax.ppermute(value, axis, [(i, i ^ bit) for i in range(size)])]
    concatenate x4, other arithmetic: 1.48 us -> 0.07 us  [local(): block = jnp.concatenate([mine, swap(theirs, 'gauge', 1)], axis=0)]
    pallas_call x1, Pallas kernels: 4.14 us -> 2.78 us  [local(): pl.pallas_call(functools.partial(normal_kernel, scale, table), in_specs=[...]
  transfers between devices with their start and end apart: 32 -> 32, of which waited for: 18 -> 19; matrix products, arithmetic and copies ran while one was open for 2% -> 1% of each run, Pallas kernels for 10% -> 5%
where the time goes in v3:
time: 105 us
  waiting for transfers between devices  38.8 us (37%)
  Pallas kernels  33.7 us (32%)
  starting transfers between devices  26.4 us (25%)
  local copies, waits for them, and re-layouts  3.72 us (4%)
  between operations  1.57 us (1%)
    ppermute x32, waiting for transfers between devices, swap(): return lax.ppermute(value, axis, [(i, i ^ bit) for i in range(size)])  38.8 us
    ppermute x32, starting transfers between devices, swap(): return lax.ppermute(value, axis, [(i, i ^ bit) for i in range(size)])  26.4 us
    pallas_call x1, Pallas kernels, local(): pl.pallas_call(functools.partial(factor_kernel, table, groups), in_specs=...  19 us
    pallas_call x2, Pallas kernels, resist_rows(): pl.pallas_call(functools.partial(resist_kernel, first), out_shape=(shape,...  11.9 us
    pallas_call x1, Pallas kernels, local(): pl.pallas_call(functools.partial(normal_kernel, scale, table), in_specs=[...  2.78 us
    unnamed x21, local copies, waits for them, and re-layouts  2.44 us
  transfers between devices with their start and end apart: 32, of which 19 were waited for; matrix products, arithmetic and copies ran while one was open for 1% of the time, Pallas kernels for 5%

profile of v3, /device:TPU:0, one launch (start us, length us, event | category | flops | bytes accessed | tf_op | source)
XLA Modules:
  0.0 104.7 jit_solution(15871756628535859819)
XLA Ops:
  0.7 1.1 %dynamic-slice_bitcast_fusion.1 = (bf16[64,1024]{1,0:T(8,128)(2,1)S(1)}, bf16[64,1024]{1,0:T(8,128)(2,1)S(1)}) fusion(bf16[1,64,8192]{2,1,0:T(8,128)(2,1)} %param.9, s32[]{:T(128)S(6)} %select_n.45, s32[]{:T(128)S(6)} %select_n.46), kind=kLoop, calls=%fused_computation.12 | loop fusion | bytes 524296 | tf_op jit(solution)/shard_map/dynamic_slice | solution.py:378
  2.3 1.0 collective-permute-done.1
  5.1 2.7 %collective-permute-start.3 = (bf16[128,1024]{1,0:T(8,128)(2,1)S(1)}, bf16[128,1024]{1,0:T(8,128)(2,1)S(1)}, u32[]{:S(2)}, u32[]{:S(2)}) collective-permute-start(bf16[128,1024]{1,0:T(8,128)(2,1)S(1)} %pad_maximum_fusion.refs_0_), channel_id=1, source_target_pairs={{0,8},{4,12},{8,0},{12,4},{16,24},{20,28},{24,16},{28,20},{1,9},{5... | collective-permute-start | bytes 786440 | tf_op jit(solution)/shard_map/ppermute | solution.py:37
  7.8 1.5 %collective-permute-start.13 = (bf16[128,1024]{1,0:T(8,128)(2,1)S(1)}, bf16[128,1024]{1,0:T(8,128)(2,1)S(1)}, u32[]{:S(2)}, u32[]{:S(2)}) collective-permute-start(bf16[128,1024]{1,0:T(8,128)(2,1)S(1)} %pad_maximum_fusion.refs_0_), channel_id=1, source_target_pairs={{0,16},{4,20},{8,24},{12,28},{16,0},{20,4},{24,8},{28,12},{1,17},{... | collective-permute-start | bytes 786440 | tf_op jit(solution)/shard_map/ppermute | solution.py:37
  11.2 3.7 %collective-permute-done.3.refs_1_ = bf16[128,1024]{1,0:T(8,128)(2,1)S(1)} collective-permute-done((bf16[128,1024]{1,0:T(8,128)(2,1)S(1)}, bf16[128,1024]{1,0:T(8,128)(2,1)S(1)}, u32[]{:S(2)}, u32[]{:S(2)}) %collective-permute-start.3) | collective-permute-done | bytes 262176 | tf_op jit(solution)/shard_map/ppermute | solution.py:37
  15.3 2.0 %collective-permute-start.4 = (bf16[128,1024]{1,0:T(8,128)(2,1)S(1)}, bf16[128,1024]{1,0:T(8,128)(2,1)S(1)}, u32[]{:S(2)}, u32[]{:S(2)}) collective-permute-start(bf16[128,1024]{1,0:T(8,128)(2,1)S(1)} %pad_maximum_fusion.1.refs_0_), channel_id=1, source_target_pairs={{0,8},{4,12},{8,0},{12,4},{16,24},{20,28},{24,16},{28,20},{1,9},{5... | collective-permute-start | bytes 786440 | tf_op jit(solution)/shard_map/ppermute | solution.py:37
  17.3 1.5 %collective-permute-start.14 = (bf16[128,1024]{1,0:T(8,128)(2,1)S(1)}, bf16[128,1024]{1,0:T(8,128)(2,1)S(1)}, u32[]{:S(2)}, u32[]{:S(2)}) collective-permute-start(bf16[128,1024]{1,0:T(8,128)(2,1)S(1)} %collective-permute-done.3.refs_1_), channel_id=1, source_target_pairs={{0,16},{4,20},{8,24},{12,28},{16,0},{20,4},{24,8},{28,12},{1,17},{... | collective-permute-start | bytes 786440 | tf_op jit(solution)/shard_map/ppermute | solution.py:37
  19.0 3.6 %collective-permute-done.9.refs_6_ = bf16[128,1024]{1,0:T(8,128)(2,1)S(1)} collective-permute-done((bf16[128,1024]{1,0:T(8,128)(2,1)S(1)}, bf16[128,1024]{1,0:T(8,128)(2,1)S(1)}, u32[]{:S(2)}, u32[]{:S(2)}) %collective-permute-start.9) | collective-permute-done | bytes 262176 | tf_op jit(solution)/shard_map/ppermute | solution.py:37
  22.6 1.5 %collective-permute-start.11 = (bf16[128,1024]{1,0:T(8,128)(2,1)S(1)}, bf16[128,1024]{1,0:T(8,128)(2,1)S(1)}, u32[]{:S(2)}, u32[]{:S(2)}) collective-permute-start(bf16[128,1024]{1,0:T(8,128)(2,1)S(1)} %pad_maximum_fusion.2.refs_4_), channel_id=1, source_target_pairs={{0,16},{4,20},{8,24},{12,28},{16,0},{20,4},{24,8},{28,12},{1,17},{... | collective-permute-start | bytes 786440 | tf_op jit(solution)/shard_map/ppermute | solution.py:37
  25.5 2.7 %collective-permute-done.14.refs_3_ = bf16[128,1024]{1,0:T(8,128)(2,1)S(1)} collective-permute-done((bf16[128,1024]{1,0:T(8,128)(2,1)S(1)}, bf16[128,1024]{1,0:T(8,128)(2,1)S(1)}, u32[]{:S(2)}, u32[]{:S(2)}) %collective-permute-start.14) | collective-permute-done | bytes 262176 | tf_op jit(solution)/shard_map/ppermute | solution.py:37
  28.2 2.0 %collective-permute-start.6 = (bf16[128,1024]{1,0:T(8,128)(2,1)S(1)}, bf16[128,1024]{1,0:T(8,128)(2,1)S(1)}, u32[]{:S(2)}, u32[]{:S(2)}) collective-permute-start(bf16[128,1024]{1,0:T(8,128)(2,1)S(1)} %collective-permute-done.4.refs_1_), channel_id=1, source_target_pairs={{0,16},{4,20},{8,24},{12,28},{16,0},{20,4},{24,8},{28,12},{1,17},{... | collective-permute-start | bytes 786440 | tf_op jit(solution)/shard_map/ppermute | solution.py:37
  30.2 3.6 %collective-permute-done.11.refs_6_ = bf16[128,1024]{1,0:T(8,128)(2,1)S(1)} collective-permute-done((bf16[128,1024]{1,0:T(8,128)(2,1)S(1)}, bf16[128,1024]{1,0:T(8,128)(2,1)S(1)}, u32[]{:S(2)}, u32[]{:S(2)}) %collective-permute-start.11) | collective-permute-done | bytes 262176 | tf_op jit(solution)/shard_map/ppermute | solution.py:37
  34.8 5.2 %resist.2 = (f32[704,512]{1,0:T(8,128)S(1)}, f32[704,512]{1,0:T(8,128)}) custom-call(s32[1]{0:T(128)} %bitcast.11.start_ref, f32[1]{0:T(128)S(6)} %mul.21.threshold_ref, f32[128,11]{1,0:T(8,128)S(1)} %copy.25.dose_ref, bf16[128,512]{1,0:T(8,128)(2,1)S(1)} %pad_maximum_fusion.4.select_ref, bf16[128,1024]{1,0:T(8,128)(2,1)S(1)} %pad_maximum_fusion.refs_0_, ...), custom_call_target="tpu_custom_call" | custom-call | flops 2952790016 | bytes 4194304 | tf_op jit(solution)/shard_map/resist/pallas_call | solution.py:143
  40.0 4.1 %collective-permute-done.6.refs_3_ = bf16[128,1024]{1,0:T(8,128)(2,1)S(1)} collective-permute-done((bf16[128,1024]{1,0:T(8,128)(2,1)S(1)}, bf16[128,1024]{1,0:T(8,128)(2,1)S(1)}, u32[]{:S(2)}, u32[]{:S(2)}) %collective-permute-start.6) | collective-permute-done | bytes 262176 | tf_op jit(solution)/shard_map/ppermute | solution.py:37
  44.1 6.7 %resist.3 = (f32[704,512]{1,0:T(8,128)S(1)}, f32[704,512]{1,0:T(8,128)}) custom-call(s32[1]{0:T(128)} %bitcast.1.start_ref, f32[1]{0:T(128)S(6)} %mul.21.threshold_ref, f32[128,11]{1,0:T(8,128)S(1)} %copy.25.dose_ref, bf16[128,512]{1,0:T(8,128)(2,1)S(1)} %pad_maximum_fusion.4.select_ref, ...), custom_call_target="tpu_custom_call", output_to_operand_aliasing={{0}: (13, {}), {1}: (14, {})} | custom-call | flops 2952790016 | bytes 4194304 | tf_op jit(solution)/shard_map/resist/pallas_call | solution.py:143
  51.0 3.3 %collective-permute-done.17.other_ref = f32[704,512]{1,0:T(8,128)S(1)} collective-permute-done((f32[704,512]{1,0:T(8,128)}, f32[704,512]{1,0:T(8,128)S(1)}, u32[]{:S(2)}, u32[]{:S(2)}) %collective-permute-start.17) | collective-permute-done | bytes 1441824 | tf_op jit(solution)/shard_map/ppermute | solution.py:37
  54.3 2.8 %normal.1 = (f32[704,512]{1,0:T(8,128)S(1)}, f32[64,11]{1,0:T(8,128)S(1)}, f32[64,11]{1,0:T(8,128)S(1)}, f32[4,136,128]{2,1,0:T(8,128)S(1)}, f32[4,136,128]{2,1,0:T(8,128)S(1)}) custom-call(s32[1]{0:T(128)} %bitcast.me_ref, f32[704,512]{1,0:T(8,128)S(1)} %get-tuple-element.35.mine_ref, f32[704,512]{1,0:T(8,128)S(1)} %collective-permute-done.17.other_ref, ...), custom_call_target="tpu_custom_call" | custom-call | tf_op jit(solution)/shard_map/normal/pallas_call | solution.py:420
  57.3 1.4 %collective-permute-done.18 = f32[4,136,128]{2,1,0:T(8,128)S(1)} collective-permute-done((f32[4,136,128]{2,1,0:T(8,128)S(1)}, f32[4,136,128]{2,1,0:T(8,128)S(1)}, u32[]{:S(2)}, u32[]{:S(2)}) %collective-permute-start.18) | collective-permute-done | bytes 278560 | tf_op jit(solution)/shard_map/ppermute | solution.py:37
  58.8 1.6 %collective-permute-start.19 = (f32[1,136,128]{2,1,0:T(8,128)S(1)}, f32[1,136,128]{2,1,0:T(8,128)S(1)}, u32[]{:S(2)}, u32[]{:S(2)}) collective-permute-start(f32[1,136,128]{2,1,0:T(8,128)S(1)} %get-tuple-element.66), channel_id=1, source_target_pairs={{0,16},{4,20},{8,24},{12,28},{16,0},{20,4},{24,8},{28,12},{1,17},{... | collective-permute-start | bytes 208904 | tf_op jit(solution)/shard_map/ppermute | solution.py:37
  60.9 1.4 %collective-permute-start.21 = (f32[1,136,128]{2,1,0:T(8,128)S(1)}, f32[1,136,128]{2,1,0:T(8,128)S(1)}, u32[]{:S(2)}, u32[]{:S(2)}) collective-permute-start(f32[1,136,128]{2,1,0:T(8,128)S(1)} %get-tuple-element.64), channel_id=1, source_target_pairs={{0,24},{4,28},{8,16},{12,20},{16,8},{20,12},{24,0},{28,4},{1,25},{... | collective-permute-start | bytes 208904 | tf_op jit(solution)/shard_map/ppermute | solution.py:37
  63.1 1.9 %collective-permute-done.20 = f32[1,136,128]{2,1,0:T(8,128)S(1)} collective-permute-done((f32[1,136,128]{2,1,0:T(8,128)S(1)}, f32[1,136,128]{2,1,0:T(8,128)S(1)}, u32[]{:S(2)}, u32[]{:S(2)}) %collective-permute-start.20) | collective-permute-done | bytes 69664 | tf_op jit(solution)/shard_map/ppermute | solution.py:37
  65.0 1.1 %collective-permute-done.21 = f32[1,136,128]{2,1,0:T(8,128)S(1)} collective-permute-done((f32[1,136,128]{2,1,0:T(8,128)S(1)}, f32[1,136,128]{2,1,0:T(8,128)S(1)}, u32[]{:S(2)}, u32[]{:S(2)}) %collective-permute-start.21) | collective-permute-done | bytes 69664 | tf_op jit(solution)/shard_map/ppermute | solution.py:37
  66.1 1.6 %collective-permute-start.22 = (f32[1,136,128]{2,1,0:T(8,128)S(1)}, f32[1,136,128]{2,1,0:T(8,128)S(1)}, u32[]{:S(2)}, u32[]{:S(2)}) collective-permute-start(f32[1,136,128]{2,1,0:T(8,128)S(1)} %fusion.1), channel_id=1, source_target_pairs={{0,1},{1,0},{2,3},{3,2},{4,5},{5,4},{6,7},{7,6},{8,9},{9,8},{10,11... | collective-permute-start | bytes 208904 | tf_op jit(solution)/shard_map/ppermute | solution.py:37
  67.8 2.6 %collective-permute-start.23 = (f32[1,136,128]{2,1,0:T(8,128)S(1)}, f32[1,136,128]{2,1,0:T(8,128)S(1)}, u32[]{:S(2)}, u32[]{:S(2)}) collective-permute-start(f32[1,136,128]{2,1,0:T(8,128)S(1)} %fusion.1), channel_id=1, source_target_pairs={{0,2},{1,3},{2,0},{3,1},{4,6},{5,7},{6,4},{7,5},{8,10},{9,11},{10,... | collective-permute-start | bytes 208904 | tf_op jit(solution)/shard_map/ppermute | solution.py:37
  71.2 3.3 %collective-permute-done.23 = f32[1,136,128]{2,1,0:T(8,128)S(1)} collective-permute-done((f32[1,136,128]{2,1,0:T(8,128)S(1)}, f32[1,136,128]{2,1,0:T(8,128)S(1)}, u32[]{:S(2)}, u32[]{:S(2)}) %collective-permute-start.23) | collective-permute-done | bytes 69664 | tf_op jit(solution)/shard_map/ppermute | solution.py:37
  74.5 1.9 %collective-permute-done.24 = f32[1,136,128]{2,1,0:T(8,128)S(1)} collective-permute-done((f32[1,136,128]{2,1,0:T(8,128)S(1)}, f32[1,136,128]{2,1,0:T(8,128)S(1)}, u32[]{:S(2)}, u32[]{:S(2)}) %collective-permute-start.24) | collective-permute-done | bytes 69664 | tf_op jit(solution)/shard_map/ppermute | solution.py:37
  76.5 1.2 %collective-permute-start.25 = (f32[1,136,128]{2,1,0:T(8,128)S(1)}, f32[1,136,128]{2,1,0:T(8,128)S(1)}, u32[]{:S(2)}, u32[]{:S(2)}) collective-permute-start(f32[1,136,128]{2,1,0:T(8,128)S(1)} %add_add_fusion.refs_0_), channel_id=1, source_target_pairs={{0,16},{4,20},{8,24},{12,28},{16,0},{20,4},{24,8},{28,12},{1,17},{... | collective-permute-start | bytes 208904 | tf_op jit(solution)/shard_map/ppermute | solution.py:37
  78.6 1.4 %collective-permute-start.27 = (f32[1,136,128]{2,1,0:T(8,128)S(1)}, f32[1,136,128]{2,1,0:T(8,128)S(1)}, u32[]{:S(2)}, u32[]{:S(2)}) collective-permute-start(f32[1,136,128]{2,1,0:T(8,128)S(1)} %add_add_fusion.refs_0_), channel_id=1, source_target_pairs={{0,24},{4,28},{8,16},{12,20},{16,8},{20,12},{24,0},{28,4},{1,25},{... | collective-permute-start | bytes 208904 | tf_op jit(solution)/shard_map/ppermute | solution.py:37
  80.9 1.1 %collective-permute-done.26.refs_2_ = f32[1,136,128]{2,1,0:T(8,128)S(1)} collective-permute-done((f32[1,136,128]{2,1,0:T(8,128)S(1)}, f32[1,136,128]{2,1,0:T(8,128)S(1)}, u32[]{:S(2)}, u32[]{:S(2)}) %collective-permute-start.26) | collective-permute-done | bytes 69664 | tf_op jit(solution)/shard_map/ppermute | solution.py:37
  82.0 1.8 %collective-permute-done.27.refs_3_ = f32[1,136,128]{2,1,0:T(8,128)S(1)} collective-permute-done((f32[1,136,128]{2,1,0:T(8,128)S(1)}, f32[1,136,128]{2,1,0:T(8,128)S(1)}, u32[]{:S(2)}, u32[]{:S(2)}) %collective-permute-start.27) | collective-permute-done | bytes 69664 | tf_op jit(solution)/shard_map/ppermute | solution.py:37
  83.8 1.2 %collective-permute-done.31.refs_7_ = f32[1,136,128]{2,1,0:T(8,128)S(1)} collective-permute-done((f32[1,136,128]{2,1,0:T(8,128)S(1)}, f32[1,136,128]{2,1,0:T(8,128)S(1)}, u32[]{:S(2)}, u32[]{:S(2)}) %collective-permute-start.31) | collective-permute-done | bytes 69664 | tf_op jit(solution)/shard_map/ppermute | solution.py:37
  85.1 19.0 %factor.1 = (f32[512,512]{1,0:T(8,128)}, f32[1,512]{1,0:T(1,128)}, f32[64,11]{1,0:T(8,128)S(1)}) custom-call(s32[1]{0:T(128)} %bitcast.me_ref, f32[1,136,128]{2,1,0:T(8,128)S(1)} %add_add_fusion.refs_0_, f32[1,136,128]{2,1,0:T(8,128)S(1)} %collective-permute-done.25.refs_1_, f32[1,136,128]{2,1,0:T(8,128)S(1)} %collective-permute-done.26.refs_2_, ...), custom_call_target="tpu_custom_call" | custom-call | tf_op jit(solution)/shard_map/factor/pallas_call | solution.py:449
  (79 shorter events, 11.4 us)
Async XLA Ops:
  1.8 1.5 %collective-permute-start.1 = (bf16[64,1024]{1,0:T(8,128)(2,1)S(1)}, bf16[64,1024]{1,0:T(8,128)(2,1)S(1)}, u32[]{:S(2)}, u32[]{:S(2)}) collective-permute-start(bf16[64,1024]{1,0:T(8,128)(2,1)S(1)} %get-tuple-element.63), channel_id=1, source_target_pairs={{0,4},{4,0},{8,12},{12,8},{16,20},{20,16},{24,28},{28,24},{1,5},{5... | collective-permute-start | bytes 393224 | tf_op jit(solution)/shard_map/ppermute | solution.py:37
  3.4 5.9 %collective-permute-start.8 = (bf16[64,1024]{1,0:T(8,128)(2,1)S(1)}, bf16[64,1024]{1,0:T(8,128)(2,1)S(1)}, u32[]{:S(2)}, u32[]{:S(2)}) collective-permute-start(bf16[64,1024]{1,0:T(8,128)(2,1)S(1)} %get-tuple-element.57), channel_id=1, source_target_pairs={{0,4},{4,0},{8,12},{12,8},{16,20},{20,16},{24,28},{28,24},{1,5},{5... | collective-permute-start | bytes 393224 | tf_op jit(solution)/shard_map/ppermute | solution.py:37
  3.8 5.5 %collective-permute-start.7 = (bf16[64,1024]{1,0:T(8,128)(2,1)S(1)}, bf16[64,1024]{1,0:T(8,128)(2,1)S(1)}, u32[]{:S(2)}, u32[]{:S(2)}) collective-permute-start(bf16[64,1024]{1,0:T(8,128)(2,1)S(1)} %get-tuple-element.58), channel_id=1, source_target_pairs={{0,4},{4,0},{8,12},{12,8},{16,20},{20,16},{24,28},{28,24},{1,5},{5... | collective-permute-start | bytes 393224 | tf_op jit(solution)/shard_map/ppermute | solution.py:37
  4.0 10.9 %collective-permute-start = (s32[64,15]{0,1:T(8,128)S(1)}, s32[64,15]{0,1:T(8,128)S(1)}, u32[]{:S(2)}, u32[]{:S(2)}) collective-permute-start(s32[64,15]{0,1:T(8,128)S(1)} %pad_add_fusion), channel_id=1, source_target_pairs={{0,4},{4,0},{8,12},{12,8},{16,20},{20,16},{24,28},{28,24},{1,5},{5... | collective-permute-start | bytes 11528 | tf_op jit(solution)/shard_map/ppermute | solution.py:37
  5.1 9.9 %collective-permute-start.3 = (bf16[128,1024]{1,0:T(8,128)(2,1)S(1)}, bf16[128,1024]{1,0:T(8,128)(2,1)S(1)}, u32[]{:S(2)}, u32[]{:S(2)}) collective-permute-start(bf16[128,1024]{1,0:T(8,128)(2,1)S(1)} %pad_maximum_fusion.refs_0_), channel_id=1, source_target_pairs={{0,8},{4,12},{8,0},{12,4},{16,24},{20,28},{24,16},{28,20},{1,9},{5... | collective-permute-start | bytes 786440 | tf_op jit(solution)/shard_map/ppermute | solution.py:37
  7.8 16.3 %collective-permute-start.13 = (bf16[128,1024]{1,0:T(8,128)(2,1)S(1)}, bf16[128,1024]{1,0:T(8,128)(2,1)S(1)}, u32[]{:S(2)}, u32[]{:S(2)}) collective-permute-start(bf16[128,1024]{1,0:T(8,128)(2,1)S(1)} %pad_maximum_fusion.refs_0_), channel_id=1, source_target_pairs={{0,16},{4,20},{8,24},{12,28},{16,0},{20,4},{24,8},{28,12},{1,17},{... | collective-permute-start | bytes 786440 | tf_op jit(solution)/shard_map/ppermute | solution.py:37
  9.3 1.3 %collective-permute-start.2 = (bf16[64,1024]{1,0:T(8,128)(2,1)S(1)}, bf16[64,1024]{1,0:T(8,128)(2,1)S(1)}, u32[]{:S(2)}, u32[]{:S(2)}) collective-permute-start(bf16[64,1024]{1,0:T(8,128)(2,1)S(1)} %get-tuple-element.60), channel_id=1, source_target_pairs={{0,4},{4,0},{8,12},{12,8},{16,20},{20,16},{24,28},{28,24},{1,5},{5... | collective-permute-start | bytes 393224 | tf_op jit(solution)/shard_map/ppermute | solution.py:37
  9.3 13.2 %collective-permute-start.9 = (bf16[128,1024]{1,0:T(8,128)(2,1)S(1)}, bf16[128,1024]{1,0:T(8,128)(2,1)S(1)}, u32[]{:S(2)}, u32[]{:S(2)}) collective-permute-start(bf16[128,1024]{1,0:T(8,128)(2,1)S(1)} %pad_maximum_fusion.3.refs_4_), channel_id=1, source_target_pairs={{0,16},{4,20},{8,24},{12,28},{16,0},{20,4},{24,8},{28,12},{1,17},{... | collective-permute-start | bytes 786440 | tf_op jit(solution)/shard_map/ppermute | solution.py:37
  10.6 14.1 %collective-permute-start.15 = (bf16[128,1024]{1,0:T(8,128)(2,1)S(1)}, bf16[128,1024]{1,0:T(8,128)(2,1)S(1)}, u32[]{:S(2)}, u32[]{:S(2)}) collective-permute-start(bf16[128,1024]{1,0:T(8,128)(2,1)S(1)} %pad_maximum_fusion.3.refs_4_), channel_id=1, source_target_pairs={{0,8},{4,12},{8,0},{12,4},{16,24},{20,28},{24,16},{28,20},{1,9},{5... | collective-permute-start | bytes 786440 | tf_op jit(solution)/shard_map/ppermute | solution.py:37
  15.3 12.9 %collective-permute-start.4 = (bf16[128,1024]{1,0:T(8,128)(2,1)S(1)}, bf16[128,1024]{1,0:T(8,128)(2,1)S(1)}, u32[]{:S(2)}, u32[]{:S(2)}) collective-permute-start(bf16[128,1024]{1,0:T(8,128)(2,1)S(1)} %pad_maximum_fusion.1.refs_0_), channel_id=1, source_target_pairs={{0,8},{4,12},{8,0},{12,4},{16,24},{20,28},{24,16},{28,20},{1,9},{5... | collective-permute-start | bytes 786440 | tf_op jit(solution)/shard_map/ppermute | solution.py:37
  17.3 10.8 %collective-permute-start.14 = (bf16[128,1024]{1,0:T(8,128)(2,1)S(1)}, bf16[128,1024]{1,0:T(8,128)(2,1)S(1)}, u32[]{:S(2)}, u32[]{:S(2)}) collective-permute-start(bf16[128,1024]{1,0:T(8,128)(2,1)S(1)} %collective-permute-done.3.refs_1_), channel_id=1, source_target_pairs={{0,16},{4,20},{8,24},{12,28},{16,0},{20,4},{24,8},{28,12},{1,17},{... | collective-permute-start | bytes 786440 | tf_op jit(solution)/shard_map/ppermute | solution.py:37
  22.6 11.2 %collective-permute-start.11 = (bf16[128,1024]{1,0:T(8,128)(2,1)S(1)}, bf16[128,1024]{1,0:T(8,128)(2,1)S(1)}, u32[]{:S(2)}, u32[]{:S(2)}) collective-permute-start(bf16[128,1024]{1,0:T(8,128)(2,1)S(1)} %pad_maximum_fusion.2.refs_4_), channel_id=1, source_target_pairs={{0,16},{4,20},{8,24},{12,28},{16,0},{20,4},{24,8},{28,12},{1,17},{... | collective-permute-start | bytes 786440 | tf_op jit(solution)/shard_map/ppermute | solution.py:37
  24.1 9.8 %collective-permute-start.16 = (bf16[128,1024]{1,0:T(8,128)(2,1)S(1)}, bf16[128,1024]{1,0:T(8,128)(2,1)S(1)}, u32[]{:S(2)}, u32[]{:S(2)}) collective-permute-start(bf16[128,1024]{1,0:T(8,128)(2,1)S(1)} %collective-permute-done.9.refs_6_), channel_id=1, source_target_pairs={{0,8},{4,12},{8,0},{12,4},{16,24},{20,28},{24,16},{28,20},{1,9},{5... | collective-permute-start | bytes 786440 | tf_op jit(solution)/shard_map/ppermute | solution.py:37
  25.4 14.6 %collective-permute-start.5 = (bf16[128,1024]{1,0:T(8,128)(2,1)S(1)}, bf16[128,1024]{1,0:T(8,128)(2,1)S(1)}, u32[]{:S(2)}, u32[]{:S(2)}) collective-permute-start(bf16[128,1024]{1,0:T(8,128)(2,1)S(1)} %pad_maximum_fusion.1.refs_0_), channel_id=1, source_target_pairs={{0,16},{4,20},{8,24},{12,28},{16,0},{20,4},{24,8},{28,12},{1,17},{... | collective-permute-start | bytes 786440 | tf_op jit(solution)/shard_map/ppermute | solution.py:37
  28.2 11.8 %collective-permute-start.10 = (bf16[128,1024]{1,0:T(8,128)(2,1)S(1)}, bf16[128,1024]{1,0:T(8,128)(2,1)S(1)}, u32[]{:S(2)}, u32[]{:S(2)}) collective-permute-start(bf16[128,1024]{1,0:T(8,128)(2,1)S(1)} %pad_maximum_fusion.2.refs_4_), channel_id=1, source_target_pairs={{0,8},{4,12},{8,0},{12,4},{16,24},{20,28},{24,16},{28,20},{1,9},{5... | collective-permute-start | bytes 786440 | tf_op jit(solution)/shard_map/ppermute | solution.py:37
  28.2 15.9 %collective-permute-start.6 = (bf16[128,1024]{1,0:T(8,128)(2,1)S(1)}, bf16[128,1024]{1,0:T(8,128)(2,1)S(1)}, u32[]{:S(2)}, u32[]{:S(2)}) collective-permute-start(bf16[128,1024]{1,0:T(8,128)(2,1)S(1)} %collective-permute-done.4.refs_1_), channel_id=1, source_target_pairs={{0,16},{4,20},{8,24},{12,28},{16,0},{20,4},{24,8},{28,12},{1,17},{... | collective-permute-start | bytes 786440 | tf_op jit(solution)/shard_map/ppermute | solution.py:37
  33.8 10.4 %collective-permute-start.12 = (bf16[128,1024]{1,0:T(8,128)(2,1)S(1)}, bf16[128,1024]{1,0:T(8,128)(2,1)S(1)}, u32[]{:S(2)}, u32[]{:S(2)}) collective-permute-start(bf16[128,1024]{1,0:T(8,128)(2,1)S(1)} %collective-permute-done.11.refs_6_), channel_id=1, source_target_pairs={{0,8},{4,12},{8,0},{12,4},{16,24},{20,28},{24,16},{28,20},{1,9},{5... | collective-permute-start | bytes 786440 | tf_op jit(solution)/shard_map/ppermute | solution.py:37
  50.8 3.5 %collective-permute-start.17 = (f32[704,512]{1,0:T(8,128)}, f32[704,512]{1,0:T(8,128)S(1)}, u32[]{:S(2)}, u32[]{:S(2)}) collective-permute-start(f32[704,512]{1,0:T(8,128)} %get-tuple-element.36), channel_id=1, source_target_pairs={{0,4},{4,0},{8,12},{12,8},{16,20},{20,16},{24,28},{28,24},{1,5},{5... | collective-permute-start | bytes 4325384 | tf_op jit(solution)/shard_map/ppermute | solution.py:37
  57.1 1.6 %collective-permute-start.18 = (f32[4,136,128]{2,1,0:T(8,128)S(1)}, f32[4,136,128]{2,1,0:T(8,128)S(1)}, u32[]{:S(2)}, u32[]{:S(2)}) collective-permute-start(f32[4,136,128]{2,1,0:T(8,128)S(1)} %get-tuple-element.38), channel_id=1, source_target_pairs={{0,4},{4,0},{8,12},{12,8},{16,20},{20,16},{24,28},{28,24},{1,5},{5... | collective-permute-start | bytes 835592 | tf_op jit(solution)/shard_map/ppermute | solution.py:37
  58.8 4.4 %collective-permute-start.19 = (f32[1,136,128]{2,1,0:T(8,128)S(1)}, f32[1,136,128]{2,1,0:T(8,128)S(1)}, u32[]{:S(2)}, u32[]{:S(2)}) collective-permute-start(f32[1,136,128]{2,1,0:T(8,128)S(1)} %get-tuple-element.66), channel_id=1, source_target_pairs={{0,16},{4,20},{8,24},{12,28},{16,0},{20,4},{24,8},{28,12},{1,17},{... | collective-permute-start | bytes 208904 | tf_op jit(solution)/shard_map/ppermute | solution.py:37
  60.4 4.7 %collective-permute-start.20 = (f32[1,136,128]{2,1,0:T(8,128)S(1)}, f32[1,136,128]{2,1,0:T(8,128)S(1)}, u32[]{:S(2)}, u32[]{:S(2)}) collective-permute-start(f32[1,136,128]{2,1,0:T(8,128)S(1)} %get-tuple-element.65), channel_id=1, source_target_pairs={{0,8},{4,12},{8,0},{12,4},{16,24},{20,28},{24,16},{28,20},{1,9},{5... | collective-permute-start | bytes 208904 | tf_op jit(solution)/shard_map/ppermute | solution.py:37
  60.9 5.2 %collective-permute-start.21 = (f32[1,136,128]{2,1,0:T(8,128)S(1)}, f32[1,136,128]{2,1,0:T(8,128)S(1)}, u32[]{:S(2)}, u32[]{:S(2)}) collective-permute-start(f32[1,136,128]{2,1,0:T(8,128)S(1)} %get-tuple-element.64), channel_id=1, source_target_pairs={{0,24},{4,28},{8,16},{12,20},{16,8},{20,12},{24,0},{28,4},{1,25},{... | collective-permute-start | bytes 208904 | tf_op jit(solution)/shard_map/ppermute | solution.py:37
  66.1 5.1 %collective-permute-start.22 = (f32[1,136,128]{2,1,0:T(8,128)S(1)}, f32[1,136,128]{2,1,0:T(8,128)S(1)}, u32[]{:S(2)}, u32[]{:S(2)}) collective-permute-start(f32[1,136,128]{2,1,0:T(8,128)S(1)} %fusion.1), channel_id=1, source_target_pairs={{0,1},{1,0},{2,3},{3,2},{4,5},{5,4},{6,7},{7,6},{8,9},{9,8},{10,11... | collective-permute-start | bytes 208904 | tf_op jit(solution)/shard_map/ppermute | solution.py:37
  67.8 6.8 %collective-permute-start.23 = (f32[1,136,128]{2,1,0:T(8,128)S(1)}, f32[1,136,128]{2,1,0:T(8,128)S(1)}, u32[]{:S(2)}, u32[]{:S(2)}) collective-permute-start(f32[1,136,128]{2,1,0:T(8,128)S(1)} %fusion.1), channel_id=1, source_target_pairs={{0,2},{1,3},{2,0},{3,1},{4,6},{5,7},{6,4},{7,5},{8,10},{9,11},{10,... | collective-permute-start | bytes 208904 | tf_op jit(solution)/shard_map/ppermute | solution.py:37
  70.4 6.1 %collective-permute-start.24 = (f32[1,136,128]{2,1,0:T(8,128)S(1)}, f32[1,136,128]{2,1,0:T(8,128)S(1)}, u32[]{:S(2)}, u32[]{:S(2)}) collective-permute-start(f32[1,136,128]{2,1,0:T(8,128)S(1)} %fusion.1), channel_id=1, source_target_pairs={{0,3},{1,2},{2,1},{3,0},{4,7},{5,6},{6,5},{7,4},{8,11},{9,10},{10,... | collective-permute-start | bytes 208904 | tf_op jit(solution)/shard_map/ppermute | solution.py:37
  76.5 4.4 %collective-permute-start.25 = (f32[1,136,128]{2,1,0:T(8,128)S(1)}, f32[1,136,128]{2,1,0:T(8,128)S(1)}, u32[]{:S(2)}, u32[]{:S(2)}) collective-permute-start(f32[1,136,128]{2,1,0:T(8,128)S(1)} %add_add_fusion.refs_0_), channel_id=1, source_target_pairs={{0,16},{4,20},{8,24},{12,28},{16,0},{20,4},{24,8},{28,12},{1,17},{... | collective-permute-start | bytes 208904 | tf_op jit(solution)/shard_map/ppermute | solution.py:37
  77.7 4.3 %collective-permute-start.26 = (f32[1,136,128]{2,1,0:T(8,128)S(1)}, f32[1,136,128]{2,1,0:T(8,128)S(1)}, u32[]{:S(2)}, u32[]{:S(2)}) collective-permute-start(f32[1,136,128]{2,1,0:T(8,128)S(1)} %add_add_fusion.refs_0_), channel_id=1, source_target_pairs={{0,8},{4,12},{8,0},{12,4},{16,24},{20,28},{24,16},{28,20},{1,9},{5... | collective-permute-start | bytes 208904 | tf_op jit(solution)/shard_map/ppermute | solution.py:37
  78.6 5.2 %collective-permute-start.27 = (f32[1,136,128]{2,1,0:T(8,128)S(1)}, f32[1,136,128]{2,1,0:T(8,128)S(1)}, u32[]{:S(2)}, u32[]{:S(2)}) collective-permute-start(f32[1,136,128]{2,1,0:T(8,128)S(1)} %add_add_fusion.refs_0_), channel_id=1, source_target_pairs={{0,24},{4,28},{8,16},{12,20},{16,8},{20,12},{24,0},{28,4},{1,25},{... | collective-permute-start | bytes 208904 | tf_op jit(solution)/shard_map/ppermute | solution.py:37
  80.0 3.8 %collective-permute-start.28 = (f32[1,136,128]{2,1,0:T(8,128)S(1)}, f32[1,136,128]{2,1,0:T(8,128)S(1)}, u32[]{:S(2)}, u32[]{:S(2)}) collective-permute-start(f32[1,136,128]{2,1,0:T(8,128)S(1)} %add_add_fusion.refs_0_), channel_id=1, source_target_pairs={{0,4},{4,0},{8,12},{12,8},{16,20},{20,16},{24,28},{28,24},{1,5},{5... | collective-permute-start | bytes 208904 | tf_op jit(solution)/shard_map/ppermute | solution.py:37
  80.9 3.0 %collective-permute-start.29 = (f32[1,136,128]{2,1,0:T(8,128)S(1)}, f32[1,136,128]{2,1,0:T(8,128)S(1)}, u32[]{:S(2)}, u32[]{:S(2)}) collective-permute-start(f32[1,136,128]{2,1,0:T(8,128)S(1)} %collective-permute-done.25.refs_1_), channel_id=1, source_target_pairs={{0,4},{4,0},{8,12},{12,8},{16,20},{20,16},{24,28},{28,24},{1,5},{5... | collective-permute-start | bytes 208904 | tf_op jit(solution)/shard_map/ppermute | solution.py:37
  82.0 1.8 %collective-permute-start.30 = (f32[1,136,128]{2,1,0:T(8,128)S(1)}, f32[1,136,128]{2,1,0:T(8,128)S(1)}, u32[]{:S(2)}, u32[]{:S(2)}) collective-permute-start(f32[1,136,128]{2,1,0:T(8,128)S(1)} %collective-permute-done.26.refs_2_), channel_id=1, source_target_pairs={{0,4},{4,0},{8,12},{12,8},{16,20},{20,16},{24,28},{28,24},{1,5},{5... | collective-permute-start | bytes 208904 | tf_op jit(solution)/shard_map/ppermute | solution.py:37
  83.8 1.3 %collective-permute-start.31 = (f32[1,136,128]{2,1,0:T(8,128)S(1)}, f32[1,136,128]{2,1,0:T(8,128)S(1)}, u32[]{:S(2)}, u32[]{:S(2)}) collective-permute-start(f32[1,136,128]{2,1,0:T(8,128)S(1)} %collective-permute-done.27.refs_3_), channel_id=1, source_target_pairs={{0,4},{4,0},{8,12},{12,8},{16,20},{20,16},{24,28},{28,24},{1,5},{5... | collective-permute-start | bytes 208904 | tf_op jit(solution)/shard_map/ppermute | solution.py:37
  (9 other events, 42.7 us)

commit v4 on v3

--- a/solution.py
+++ b/solution.py
@@ -68,6 +68,16 @@
     return lax.dot_general(
         left, right, (((1,), (1,)), ((), ())), precision=HIGHEST, preferred_element_type=jnp.float32
     )
+
+
+def halves(value):
+    high = value.astype(jnp.bfloat16)
+    return high, (value - high.astype(jnp.float32)).astype(jnp.bfloat16)
+
+
+def dot_halves(left, right):
+    dot = lambda a, b: lax.dot_general(a, b, (((0,), (0,)), ((), ())), preferred_element_type=jnp.float32)
+    return dot(left[0], right[0]) + (dot(left[0], right[1]) + dot(left[1], right[0]))
 
 
 def full(value):
@@ -190,8 +200,10 @@
     row = lax.broadcasted_iota(jnp.int32, (TILE, TILE), 0)
     col = lax.broadcasted_iota(jnp.int32, (TILE, TILE), 1)
     blocks = {}
+    high, low = halves(jac_ref[...])
     for b in range(count):
-        strip = dot_rows(jac_ref[:, b * TILE : (b + 1) * TILE], jac_ref[:, b * TILE :])
+        lo, hi = b * TILE, (b + 1) * TILE
+        strip = dot_halves((high[:, lo:hi], low[:, lo:hi]), (high[:, lo:], low[:, lo:]))
         for c in range(b, count):
             blocks[b, c] = strip[:, (c - b) * TILE : (c - b + 1) * TILE]
     extra = [projected[:, b * TILE : (b + 1) * TILE] for b in range(count)]

time: 105 us -> 104 us (level)
  Pallas kernels: 33.7 us -> 32.6 us
where the time goes in v4:
time: 104 us
  waiting for transfers between devices  38.8 us (37%)
  Pallas kernels  32.6 us (31%)
  starting transfers between devices  26.4 us (25%)
  local copies, waits for them, and re-layouts  3.72 us (4%)
  between operations  1.57 us (2%)
    ppermute x32, waiting for transfers between devices, swap(): return lax.ppermute(value, axis, [(i, i ^ bit) for i in range(size)])  38.8 us
    ppermute x32, starting transfers between devices, swap(): return lax.ppermute(value, axis, [(i, i ^ bit) for i in range(size)])  26.4 us
    pallas_call x1, Pallas kernels, local(): pl.pallas_call(functools.partial(factor_kernel, table, groups), in_specs=...  18.8 us
    pallas_call x2, Pallas kernels, resist_rows(): pl.pallas_call(functools.partial(resist_kernel, first), out_shape=(shape,...  11.9 us
    unnamed x21, local copies, waits for them, and re-layouts  2.44 us
  transfers between devices with their start and end apart: 32, of which 19 were waited for; matrix products, arithmetic and copies ran while one was open for 1% of the time, Pallas kernels for 5%

profile of v4, /device:TPU:0, one launch (start us, length us, event | category | flops | bytes accessed | tf_op | source)
XLA Modules:
  0.0 103.7 jit_solution(7919621201984558307)
XLA Ops:
  0.7 1.1 %dynamic-slice_bitcast_fusion.1 = (bf16[64,1024]{1,0:T(8,128)(2,1)S(1)}, bf16[64,1024]{1,0:T(8,128)(2,1)S(1)}) fusion(bf16[1,64,8192]{2,1,0:T(8,128)(2,1)} %param.9, s32[]{:T(128)S(6)} %select_n.45, s32[]{:T(128)S(6)} %select_n.46), kind=kLoop, calls=%fused_computation.12 | loop fusion | bytes 524296 | tf_op jit(solution)/shard_map/dynamic_slice | solution.py:390
  2.3 1.0 collective-permute-done.1
  5.1 2.7 %collective-permute-start.3 = (bf16[128,1024]{1,0:T(8,128)(2,1)S(1)}, bf16[128,1024]{1,0:T(8,128)(2,1)S(1)}, u32[]{:S(2)}, u32[]{:S(2)}) collective-permute-start(bf16[128,1024]{1,0:T(8,128)(2,1)S(1)} %pad_maximum_fusion.refs_0_), channel_id=1, source_target_pairs={{0,8},{4,12},{8,0},{12,4},{16,24},{20,28},{24,16},{28,20},{1,9},{5... | collective-permute-start | bytes 786440 | tf_op jit(solution)/shard_map/ppermute | solution.py:37
  7.8 1.5 %collective-permute-start.13 = (bf16[128,1024]{1,0:T(8,128)(2,1)S(1)}, bf16[128,1024]{1,0:T(8,128)(2,1)S(1)}, u32[]{:S(2)}, u32[]{:S(2)}) collective-permute-start(bf16[128,1024]{1,0:T(8,128)(2,1)S(1)} %pad_maximum_fusion.refs_0_), channel_id=1, source_target_pairs={{0,16},{4,20},{8,24},{12,28},{16,0},{20,4},{24,8},{28,12},{1,17},{... | collective-permute-start | bytes 786440 | tf_op jit(solution)/shard_map/ppermute | solution.py:37
  11.2 3.7 %collective-permute-done.3.refs_1_ = bf16[128,1024]{1,0:T(8,128)(2,1)S(1)} collective-permute-done((bf16[128,1024]{1,0:T(8,128)(2,1)S(1)}, bf16[128,1024]{1,0:T(8,128)(2,1)S(1)}, u32[]{:S(2)}, u32[]{:S(2)}) %collective-permute-start.3) | collective-permute-done | bytes 262176 | tf_op jit(solution)/shard_map/ppermute | solution.py:37
  15.3 2.0 %collective-permute-start.4 = (bf16[128,1024]{1,0:T(8,128)(2,1)S(1)}, bf16[128,1024]{1,0:T(8,128)(2,1)S(1)}, u32[]{:S(2)}, u32[]{:S(2)}) collective-permute-start(bf16[128,1024]{1,0:T(8,128)(2,1)S(1)} %pad_maximum_fusion.1.refs_0_), channel_id=1, source_target_pairs={{0,8},{4,12},{8,0},{12,4},{16,24},{20,28},{24,16},{28,20},{1,9},{5... | collective-permute-start | bytes 786440 | tf_op jit(solution)/shard_map/ppermute | solution.py:37
  17.3 1.5 %collective-permute-start.14 = (bf16[128,1024]{1,0:T(8,128)(2,1)S(1)}, bf16[128,1024]{1,0:T(8,128)(2,1)S(1)}, u32[]{:S(2)}, u32[]{:S(2)}) collective-permute-start(bf16[128,1024]{1,0:T(8,128)(2,1)S(1)} %collective-permute-done.3.refs_1_), channel_id=1, source_target_pairs={{0,16},{4,20},{8,24},{12,28},{16,0},{20,4},{24,8},{28,12},{1,17},{... | collective-permute-start | bytes 786440 | tf_op jit(solution)/shard_map/ppermute | solution.py:37
  19.0 3.6 %collective-permute-done.9.refs_6_ = bf16[128,1024]{1,0:T(8,128)(2,1)S(1)} collective-permute-done((bf16[128,1024]{1,0:T(8,128)(2,1)S(1)}, bf16[128,1024]{1,0:T(8,128)(2,1)S(1)}, u32[]{:S(2)}, u32[]{:S(2)}) %collective-permute-start.9) | collective-permute-done | bytes 262176 | tf_op jit(solution)/shard_map/ppermute | solution.py:37
  22.6 1.5 %collective-permute-start.11 = (bf16[128,1024]{1,0:T(8,128)(2,1)S(1)}, bf16[128,1024]{1,0:T(8,128)(2,1)S(1)}, u32[]{:S(2)}, u32[]{:S(2)}) collective-permute-start(bf16[128,1024]{1,0:T(8,128)(2,1)S(1)} %pad_maximum_fusion.2.refs_4_), channel_id=1, source_target_pairs={{0,16},{4,20},{8,24},{12,28},{16,0},{20,4},{24,8},{28,12},{1,17},{... | collective-permute-start | bytes 786440 | tf_op jit(solution)/shard_map/ppermute | solution.py:37
  25.5 2.7 %collective-permute-done.14.refs_3_ = bf16[128,1024]{1,0:T(8,128)(2,1)S(1)} collective-permute-done((bf16[128,1024]{1,0:T(8,128)(2,1)S(1)}, bf16[128,1024]{1,0:T(8,128)(2,1)S(1)}, u32[]{:S(2)}, u32[]{:S(2)}) %collective-permute-start.14) | collective-permute-done | bytes 262176 | tf_op jit(solution)/shard_map/ppermute | solution.py:37
  28.2 2.0 %collective-permute-start.6 = (bf16[128,1024]{1,0:T(8,128)(2,1)S(1)}, bf16[128,1024]{1,0:T(8,128)(2,1)S(1)}, u32[]{:S(2)}, u32[]{:S(2)}) collective-permute-start(bf16[128,1024]{1,0:T(8,128)(2,1)S(1)} %collective-permute-done.4.refs_1_), channel_id=1, source_target_pairs={{0,16},{4,20},{8,24},{12,28},{16,0},{20,4},{24,8},{28,12},{1,17},{... | collective-permute-start | bytes 786440 | tf_op jit(solution)/shard_map/ppermute | solution.py:37
  30.2 3.6 %collective-permute-done.11.refs_6_ = bf16[128,1024]{1,0:T(8,128)(2,1)S(1)} collective-permute-done((bf16[128,1024]{1,0:T(8,128)(2,1)S(1)}, bf16[128,1024]{1,0:T(8,128)(2,1)S(1)}, u32[]{:S(2)}, u32[]{:S(2)}) %collective-permute-start.11) | collective-permute-done | bytes 262176 | tf_op jit(solution)/shard_map/ppermute | solution.py:37
  34.8 5.2 %resist.2 = (f32[704,512]{1,0:T(8,128)S(1)}, f32[704,512]{1,0:T(8,128)}) custom-call(s32[1]{0:T(128)} %bitcast.11.start_ref, f32[1]{0:T(128)S(6)} %mul.21.threshold_ref, f32[128,11]{1,0:T(8,128)S(1)} %copy.25.dose_ref, bf16[128,512]{1,0:T(8,128)(2,1)S(1)} %pad_maximum_fusion.4.select_ref, bf16[128,1024]{1,0:T(8,128)(2,1)S(1)} %pad_maximum_fusion.refs_0_, ...), custom_call_target="tpu_custom_call" | custom-call | flops 2952790016 | bytes 4194304 | tf_op jit(solution)/shard_map/resist/pallas_call | solution.py:153
  40.0 4.1 %collective-permute-done.6.refs_3_ = bf16[128,1024]{1,0:T(8,128)(2,1)S(1)} collective-permute-done((bf16[128,1024]{1,0:T(8,128)(2,1)S(1)}, bf16[128,1024]{1,0:T(8,128)(2,1)S(1)}, u32[]{:S(2)}, u32[]{:S(2)}) %collective-permute-start.6) | collective-permute-done | bytes 262176 | tf_op jit(solution)/shard_map/ppermute | solution.py:37
  44.1 6.7 %resist.3 = (f32[704,512]{1,0:T(8,128)S(1)}, f32[704,512]{1,0:T(8,128)}) custom-call(s32[1]{0:T(128)} %bitcast.1.start_ref, f32[1]{0:T(128)S(6)} %mul.21.threshold_ref, f32[128,11]{1,0:T(8,128)S(1)} %copy.25.dose_ref, bf16[128,512]{1,0:T(8,128)(2,1)S(1)} %pad_maximum_fusion.4.select_ref, ...), custom_call_target="tpu_custom_call", output_to_operand_aliasing={{0}: (13, {}), {1}: (14, {})} | custom-call | flops 2952790016 | bytes 4194304 | tf_op jit(solution)/shard_map/resist/pallas_call | solution.py:153
  51.0 3.3 %collective-permute-done.17.other_ref = f32[704,512]{1,0:T(8,128)S(1)} collective-permute-done((f32[704,512]{1,0:T(8,128)}, f32[704,512]{1,0:T(8,128)S(1)}, u32[]{:S(2)}, u32[]{:S(2)}) %collective-permute-start.17) | collective-permute-done | bytes 1441824 | tf_op jit(solution)/shard_map/ppermute | solution.py:37
  54.3 1.9 %normal.1 = (f32[704,512]{1,0:T(8,128)S(1)}, f32[64,11]{1,0:T(8,128)S(1)}, f32[64,11]{1,0:T(8,128)S(1)}, f32[4,136,128]{2,1,0:T(8,128)S(1)}, f32[4,136,128]{2,1,0:T(8,128)S(1)}) custom-call(s32[1]{0:T(128)} %bitcast.me_ref, f32[704,512]{1,0:T(8,128)S(1)} %get-tuple-element.35.mine_ref, f32[704,512]{1,0:T(8,128)S(1)} %collective-permute-done.17.other_ref, ...), custom_call_target="tpu_custom_call" | custom-call | tf_op jit(solution)/shard_map/normal/pallas_call | solution.py:432
  56.5 1.4 %collective-permute-done.18 = f32[4,136,128]{2,1,0:T(8,128)S(1)} collective-permute-done((f32[4,136,128]{2,1,0:T(8,128)S(1)}, f32[4,136,128]{2,1,0:T(8,128)S(1)}, u32[]{:S(2)}, u32[]{:S(2)}) %collective-permute-start.18) | collective-permute-done | bytes 278560 | tf_op jit(solution)/shard_map/ppermute | solution.py:37
  57.9 1.6 %collective-permute-start.19 = (f32[1,136,128]{2,1,0:T(8,128)S(1)}, f32[1,136,128]{2,1,0:T(8,128)S(1)}, u32[]{:S(2)}, u32[]{:S(2)}) collective-permute-start(f32[1,136,128]{2,1,0:T(8,128)S(1)} %get-tuple-element.66), channel_id=1, source_target_pairs={{0,16},{4,20},{8,24},{12,28},{16,0},{20,4},{24,8},{28,12},{1,17},{... | collective-permute-start | bytes 208904 | tf_op jit(solution)/shard_map/ppermute | solution.py:37
  60.0 1.4 %collective-permute-start.21 = (f32[1,136,128]{2,1,0:T(8,128)S(1)}, f32[1,136,128]{2,1,0:T(8,128)S(1)}, u32[]{:S(2)}, u32[]{:S(2)}) collective-permute-start(f32[1,136,128]{2,1,0:T(8,128)S(1)} %get-tuple-element.64), channel_id=1, source_target_pairs={{0,24},{4,28},{8,16},{12,20},{16,8},{20,12},{24,0},{28,4},{1,25},{... | collective-permute-start | bytes 208904 | tf_op jit(solution)/shard_map/ppermute | solution.py:37
  62.3 1.9 %collective-permute-done.20 = f32[1,136,128]{2,1,0:T(8,128)S(1)} collective-permute-done((f32[1,136,128]{2,1,0:T(8,128)S(1)}, f32[1,136,128]{2,1,0:T(8,128)S(1)}, u32[]{:S(2)}, u32[]{:S(2)}) %collective-permute-start.20) | collective-permute-done | bytes 69664 | tf_op jit(solution)/shard_map/ppermute | solution.py:37
  64.2 1.1 %collective-permute-done.21 = f32[1,136,128]{2,1,0:T(8,128)S(1)} collective-permute-done((f32[1,136,128]{2,1,0:T(8,128)S(1)}, f32[1,136,128]{2,1,0:T(8,128)S(1)}, u32[]{:S(2)}, u32[]{:S(2)}) %collective-permute-start.21) | collective-permute-done | bytes 69664 | tf_op jit(solution)/shard_map/ppermute | solution.py:37
  65.3 1.6 %collective-permute-start.22 = (f32[1,136,128]{2,1,0:T(8,128)S(1)}, f32[1,136,128]{2,1,0:T(8,128)S(1)}, u32[]{:S(2)}, u32[]{:S(2)}) collective-permute-start(f32[1,136,128]{2,1,0:T(8,128)S(1)} %fusion.1), channel_id=1, source_target_pairs={{0,1},{1,0},{2,3},{3,2},{4,5},{5,4},{6,7},{7,6},{8,9},{9,8},{10,11... | collective-permute-start | bytes 208904 | tf_op jit(solution)/shard_map/ppermute | solution.py:37
  66.9 2.6 %collective-permute-start.23 = (f32[1,136,128]{2,1,0:T(8,128)S(1)}, f32[1,136,128]{2,1,0:T(8,128)S(1)}, u32[]{:S(2)}, u32[]{:S(2)}) collective-permute-start(f32[1,136,128]{2,1,0:T(8,128)S(1)} %fusion.1), channel_id=1, source_target_pairs={{0,2},{1,3},{2,0},{3,1},{4,6},{5,7},{6,4},{7,5},{8,10},{9,11},{10,... | collective-permute-start | bytes 208904 | tf_op jit(solution)/shard_map/ppermute | solution.py:37
  70.3 3.3 %collective-permute-done.23 = f32[1,136,128]{2,1,0:T(8,128)S(1)} collective-permute-done((f32[1,136,128]{2,1,0:T(8,128)S(1)}, f32[1,136,128]{2,1,0:T(8,128)S(1)}, u32[]{:S(2)}, u32[]{:S(2)}) %collective-permute-start.23) | collective-permute-done | bytes 69664 | tf_op jit(solution)/shard_map/ppermute | solution.py:37
  73.7 1.9 %collective-permute-done.24 = f32[1,136,128]{2,1,0:T(8,128)S(1)} collective-permute-done((f32[1,136,128]{2,1,0:T(8,128)S(1)}, f32[1,136,128]{2,1,0:T(8,128)S(1)}, u32[]{:S(2)}, u32[]{:S(2)}) %collective-permute-start.24) | collective-permute-done | bytes 69664 | tf_op jit(solution)/shard_map/ppermute | solution.py:37
  75.6 1.2 %collective-permute-start.25 = (f32[1,136,128]{2,1,0:T(8,128)S(1)}, f32[1,136,128]{2,1,0:T(8,128)S(1)}, u32[]{:S(2)}, u32[]{:S(2)}) collective-permute-start(f32[1,136,128]{2,1,0:T(8,128)S(1)} %add_add_fusion.refs_0_), channel_id=1, source_target_pairs={{0,16},{4,20},{8,24},{12,28},{16,0},{20,4},{24,8},{28,12},{1,17},{... | collective-permute-start | bytes 208904 | tf_op jit(solution)/shard_map/ppermute | solution.py:37
  77.8 1.4 %collective-permute-start.27 = (f32[1,136,128]{2,1,0:T(8,128)S(1)}, f32[1,136,128]{2,1,0:T(8,128)S(1)}, u32[]{:S(2)}, u32[]{:S(2)}) collective-permute-start(f32[1,136,128]{2,1,0:T(8,128)S(1)} %add_add_fusion.refs_0_), channel_id=1, source_target_pairs={{0,24},{4,28},{8,16},{12,20},{16,8},{20,12},{24,0},{28,4},{1,25},{... | collective-permute-start | bytes 208904 | tf_op jit(solution)/shard_map/ppermute | solution.py:37
  80.0 1.2 %collective-permute-done.26.refs_2_ = f32[1,136,128]{2,1,0:T(8,128)S(1)} collective-permute-done((f32[1,136,128]{2,1,0:T(8,128)S(1)}, f32[1,136,128]{2,1,0:T(8,128)S(1)}, u32[]{:S(2)}, u32[]{:S(2)}) %collective-permute-start.26) | collective-permute-done | bytes 69664 | tf_op jit(solution)/shard_map/ppermute | solution.py:37
  81.2 1.8 %collective-permute-done.27.refs_3_ = f32[1,136,128]{2,1,0:T(8,128)S(1)} collective-permute-done((f32[1,136,128]{2,1,0:T(8,128)S(1)}, f32[1,136,128]{2,1,0:T(8,128)S(1)}, u32[]{:S(2)}, u32[]{:S(2)}) %collective-permute-start.27) | collective-permute-done | bytes 69664 | tf_op jit(solution)/shard_map/ppermute | solution.py:37
  83.0 1.2 %collective-permute-done.31.refs_7_ = f32[1,136,128]{2,1,0:T(8,128)S(1)} collective-permute-done((f32[1,136,128]{2,1,0:T(8,128)S(1)}, f32[1,136,128]{2,1,0:T(8,128)S(1)}, u32[]{:S(2)}, u32[]{:S(2)}) %collective-permute-start.31) | collective-permute-done | bytes 69664 | tf_op jit(solution)/shard_map/ppermute | solution.py:37
  84.2 18.8 %factor.1 = (f32[512,512]{1,0:T(8,128)}, f32[1,512]{1,0:T(1,128)}, f32[64,11]{1,0:T(8,128)S(1)}) custom-call(s32[1]{0:T(128)} %bitcast.me_ref, f32[1,136,128]{2,1,0:T(8,128)S(1)} %add_add_fusion.refs_0_, f32[1,136,128]{2,1,0:T(8,128)S(1)} %collective-permute-done.25.refs_1_, f32[1,136,128]{2,1,0:T(8,128)S(1)} %collective-permute-done.26.refs_2_, ...), custom_call_target="tpu_custom_call" | custom-call | tf_op jit(solution)/shard_map/factor/pallas_call | solution.py:461
  (79 shorter events, 11.4 us)
Async XLA Ops:
  1.8 1.5 %collective-permute-start.1 = (bf16[64,1024]{1,0:T(8,128)(2,1)S(1)}, bf16[64,1024]{1,0:T(8,128)(2,1)S(1)}, u32[]{:S(2)}, u32[]{:S(2)}) collective-permute-start(bf16[64,1024]{1,0:T(8,128)(2,1)S(1)} %get-tuple-element.63), channel_id=1, source_target_pairs={{0,4},{4,0},{8,12},{12,8},{16,20},{20,16},{24,28},{28,24},{1,5},{5... | collective-permute-start | bytes 393224 | tf_op jit(solution)/shard_map/ppermute | solution.py:37
  3.4 5.9 %collective-permute-start.8 = (bf16[64,1024]{1,0:T(8,128)(2,1)S(1)}, bf16[64,1024]{1,0:T(8,128)(2,1)S(1)}, u32[]{:S(2)}, u32[]{:S(2)}) collective-permute-start(bf16[64,1024]{1,0:T(8,128)(2,1)S(1)} %get-tuple-element.57), channel_id=1, source_target_pairs={{0,4},{4,0},{8,12},{12,8},{16,20},{20,16},{24,28},{28,24},{1,5},{5... | collective-permute-start | bytes 393224 | tf_op jit(solution)/shard_map/ppermute | solution.py:37
  3.8 5.5 %collective-permute-start.7 = (bf16[64,1024]{1,0:T(8,128)(2,1)S(1)}, bf16[64,1024]{1,0:T(8,128)(2,1)S(1)}, u32[]{:S(2)}, u32[]{:S(2)}) collective-permute-start(bf16[64,1024]{1,0:T(8,128)(2,1)S(1)} %get-tuple-element.58), channel_id=1, source_target_pairs={{0,4},{4,0},{8,12},{12,8},{16,20},{20,16},{24,28},{28,24},{1,5},{5... | collective-permute-start | bytes 393224 | tf_op jit(solution)/shard_map/ppermute | solution.py:37
  4.0 10.9 %collective-permute-start = (s32[64,15]{0,1:T(8,128)S(1)}, s32[64,15]{0,1:T(8,128)S(1)}, u32[]{:S(2)}, u32[]{:S(2)}) collective-permute-start(s32[64,15]{0,1:T(8,128)S(1)} %pad_add_fusion), channel_id=1, source_target_pairs={{0,4},{4,0},{8,12},{12,8},{16,20},{20,16},{24,28},{28,24},{1,5},{5... | collective-permute-start | bytes 11528 | tf_op jit(solution)/shard_map/ppermute | solution.py:37
  5.1 9.9 %collective-permute-start.3 = (bf16[128,1024]{1,0:T(8,128)(2,1)S(1)}, bf16[128,1024]{1,0:T(8,128)(2,1)S(1)}, u32[]{:S(2)}, u32[]{:S(2)}) collective-permute-start(bf16[128,1024]{1,0:T(8,128)(2,1)S(1)} %pad_maximum_fusion.refs_0_), channel_id=1, source_target_pairs={{0,8},{4,12},{8,0},{12,4},{16,24},{20,28},{24,16},{28,20},{1,9},{5... | collective-permute-start | bytes 786440 | tf_op jit(solution)/shard_map/ppermute | solution.py:37
  7.8 16.3 %collective-permute-start.13 = (bf16[128,1024]{1,0:T(8,128)(2,1)S(1)}, bf16[128,1024]{1,0:T(8,128)(2,1)S(1)}, u32[]{:S(2)}, u32[]{:S(2)}) collective-permute-start(bf16[128,1024]{1,0:T(8,128)(2,1)S(1)} %pad_maximum_fusion.refs_0_), channel_id=1, source_target_pairs={{0,16},{4,20},{8,24},{12,28},{16,0},{20,4},{24,8},{28,12},{1,17},{... | collective-permute-start | bytes 786440 | tf_op jit(solution)/shard_map/ppermute | solution.py:37
  9.3 1.3 %collective-permute-start.2 = (bf16[64,1024]{1,0:T(8,128)(2,1)S(1)}, bf16[64,1024]{1,0:T(8,128)(2,1)S(1)}, u32[]{:S(2)}, u32[]{:S(2)}) collective-permute-start(bf16[64,1024]{1,0:T(8,128)(2,1)S(1)} %get-tuple-element.60), channel_id=1, source_target_pairs={{0,4},{4,0},{8,12},{12,8},{16,20},{20,16},{24,28},{28,24},{1,5},{5... | collective-permute-start | bytes 393224 | tf_op jit(solution)/shard_map/ppermute | solution.py:37
  9.3 13.2 %collective-permute-start.9 = (bf16[128,1024]{1,0:T(8,128)(2,1)S(1)}, bf16[128,1024]{1,0:T(8,128)(2,1)S(1)}, u32[]{:S(2)}, u32[]{:S(2)}) collective-permute-start(bf16[128,1024]{1,0:T(8,128)(2,1)S(1)} %pad_maximum_fusion.3.refs_4_), channel_id=1, source_target_pairs={{0,16},{4,20},{8,24},{12,28},{16,0},{20,4},{24,8},{28,12},{1,17},{... | collective-permute-start | bytes 786440 | tf_op jit(solution)/shard_map/ppermute | solution.py:37
  10.6 14.1 %collective-permute-start.15 = (bf16[128,1024]{1,0:T(8,128)(2,1)S(1)}, bf16[128,1024]{1,0:T(8,128)(2,1)S(1)}, u32[]{:S(2)}, u32[]{:S(2)}) collective-permute-start(bf16[128,1024]{1,0:T(8,128)(2,1)S(1)} %pad_maximum_fusion.3.refs_4_), channel_id=1, source_target_pairs={{0,8},{4,12},{8,0},{12,4},{16,24},{20,28},{24,16},{28,20},{1,9},{5... | collective-permute-start | bytes 786440 | tf_op jit(solution)/shard_map/ppermute | solution.py:37
  15.3 12.9 %collective-permute-start.4 = (bf16[128,1024]{1,0:T(8,128)(2,1)S(1)}, bf16[128,1024]{1,0:T(8,128)(2,1)S(1)}, u32[]{:S(2)}, u32[]{:S(2)}) collective-permute-start(bf16[128,1024]{1,0:T(8,128)(2,1)S(1)} %pad_maximum_fusion.1.refs_0_), channel_id=1, source_target_pairs={{0,8},{4,12},{8,0},{12,4},{16,24},{20,28},{24,16},{28,20},{1,9},{5... | collective-permute-start | bytes 786440 | tf_op jit(solution)/shard_map/ppermute | solution.py:37
  17.3 10.8 %collective-permute-start.14 = (bf16[128,1024]{1,0:T(8,128)(2,1)S(1)}, bf16[128,1024]{1,0:T(8,128)(2,1)S(1)}, u32[]{:S(2)}, u32[]{:S(2)}) collective-permute-start(bf16[128,1024]{1,0:T(8,128)(2,1)S(1)} %collective-permute-done.3.refs_1_), channel_id=1, source_target_pairs={{0,16},{4,20},{8,24},{12,28},{16,0},{20,4},{24,8},{28,12},{1,17},{... | collective-permute-start | bytes 786440 | tf_op jit(solution)/shard_map/ppermute | solution.py:37
  22.6 11.2 %collective-permute-start.11 = (bf16[128,1024]{1,0:T(8,128)(2,1)S(1)}, bf16[128,1024]{1,0:T(8,128)(2,1)S(1)}, u32[]{:S(2)}, u32[]{:S(2)}) collective-permute-start(bf16[128,1024]{1,0:T(8,128)(2,1)S(1)} %pad_maximum_fusion.2.refs_4_), channel_id=1, source_target_pairs={{0,16},{4,20},{8,24},{12,28},{16,0},{20,4},{24,8},{28,12},{1,17},{... | collective-permute-start | bytes 786440 | tf_op jit(solution)/shard_map/ppermute | solution.py:37
  24.1 9.8 %collective-permute-start.16 = (bf16[128,1024]{1,0:T(8,128)(2,1)S(1)}, bf16[128,1024]{1,0:T(8,128)(2,1)S(1)}, u32[]{:S(2)}, u32[]{:S(2)}) collective-permute-start(bf16[128,1024]{1,0:T(8,128)(2,1)S(1)} %collective-permute-done.9.refs_6_), channel_id=1, source_target_pairs={{0,8},{4,12},{8,0},{12,4},{16,24},{20,28},{24,16},{28,20},{1,9},{5... | collective-permute-start | bytes 786440 | tf_op jit(solution)/shard_map/ppermute | solution.py:37
  25.4 14.6 %collective-permute-start.5 = (bf16[128,1024]{1,0:T(8,128)(2,1)S(1)}, bf16[128,1024]{1,0:T(8,128)(2,1)S(1)}, u32[]{:S(2)}, u32[]{:S(2)}) collective-permute-start(bf16[128,1024]{1,0:T(8,128)(2,1)S(1)} %pad_maximum_fusion.1.refs_0_), channel_id=1, source_target_pairs={{0,16},{4,20},{8,24},{12,28},{16,0},{20,4},{24,8},{28,12},{1,17},{... | collective-permute-start | bytes 786440 | tf_op jit(solution)/shard_map/ppermute | solution.py:37
  28.2 11.8 %collective-permute-start.10 = (bf16[128,1024]{1,0:T(8,128)(2,1)S(1)}, bf16[128,1024]{1,0:T(8,128)(2,1)S(1)}, u32[]{:S(2)}, u32[]{:S(2)}) collective-permute-start(bf16[128,1024]{1,0:T(8,128)(2,1)S(1)} %pad_maximum_fusion.2.refs_4_), channel_id=1, source_target_pairs={{0,8},{4,12},{8,0},{12,4},{16,24},{20,28},{24,16},{28,20},{1,9},{5... | collective-permute-start | bytes 786440 | tf_op jit(solution)/shard_map/ppermute | solution.py:37
  28.2 15.9 %collective-permute-start.6 = (bf16[128,1024]{1,0:T(8,128)(2,1)S(1)}, bf16[128,1024]{1,0:T(8,128)(2,1)S(1)}, u32[]{:S(2)}, u32[]{:S(2)}) collective-permute-start(bf16[128,1024]{1,0:T(8,128)(2,1)S(1)} %collective-permute-done.4.refs_1_), channel_id=1, source_target_pairs={{0,16},{4,20},{8,24},{12,28},{16,0},{20,4},{24,8},{28,12},{1,17},{... | collective-permute-start | bytes 786440 | tf_op jit(solution)/shard_map/ppermute | solution.py:37
  33.8 10.4 %collective-permute-start.12 = (bf16[128,1024]{1,0:T(8,128)(2,1)S(1)}, bf16[128,1024]{1,0:T(8,128)(2,1)S(1)}, u32[]{:S(2)}, u32[]{:S(2)}) collective-permute-start(bf16[128,1024]{1,0:T(8,128)(2,1)S(1)} %collective-permute-done.11.refs_6_), channel_id=1, source_target_pairs={{0,8},{4,12},{8,0},{12,4},{16,24},{20,28},{24,16},{28,20},{1,9},{5... | collective-permute-start | bytes 786440 | tf_op jit(solution)/shard_map/ppermute | solution.py:37
  50.8 3.5 %collective-permute-start.17 = (f32[704,512]{1,0:T(8,128)}, f32[704,512]{1,0:T(8,128)S(1)}, u32[]{:S(2)}, u32[]{:S(2)}) collective-permute-start(f32[704,512]{1,0:T(8,128)} %get-tuple-element.36), channel_id=1, source_target_pairs={{0,4},{4,0},{8,12},{12,8},{16,20},{20,16},{24,28},{28,24},{1,5},{5... | collective-permute-start | bytes 4325384 | tf_op jit(solution)/shard_map/ppermute | solution.py:37
  56.3 1.6 %collective-permute-start.18 = (f32[4,136,128]{2,1,0:T(8,128)S(1)}, f32[4,136,128]{2,1,0:T(8,128)S(1)}, u32[]{:S(2)}, u32[]{:S(2)}) collective-permute-start(f32[4,136,128]{2,1,0:T(8,128)S(1)} %get-tuple-element.38), channel_id=1, source_target_pairs={{0,4},{4,0},{8,12},{12,8},{16,20},{20,16},{24,28},{28,24},{1,5},{5... | collective-permute-start | bytes 835592 | tf_op jit(solution)/shard_map/ppermute | solution.py:37
  57.9 4.4 %collective-permute-start.19 = (f32[1,136,128]{2,1,0:T(8,128)S(1)}, f32[1,136,128]{2,1,0:T(8,128)S(1)}, u32[]{:S(2)}, u32[]{:S(2)}) collective-permute-start(f32[1,136,128]{2,1,0:T(8,128)S(1)} %get-tuple-element.66), channel_id=1, source_target_pairs={{0,16},{4,20},{8,24},{12,28},{16,0},{20,4},{24,8},{28,12},{1,17},{... | collective-permute-start | bytes 208904 | tf_op jit(solution)/shard_map/ppermute | solution.py:37
  59.5 4.7 %collective-permute-start.20 = (f32[1,136,128]{2,1,0:T(8,128)S(1)}, f32[1,136,128]{2,1,0:T(8,128)S(1)}, u32[]{:S(2)}, u32[]{:S(2)}) collective-permute-start(f32[1,136,128]{2,1,0:T(8,128)S(1)} %get-tuple-element.65), channel_id=1, source_target_pairs={{0,8},{4,12},{8,0},{12,4},{16,24},{20,28},{24,16},{28,20},{1,9},{5... | collective-permute-start | bytes 208904 | tf_op jit(solution)/shard_map/ppermute | solution.py:37
  60.0 5.2 %collective-permute-start.21 = (f32[1,136,128]{2,1,0:T(8,128)S(1)}, f32[1,136,128]{2,1,0:T(8,128)S(1)}, u32[]{:S(2)}, u32[]{:S(2)}) collective-permute-start(f32[1,136,128]{2,1,0:T(8,128)S(1)} %get-tuple-element.64), channel_id=1, source_target_pairs={{0,24},{4,28},{8,16},{12,20},{16,8},{20,12},{24,0},{28,4},{1,25},{... | collective-permute-start | bytes 208904 | tf_op jit(solution)/shard_map/ppermute | solution.py:37
  65.3 5.1 %collective-permute-start.22 = (f32[1,136,128]{2,1,0:T(8,128)S(1)}, f32[1,136,128]{2,1,0:T(8,128)S(1)}, u32[]{:S(2)}, u32[]{:S(2)}) collective-permute-start(f32[1,136,128]{2,1,0:T(8,128)S(1)} %fusion.1), channel_id=1, source_target_pairs={{0,1},{1,0},{2,3},{3,2},{4,5},{5,4},{6,7},{7,6},{8,9},{9,8},{10,11... | collective-permute-start | bytes 208904 | tf_op jit(solution)/shard_map/ppermute | solution.py:37
  66.9 6.8 %collective-permute-start.23 = (f32[1,136,128]{2,1,0:T(8,128)S(1)}, f32[1,136,128]{2,1,0:T(8,128)S(1)}, u32[]{:S(2)}, u32[]{:S(2)}) collective-permute-start(f32[1,136,128]{2,1,0:T(8,128)S(1)} %fusion.1), channel_id=1, source_target_pairs={{0,2},{1,3},{2,0},{3,1},{4,6},{5,7},{6,4},{7,5},{8,10},{9,11},{10,... | collective-permute-start | bytes 208904 | tf_op jit(solution)/shard_map/ppermute | solution.py:37
  69.5 6.1 %collective-permute-start.24 = (f32[1,136,128]{2,1,0:T(8,128)S(1)}, f32[1,136,128]{2,1,0:T(8,128)S(1)}, u32[]{:S(2)}, u32[]{:S(2)}) collective-permute-start(f32[1,136,128]{2,1,0:T(8,128)S(1)} %fusion.1), channel_id=1, source_target_pairs={{0,3},{1,2},{2,1},{3,0},{4,7},{5,6},{6,5},{7,4},{8,11},{9,10},{10,... | collective-permute-start | bytes 208904 | tf_op jit(solution)/shard_map/ppermute | solution.py:37
  75.6 4.4 %collective-permute-start.25 = (f32[1,136,128]{2,1,0:T(8,128)S(1)}, f32[1,136,128]{2,1,0:T(8,128)S(1)}, u32[]{:S(2)}, u32[]{:S(2)}) collective-permute-start(f32[1,136,128]{2,1,0:T(8,128)S(1)} %add_add_fusion.refs_0_), channel_id=1, source_target_pairs={{0,16},{4,20},{8,24},{12,28},{16,0},{20,4},{24,8},{28,12},{1,17},{... | collective-permute-start | bytes 208904 | tf_op jit(solution)/shard_map/ppermute | solution.py:37
  76.9 4.3 %collective-permute-start.26 = (f32[1,136,128]{2,1,0:T(8,128)S(1)}, f32[1,136,128]{2,1,0:T(8,128)S(1)}, u32[]{:S(2)}, u32[]{:S(2)}) collective-permute-start(f32[1,136,128]{2,1,0:T(8,128)S(1)} %add_add_fusion.refs_0_), channel_id=1, source_target_pairs={{0,8},{4,12},{8,0},{12,4},{16,24},{20,28},{24,16},{28,20},{1,9},{5... | collective-permute-start | bytes 208904 | tf_op jit(solution)/shard_map/ppermute | solution.py:37
  77.8 5.2 %collective-permute-start.27 = (f32[1,136,128]{2,1,0:T(8,128)S(1)}, f32[1,136,128]{2,1,0:T(8,128)S(1)}, u32[]{:S(2)}, u32[]{:S(2)}) collective-permute-start(f32[1,136,128]{2,1,0:T(8,128)S(1)} %add_add_fusion.refs_0_), channel_id=1, source_target_pairs={{0,24},{4,28},{8,16},{12,20},{16,8},{20,12},{24,0},{28,4},{1,25},{... | collective-permute-start | bytes 208904 | tf_op jit(solution)/shard_map/ppermute | solution.py:37
  79.2 3.8 %collective-permute-start.28 = (f32[1,136,128]{2,1,0:T(8,128)S(1)}, f32[1,136,128]{2,1,0:T(8,128)S(1)}, u32[]{:S(2)}, u32[]{:S(2)}) collective-permute-start(f32[1,136,128]{2,1,0:T(8,128)S(1)} %add_add_fusion.refs_0_), channel_id=1, source_target_pairs={{0,4},{4,0},{8,12},{12,8},{16,20},{20,16},{24,28},{28,24},{1,5},{5... | collective-permute-start | bytes 208904 | tf_op jit(solution)/shard_map/ppermute | solution.py:37
  80.0 3.0 %collective-permute-start.29 = (f32[1,136,128]{2,1,0:T(8,128)S(1)}, f32[1,136,128]{2,1,0:T(8,128)S(1)}, u32[]{:S(2)}, u32[]{:S(2)}) collective-permute-start(f32[1,136,128]{2,1,0:T(8,128)S(1)} %collective-permute-done.25.refs_1_), channel_id=1, source_target_pairs={{0,4},{4,0},{8,12},{12,8},{16,20},{20,16},{24,28},{28,24},{1,5},{5... | collective-permute-start | bytes 208904 | tf_op jit(solution)/shard_map/ppermute | solution.py:37
  81.2 1.8 %collective-permute-start.30 = (f32[1,136,128]{2,1,0:T(8,128)S(1)}, f32[1,136,128]{2,1,0:T(8,128)S(1)}, u32[]{:S(2)}, u32[]{:S(2)}) collective-permute-start(f32[1,136,128]{2,1,0:T(8,128)S(1)} %collective-permute-done.26.refs_2_), channel_id=1, source_target_pairs={{0,4},{4,0},{8,12},{12,8},{16,20},{20,16},{24,28},{28,24},{1,5},{5... | collective-permute-start | bytes 208904 | tf_op jit(solution)/shard_map/ppermute | solution.py:37
  83.0 1.3 %collective-permute-start.31 = (f32[1,136,128]{2,1,0:T(8,128)S(1)}, f32[1,136,128]{2,1,0:T(8,128)S(1)}, u32[]{:S(2)}, u32[]{:S(2)}) collective-permute-start(f32[1,136,128]{2,1,0:T(8,128)S(1)} %collective-permute-done.27.refs_3_), channel_id=1, source_target_pairs={{0,4},{4,0},{8,12},{12,8},{16,20},{20,16},{24,28},{28,24},{1,5},{5... | collective-permute-start | bytes 208904 | tf_op jit(solution)/shard_map/ppermute | solution.py:37
  (9 other events, 42.7 us)
